TPU v7x, 32 devices: a whole 2x2x4 slice. The times are simulated.
32 devices in a mesh: ctx: 8 (over y, x, core), tp: 4 (over z).
Axes of the slice: x: 2, y: 2, z: 4, core: 2. Of those that a mesh axis runs over, the one named last changes fastest.
Arguments:
- query_proj: bfloat16 [16384, 1024], P(('ctx', 'tp')), may hold values from -6 to 6
- key_proj: bfloat16 [16384, 1024], P(('ctx', 'tp')), may hold values from -6 to 6
- value_proj: bfloat16 [16384, 1024], P(('ctx', 'tp')), may hold values from -6 to 6
- long_filter: float32 [16384, 1024], P('ctx', 'tp'), may hold values from 0 to 0.4
- short_filter: float32 [3, 3, 1024], P(None, None, 'tp'), may hold values from -3 to 3
- skip_bias: float32 [1024], P('tp'), may hold values from 0.5 to 1.5
Outputs:
- gated_output: float32 [16384, 1024], P(('ctx', 'tp'))
All inputs are finite; a program needn't handle non-finite values.
Results may differ from a plain program's by a relative error of at most 0.0003.
Values may be sent and summed in bfloat16 or wider, within the bound.
No kernel may reach another device: no remote copies, remote signals or barrier semaphores. Data moves between devices by JAX's collectives and lax.ppermute only.
A program may use at most 128 MiB of HBM per device.

v0:
```python
import math

import jax
import jax.numpy as jnp
from jax import lax
from jax.sharding import PartitionSpec as P

highest = lax.Precision.HIGHEST


def passed_along(value, axis, by):
    length = lax.axis_size(axis)
    pairs = [(i, i + by) for i in range(length) if 0 <= i + by < length]
    return lax.ppermute(value, axis, pairs)


def product(formula, left, right):
    return jnp.einsum(formula, left, right, precision=highest)


def phase_table(left_index, right_index, modulus, direction):
    winding = left_index[:, None] * right_index[None, :] % modulus
    angles = winding.astype(jnp.float32) * (2.0 * math.pi / modulus)
    return (jnp.cos(angles), direction * jnp.sin(angles))


def apply_table(formula, phase, real_part, imag_part):
    if imag_part is None:
        return (product(formula, phase[0], real_part), product(formula, phase[1], real_part))
    return (
        product(formula, phase[0], real_part) - product(formula, phase[1], imag_part),
        product(formula, phase[0], imag_part) + product(formula, phase[1], real_part),
    )


def multiply_pair(complex_pair, factor):
    return (
        complex_pair[0] * factor[0] - complex_pair[1] * factor[1],
        complex_pair[0] * factor[1] + complex_pair[1] * factor[0],
    )


def split_length(length):
    inner_size = 128 if length % 128 == 0 else length
    return (length // inner_size, inner_size)


def row_transform(complex_pair, lead, tail, direction):
    full_shape = complex_pair[0].shape
    element_offset = len(lead) + 1
    outer_size, inner_size = split_length(full_shape[element_offset])
    folded = (
        full_shape[:element_offset] + (outer_size, inner_size) + full_shape[element_offset + 1 :]
    )
    real_part = complex_pair[0].reshape(folded)
    imag_part = complex_pair[1].reshape(folded)
    outer_iota = jnp.arange(outer_size, dtype=jnp.int32)
    inner_iota = jnp.arange(inner_size, dtype=jnp.int32)
    outer_table = phase_table(outer_iota, outer_iota, outer_size, direction)
    inner_table = phase_table(inner_iota, inner_iota, inner_size, direction)
    twist = phase_table(outer_iota, inner_iota, full_shape[element_offset], direction)
    source = lead + "kab" + tail
    middle = lead + "kfb" + tail
    target = lead + "kfg" + tail
    if direction < 0:
        sectioned = apply_table("fa," + source + "->" + middle, outer_table, real_part, imag_part)
        sectioned = multiply_pair(sectioned, twist)
        sectioned = apply_table(
            "gb," + middle + "->" + target, inner_table, sectioned[0], sectioned[1]
        )
    else:
        sectioned = apply_table("gb," + target + "->" + middle, inner_table, real_part, imag_part)
        sectioned = multiply_pair(sectioned, twist)
        sectioned = apply_table(
            "fa," + middle + "->" + source, outer_table, sectioned[0], sectioned[1]
        )
    return (sectioned[0].reshape(full_shape), sectioned[1].reshape(full_shape))


def cross_forward(signal, blocks, lead, tail):
    phase = phase_table(
        jnp.arange(2 * blocks, dtype=jnp.int32),
        jnp.arange(blocks, dtype=jnp.int32),
        2 * blocks,
        -1.0,
    )
    return apply_table("kp," + lead + "pj" + tail + "->" + lead + "kj" + tail, phase, signal, None)


def twist_rows(complex_pair, k_values, modulus, lead, direction):
    length = complex_pair[0].shape[len(lead) + 1]
    phase = phase_table(k_values, jnp.arange(length, dtype=jnp.int32), modulus, direction)
    return multiply_pair(complex_pair, phase)


def cross_inverse(complex_pair, blocks, modulus, lead, tail):
    phase = phase_table(
        jnp.arange(blocks, dtype=jnp.int32),
        jnp.arange(2 * blocks, dtype=jnp.int32),
        2 * blocks,
        1.0,
    )
    formula = "pk," + lead + "kj" + tail + "->" + lead + "pj" + tail
    return (
        product(formula, phase[0], complex_pair[0]) - product(formula, phase[1], complex_pair[1])
    ) * (1.0 / modulus)


def spectrum(complex_pair, k_values, modulus, lead, tail):
    return row_transform(twist_rows(complex_pair, k_values, modulus, lead, -1.0), lead, tail, -1.0)


def restore(complex_pair, k_values, modulus, lead, tail):
    return twist_rows(row_transform(complex_pair, lead, tail, 1.0), k_values, modulus, lead, 1.0)


def short_conv(current, previous, weights):
    extended = jnp.concatenate([previous, current], 0).astype(jnp.float32)
    return (
        weights[0][None, :] * extended[2:]
        + weights[1][None, :] * extended[1:-1]
        + weights[2][None, :] * extended[:-2]
    )


def short_parts(grouped, before, short_filter):
    query_short = short_conv(grouped[0], before[0], short_filter[0])
    key_short = short_conv(grouped[1], before[1], short_filter[1])
    value_short = short_conv(grouped[2], before[2], short_filter[2])
    return (query_short, key_short * value_short)


def edge_stack(grouped):
    return jnp.stack([grouped[0][-2:], grouped[1][-2:], grouped[2][-2:]])


def sequence_conv(signal_rows, kernel_rows, blocks, length):
    channel_count = signal_rows.shape[0]
    modulus = 2 * blocks * length
    signal = cross_forward(signal_rows.reshape(channel_count, blocks, length), blocks, "z", "")
    kernel = cross_forward(kernel_rows.reshape(channel_count, blocks, length), blocks, "z", "")
    k_values = jnp.arange(2 * blocks, dtype=jnp.int32)
    signal = spectrum(signal, k_values, modulus, "z", "")
    kernel = spectrum(kernel, k_values, modulus, "z", "")
    joined = restore(multiply_pair(signal, kernel), k_values, modulus, "z", "")
    return cross_inverse(joined, blocks, modulus, "z", "").reshape(channel_count, blocks * length)


def gate(query_short, long_conv, skip_bias, mixed_input):
    return query_short * (long_conv + skip_bias[None, :] * mixed_input)


def local(query_proj, key_proj, value_proj, long_filter, short_filter, skip_bias):
    blocks = lax.axis_size("ctx")
    length = query_proj.shape[0] * lax.axis_size("tp")
    grouped = (
        lax.all_to_all(query_proj, "tp", split_axis=1, concat_axis=0, tiled=True),
        lax.all_to_all(key_proj, "tp", split_axis=1, concat_axis=0, tiled=True),
        lax.all_to_all(value_proj, "tp", split_axis=1, concat_axis=0, tiled=True),
    )
    before = passed_along(edge_stack(grouped), "ctx", 1)
    query_short, mixed_input = short_parts(grouped, before, short_filter)
    sequences = (
        lax.all_to_all(mixed_input.T, "ctx", split_axis=0, concat_axis=1, tiled=True),
        lax.all_to_all(long_filter.T, "ctx", split_axis=0, concat_axis=1, tiled=True),
    )
    convolved = sequence_conv(sequences[0], sequences[1], blocks, length)
    long_conv = lax.all_to_all(convolved, "ctx", split_axis=1, concat_axis=0, tiled=True).T
    result = gate(query_short, long_conv, skip_bias, mixed_input)
    return lax.all_to_all(result, "tp", split_axis=0, concat_axis=1, tiled=True)


def solution(mesh):
    return jax.shard_map(
        local,
        mesh=mesh,
        in_specs=(
            P(("ctx", "tp"), None),
            P(("ctx", "tp"), None),
            P(("ctx", "tp"), None),
            P("ctx", "tp"),
            P(None, None, "tp"),
            P("tp"),
        ),
        out_specs=P(("ctx", "tp"), None),
        check_vma=False,
    )
```

profile of v0, /device:TPU:2, one launch (start us, length us, event | category | flops | bytes accessed | tf_op | source)
XLA Modules:
  0.0 393.6 jit_solution(10751548027431262199)
XLA Ops:
  0.0 2.4 copy.51
  2.4 4.9 %all-to-all-start = ((bf16[512,4,256]{0,2,1:T(8,128)(2,1)}), bf16[512,4,256]{0,2,1:T(8,128)(2,1)S(1)}, u32[]{:S(2)}, u32[]{:S(2)}) async-start(bf16[512,4,256]{0,2,1:T(8,128)(2,1)} %bitcast.1), calls=%async_computation | async-start | bytes 2097152 | tf_op jit(solution)/shard_map/all_to_all | solution.py:157
  7.2 1.3 copy.53
  8.5 24.4 %all-to-all-done = bf16[512,4,256]{0,2,1:T(8,128)(2,1)S(1)} async-done(((bf16[512,4,256]{0,2,1:T(8,128)(2,1)}), bf16[512,4,256]{0,2,1:T(8,128)(2,1)S(1)}, u32[]{:S(2)}, u32[]{:S(2)}) %all-to-all-start) | async-done | bytes 1048608 | tf_op jit(solution)/shard_map/all_to_all | solution.py:157
  33.0 3.5 all-to-all-start.1
  36.5 2.3 copy.55
  38.8 22.9 %all-to-all-done.1 = bf16[512,4,256]{0,2,1:T(8,128)(2,1)S(1)} async-done(((bf16[512,4,256]{0,2,1:T(8,128)(2,1)}), bf16[512,4,256]{0,2,1:T(8,128)(2,1)S(1)}, u32[]{:S(2)}, u32[]{:S(2)}) %all-to-all-start.1) | async-done | bytes 1048608 | tf_op jit(solution)/shard_map/all_to_all | solution.py:158
  61.7 4.2 %all-to-all-start.2 = ((bf16[512,4,256]{0,2,1:T(8,128)(2,1)}), bf16[512,4,256]{0,2,1:T(8,128)(2,1)}, u32[]{:S(2)}, u32[]{:S(2)}) async-start(bf16[512,4,256]{0,2,1:T(8,128)(2,1)} %bitcast.9), calls=%async_computation.2 | async-start | bytes 2097152 | tf_op jit(solution)/shard_map/all_to_all | solution.py:159
  65.9 2.9 copy.63
  68.9 1.2 fusion.114
  71.2 1.9 copy.54
  73.0 18.2 %all-to-all-done.2 = bf16[512,4,256]{0,2,1:T(8,128)(2,1)} async-done(((bf16[512,4,256]{0,2,1:T(8,128)(2,1)}), bf16[512,4,256]{0,2,1:T(8,128)(2,1)}, u32[]{:S(2)}, u32[]{:S(2)}) %all-to-all-start.2) | async-done | bytes 1048608 | tf_op jit(solution)/shard_map/all_to_all | solution.py:159
  91.2 4.3 %all-to-all-start.4 = ((f32[8,32,2048]{2,1,0:T(8,128)}), f32[8,32,2048]{2,1,0:T(8,128)S(1)}, u32[]{:S(2)}, u32[]{:S(2)}) async-start(f32[8,32,2048]{2,1,0:T(8,128)} %bitcast.299), calls=%async_computation.4 | async-start | bytes 4194304 | tf_op jit(solution)/shard_map/all_to_all | solution.py:165
  95.5 2.3 copy.56
  98.4 2.1 collective-permute-start
  100.6 18.9 %collective-permute-done = bf16[3,2,256]{2,1,0:T(2,128)(2,1)S(1)} collective-permute-done((bf16[3,2,256]{2,1,0:T(2,128)(2,1)S(1)}, bf16[3,2,256]{2,1,0:T(2,128)(2,1)S(1)}, u32[]{:S(2)}, u32[]{:S(2)}) %collective-permute-start) | collective-permute-done | bytes 3104 | tf_op jit(solution)/shard_map/ppermute | solution.py:14
  119.7 1.4 maximum_convert_fusion.2
  121.1 2.7 fusion.52
  123.8 2.9 copy.57
  126.7 4.5 %all-to-all-start.3 = ((f32[8,32,2048]{2,1,0:T(8,128)}), f32[8,32,2048]{2,1,0:T(8,128)}, u32[]{:S(2)}, u32[]{:S(2)}) async-start(f32[8,32,2048]{2,1,0:T(8,128)} %bitcast.300), calls=%async_computation.3 | async-start | bytes 4194304 | tf_op jit(solution)/shard_map/all_to_all | solution.py:164
  131.2 4.3 %fusion.61 = f32[16,32,2048]{2,0,1:T(8,128)S(1)} fusion(f32[8,32,2048]{2,1,0:T(8,128)S(1)} %all-to-all-done.4), kind=kOutput, calls=%fused_computation.83 | convolution fusion | flops 100665088 | bytes 6291456 | tf_op jit(solution)/shard_map/kp,zpj->zkj/dot_general | solution.py:18
  135.5 5.1 %multiply_subtract_fusion.2 = (f32[16,32,2048]{2,0,1:T(8,128)S(1)}, f32[16,32,2048]{2,0,1:T(8,128)S(1)}) fusion(f32[16,32,2048]{2,0,1:T(8,128)S(1)} %fusion.61, f32[16,2048]{1,0:T(8,128)S(1)} %get-tuple-element.25, f32[16,2048]{1,0:T(8,128)S(1)} %get-tuple-element.26, f32[8,32,2048]{2,1,0:T(8,128)S(1)} %all-to-all-done.4), kind=kOutput, calls=%fused_computation.49 | convolution fusion | flops 106956672 | bytes 14942208 | tf_op jit(solution)/shard_map/kp,zpj->zkj/dot_general | solution.py:18
  140.6 0.9 copy.96
  141.6 0.9 copy.97
  142.5 4.4 %fusion.2 = f32[32,16,128,16]{2,3,1,0:T(8,128)S(1)} fusion(f32[32,16,16,128]{3,2,1,0:T(8,128)S(1)} %bitcast.290), kind=kOutput, calls=%fused_computation.2 | convolution fusion | flops 201330432 | bytes 8388608 | tf_op jit(solution)/shard_map/fa,zkab->zkfb/dot_general | solution.py:18
  146.9 4.2 %fusion = f32[32,16,128,16]{2,3,1,0:T(8,128)S(1)} fusion(f32[32,16,16,128]{3,2,1,0:T(8,128)S(1)} %bitcast.291), kind=kOutput, calls=%fused_computation | convolution fusion | flops 201330176 | bytes 8388608 | tf_op jit(solution)/shard_map/fa,zkab->zkfb/dot_general | solution.py:18
  151.1 4.2 %fusion.45 = f32[32,16,128,16]{2,3,1,0:T(8,128)S(1)} fusion(f32[32,16,128,16]{2,3,1,0:T(8,128)S(1)} %fusion.2, f32[32,16,16,128]{3,2,1,0:T(8,128)S(1)} %bitcast.286), kind=kOutput, calls=%fused_computation.55 | convolution fusion | flops 202378752 | bytes 12582912 | tf_op jit(solution)/shard_map/fa,zkab->zkfb/dot_general | solution.py:18
  155.4 4.9 %fusion.48 = f32[32,16,128,16]{2,3,1,0:T(8,128)S(1)} fusion(f32[32,16,128,16]{2,3,1,0:T(8,128)S(1)} %fusion, f32[32,16,16,128]{3,2,1,0:T(8,128)S(1)} %bitcast.287), kind=kOutput, calls=%fused_computation.56 | convolution fusion | flops 202379008 | bytes 12582912 | tf_op jit(solution)/shard_map/fa,zkab->zkfb/dot_general | solution.py:18
  160.2 3.8 fusion.83
  164.0 3.8 fusion.87
  167.8 5.6 %convolution_add_fusion.1 = f32[32,16,16,128]{3,2,1,0:T(8,128)} fusion(f32[32,16,16,128]{3,2,1,0:T(8,128)S(1)} %fusion.83, f32[32,16,128,16]{2,3,1,0:T(8,128)S(1)} %fusion.48, f32[32,16,128,16]{2,3,1,0:T(8,128)S(1)} %fusion.45, f32[16,128]{1,0:T(8,128)S(1)} %get-tuple-element.27, f32[16,128]{1,0:T(8,128)S(1)} %get-tuple-element.28), kind=kOutput, calls=%fused_computation.59 | convolution fusion | flops 1615052800 | bytes 16793600 | tf_op jit(solution)/shard_map/gb,zkfb->zkfg/dot_general | solution.py:18
  173.4 5.7 %convolution_subtract_fusion.1 = f32[32,16,16,128]{3,2,1,0:T(8,128)} fusion(f32[32,16,16,128]{3,2,1,0:T(8,128)S(1)} %fusion.87, f32[32,16,128,16]{2,3,1,0:T(8,128)S(1)} %fusion.48, f32[32,16,128,16]{2,3,1,0:T(8,128)S(1)} %fusion.45, f32[16,128]{1,0:T(8,128)S(1)} %get-tuple-element.27, f32[16,128]{1,0:T(8,128)S(1)} %get-tuple-element.28), kind=kOutput, calls=%fused_computation.61 | convolution fusion | flops 1615052800 | bytes 16793600 | tf_op jit(solution)/shard_map/gb,zkfb->zkfg/dot_general | solution.py:18
  179.2 7.5 %fusion.65 = f32[32,2048,16]{1,2,0:T(8,128)S(1)} fusion(f32[8,32,2048]{2,1,0:T(8,128)} %all-to-all-done.3), kind=kOutput, calls=%fused_computation.87 | convolution fusion | flops 100665088 | bytes 6291456 | tf_op jit(solution)/shard_map/kp,zpj->zkj/dot_general | solution.py:18
  186.6 8.5 %fusion.20 = (f32[32,16,2048]{2,1,0:T(8,128)S(1)}, f32[32,16,2048]{2,1,0:T(8,128)S(1)}) fusion(f32[32,2048,16]{1,2,0:T(8,128)S(1)} %fusion.65, f32[16,2048]{1,0:T(8,128)S(1)} %get-tuple-element.25, f32[16,2048]{1,0:T(8,128)S(1)} %get-tuple-element.26, f32[8,32,2048]{2,1,0:T(8,128)} %all-to-all-done.3), kind=kOutput, calls=%fused_computation.30 | convolution fusion | flops 106956672 | bytes 14942208 | tf_op jit(solution)/shard_map/kp,zpj->zkj/dot_general | solution.py:18
  195.2 0.9 copy.94
  196.1 1.1 copy.95
  197.3 4.2 %fusion.10 = f32[32,16,128,16]{2,3,1,0:T(8,128)S(1)} fusion(f32[32,16,16,128]{3,2,1,0:T(8,128)S(1)} %bitcast.292), kind=kOutput, calls=%fused_computation.10 | convolution fusion | flops 201330432 | bytes 8388608 | tf_op jit(solution)/shard_map/fa,zkab->zkfb/dot_general | solution.py:18
  201.4 4.3 %fusion.8 = f32[32,16,128,16]{2,3,1,0:T(8,128)S(1)} fusion(f32[32,16,16,128]{3,2,1,0:T(8,128)S(1)} %bitcast.293), kind=kOutput, calls=%fused_computation.8 | convolution fusion | flops 201330176 | bytes 8388608 | tf_op jit(solution)/shard_map/fa,zkab->zkfb/dot_general | solution.py:18
  205.7 4.4 %fusion.39 = f32[32,16,128,16]{2,3,1,0:T(8,128)S(1)} fusion(f32[32,16,128,16]{2,3,1,0:T(8,128)S(1)} %fusion.10, f32[32,16,16,128]{3,2,1,0:T(8,128)S(1)} %bitcast.288), kind=kOutput, calls=%fused_computation.53 | convolution fusion | flops 202378752 | bytes 12582912 | tf_op jit(solution)/shard_map/fa,zkab->zkfb/dot_general | solution.py:18
  210.1 4.4 %fusion.42 = f32[32,16,128,16]{2,3,1,0:T(8,128)S(1)} fusion(f32[32,16,128,16]{2,3,1,0:T(8,128)S(1)} %fusion.8, f32[32,16,16,128]{3,2,1,0:T(8,128)S(1)} %bitcast.289), kind=kOutput, calls=%fused_computation.54 | convolution fusion | flops 202379008 | bytes 12582912 | tf_op jit(solution)/shard_map/fa,zkab->zkfb/dot_general | solution.py:18
  214.5 5.9 %fusion.77 = f32[32,16,16,128]{3,2,1,0:T(8,128)} fusion(f32[32,16,128,16]{2,3,1,0:T(8,128)S(1)} %fusion.42, f32[32,16,128,16]{2,3,1,0:T(8,128)S(1)} %fusion.39, f32[16,128]{1,0:T(8,128)S(1)} %get-tuple-element.27, f32[16,128]{1,0:T(8,128)S(1)} %get-tuple-element.28), kind=kOutput, calls=%fused_computation.99 | convolution fusion | flops 1613987840 | bytes 12599296 | tf_op jit(solution)/shard_map/gb,zkfb->zkfg/dot_general | solution.py:18
  220.4 3.8 fusion.81
  224.2 5.6 %convolution_subtract_fusion.2 = f32[32,16,16,128]{3,2,1,0:T(8,128)} fusion(f32[32,16,16,128]{3,2,1,0:T(8,128)S(1)} %fusion.81, f32[32,16,128,16]{2,3,1,0:T(8,128)S(1)} %fusion.42, f32[32,16,128,16]{2,3,1,0:T(8,128)S(1)} %fusion.39, f32[16,128]{1,0:T(8,128)S(1)} %get-tuple-element.27, f32[16,128]{1,0:T(8,128)S(1)} %get-tuple-element.28), kind=kOutput, calls=%fused_computation.62 | convolution fusion | flops 1615052800 | bytes 16793600 | tf_op jit(solution)/shard_map/gb,zkfb->zkfg/dot_general | solution.py:18
  229.8 8.4 %multiply_subtract_fusion.1 = (f32[32,16,16,128]{3,2,1,0:T(8,128)S(1)}, f32[32,16,16,128]{3,2,1,0:T(8,128)S(1)}) fusion(f32[32,16,16,128]{3,2,1,0:T(8,128)S(1)} %copy-done.4, f32[32,16,16,128]{3,2,1,0:T(8,128)} %convolution_subtract_fusion.2, f32[32,16,16,128]{3,2,1,0:T(8,128)} %convolution_subtract_fusion.1, f32[32,16,16,128]{3,2,1,0:T(8,128)} %fusion.77, ...), kind=kOutput, calls=%fused_computation.47 | convolution fusion | flops 1621344256 | bytes 33570816 | tf_op jit(solution)/shard_map/gb,zkfb->zkfg/dot_general | solution.py:18
  238.1 3.9 fusion.106
  242.0 3.8 fusion.104
  245.8 3.9 convolution_subtract_fusion
  249.7 4.4 %convolution_add_fusion = f32[32,16,16,128]{3,2,1,0:T(8,128)S(1)} fusion(f32[32,16,16,128]{3,2,1,0:T(8,128)S(1)} %fusion.104, f32[32,16,16,128]{3,2,1,0:T(8,128)S(1)} %get-tuple-element.5), kind=kOutput, calls=%fused_computation.57 | convolution fusion | flops 1611890688 | bytes 12582912 | tf_op jit(solution)/shard_map/gb,zkfg->zkfb/dot_general | solution.py:18
  254.2 4.4 %fusion.76 = f32[32,16,128,16]{2,3,1,0:T(8,128)S(1)} fusion(f32[32,16,16,128]{3,2,1,0:T(8,128)S(1)} %convolution_add_fusion, f32[32,16,16,128]{3,2,1,0:T(8,128)S(1)} %convolution_subtract_fusion, f32[16,128]{1,0:T(8,128)S(1)} %fusion.183, f32[16,128]{1,0:T(8,128)S(1)} %get-tuple-element.28), kind=kOutput, calls=%fused_computation.98 | convolution fusion | flops 204475904 | bytes 12599296 | tf_op jit(solution)/shard_map/fa,zkfb->zkab/dot_general | solution.py:18
  258.6 5.6 %fusion.75 = f32[32,16,128,16]{2,3,1,0:T(8,128)} fusion(f32[32,16,16,128]{3,2,1,0:T(8,128)S(1)} %convolution_add_fusion, f32[32,16,16,128]{3,2,1,0:T(8,128)S(1)} %convolution_subtract_fusion, f32[16,128]{1,0:T(8,128)S(1)} %fusion.183, f32[16,128]{1,0:T(8,128)S(1)} %get-tuple-element.28), kind=kOutput, calls=%fused_computation.97 | convolution fusion | flops 204475904 | bytes 12599296 | tf_op jit(solution)/shard_map/fa,zkfb->zkab/dot_general | solution.py:18
  264.2 5.7 %add_bitcast_fusion = f32[32,16,16,128]{3,2,1,0:T(8,128)} fusion(f32[32,16,128,16]{2,3,1,0:T(8,128)S(1)} %fusion.76, f32[32,16,16,128]{3,2,1,0:T(8,128)S(1)} %convolution_add_fusion, f32[32,16,16,128]{3,2,1,0:T(8,128)S(1)} %convolution_subtract_fusion, f32[16,128]{1,0:T(8,128)S(1)} %fusion.183, f32[16,128]{1,0:T(8,128)S(1)} %get-tuple-element.28), kind=kOutput, calls=%fused_computation.41 | convolution fusion | flops 205524480 | bytes 16793600 | tf_op jit(solution)/shard_map/fa,zkfb->zkab/dot_general | solution.py:18
  269.9 5.0 %reshape.167 = f32[32,16,2048]{2,1,0:T(8,128)} reshape(f32[32,16,16,128]{3,2,1,0:T(8,128)} %add_bitcast_fusion) | data formatting | bytes 8388608 | tf_op jit(solution)/shard_map/reshape | solution.py:77
  274.9 10.7 %subtract_bitcast_fusion = f32[32,16,16,128]{3,2,1,0:T(8,128)} fusion(f32[32,16,128,16]{2,3,1,0:T(8,128)} %fusion.75, f32[32,16,16,128]{3,2,1,0:T(8,128)} %copy-done.1, f32[32,16,16,128]{3,2,1,0:T(8,128)} %copy-done, f32[16,128]{1,0:T(8,128)S(1)} %fusion.183, f32[16,128]{1,0:T(8,128)S(1)} %get-tuple-element.28), kind=kOutput, calls=%fused_computation.43 | convolution fusion | flops 205524480 | bytes 16793600 | tf_op jit(solution)/shard_map/fa,zkfb->zkab/dot_general | solution.py:18
  285.6 5.0 %reshape.166 = f32[32,16,2048]{2,1,0:T(8,128)} reshape(f32[32,16,16,128]{3,2,1,0:T(8,128)} %subtract_bitcast_fusion) | data formatting | bytes 8388608 | tf_op jit(solution)/shard_map/reshape | solution.py:77
  290.6 5.4 %fusion.22 = f32[32,2048,8]{1,2,0:T(8,128)S(1)} fusion(f32[32,16,2048]{2,1,0:T(8,128)} %reshape.167, f32[32,16,2048]{2,1,0:T(8,128)} %reshape.166, f32[16,2048]{1,0:T(8,128)S(1)} %copy-done.10, f32[16,2048]{1,0:T(8,128)S(1)} %copy-done.9), kind=kOutput, calls=%fused_computation.34 | convolution fusion | flops 103810816 | bytes 10747904 | tf_op jit(solution)/shard_map/pk,zkj->zpj/dot_general | solution.py:18
  296.6 3.1 fusion.36
  299.7 2.5 copy.69
  302.2 4.3 %all-to-all-start.5 = ((f32[32,8,2048]{2,0,1:T(8,128)}), f32[32,8,2048]{2,0,1:T(8,128)}, u32[]{:S(2)}, u32[]{:S(2)}) async-start(f32[32,8,2048]{2,0,1:T(8,128)} %copy.69), calls=%async_computation.5 | async-start | bytes 4194304 | tf_op jit(solution)/shard_map/all_to_all | solution.py:168
  306.8 24.8 %all-to-all-done.5 = f32[32,8,2048]{2,0,1:T(8,128)} async-done(((f32[32,8,2048]{2,0,1:T(8,128)}), f32[32,8,2048]{2,0,1:T(8,128)}, u32[]{:S(2)}, u32[]{:S(2)}) %all-to-all-start.5) | async-done | bytes 2097184 | tf_op jit(solution)/shard_map/all_to_all | solution.py:168
  331.6 2.9 copy.70
  334.5 3.0 fusion.57
  337.5 51.2 %all_to_all.124 = f32[4,512,256]{2,1,0:T(8,128)S(1)} all-to-all(f32[4,512,256]{2,1,0:T(8,128)S(1)} %bitcast.303), channel_id=1, replica_groups=mesh['ctx'=8,'tp'=4] {'tp'}, dimensions={0} | all-to-all | bytes 4194304 | tf_op jit(solution)/shard_map/all_to_all | solution.py:170
  388.7 1.8 copy.71
  390.5 2.9 copy.72
  (41 shorter events, 2.9 us)
Async XLA Ops:
  0.0 7.2 %copy-start.11 = (bf16[512,1024]{1,0:T(8,128)(2,1)S(1)}, bf16[512,1024]{1,0:T(8,128)(2,1)}, u32[]{:S(2)}) copy-start(bf16[512,1024]{1,0:T(8,128)(2,1)} %param.7) | copy-start | bytes 3145732
  2.4 30.6 %all-to-all-start = ((bf16[512,4,256]{0,2,1:T(8,128)(2,1)}), bf16[512,4,256]{0,2,1:T(8,128)(2,1)S(1)}, u32[]{:S(2)}, u32[]{:S(2)}) async-start(bf16[512,4,256]{0,2,1:T(8,128)(2,1)} %bitcast.1), calls=%async_computation | async-start | bytes 2097152 | tf_op jit(solution)/shard_map/all_to_all | solution.py:157
  33.0 28.7 %all-to-all-start.1 = ((bf16[512,4,256]{0,2,1:T(8,128)(2,1)}), bf16[512,4,256]{0,2,1:T(8,128)(2,1)S(1)}, u32[]{:S(2)}, u32[]{:S(2)}) async-start(bf16[512,4,256]{0,2,1:T(8,128)(2,1)} %bitcast.5), calls=%async_computation.1 | async-start | bytes 2097152 | tf_op jit(solution)/shard_map/all_to_all | solution.py:158
  36.5 32.4 %copy-start.12 = (f32[3,3,256]{2,1,0:T(4,128)S(1)}, f32[3,3,256]{2,1,0:T(4,128)}, u32[]{:S(2)}) copy-start(f32[3,3,256]{2,1,0:T(4,128)} %param.10) | copy-start | bytes 27652
  61.7 9.5 %copy-start.7 = (bf16[512,4,256]{0,2,1:T(8,128)(2,1)}, bf16[512,4,256]{0,2,1:T(8,128)(2,1)S(1)}, u32[]{:S(2)}) copy-start(bf16[512,4,256]{0,2,1:T(8,128)(2,1)S(1)} %all-to-all-done.1) | copy-start | bytes 3145732
  61.7 29.5 %all-to-all-start.2 = ((bf16[512,4,256]{0,2,1:T(8,128)(2,1)}), bf16[512,4,256]{0,2,1:T(8,128)(2,1)}, u32[]{:S(2)}, u32[]{:S(2)}) async-start(bf16[512,4,256]{0,2,1:T(8,128)(2,1)} %bitcast.9), calls=%async_computation.2 | async-start | bytes 2097152 | tf_op jit(solution)/shard_map/all_to_all | solution.py:159
  70.6 116.0 %copy-start.8 = (f32[16,2048]{1,0:T(8,128)}, f32[16,2048]{1,0:T(8,128)S(1)}, u32[]{:S(2)}) copy-start(f32[16,2048]{1,0:T(8,128)S(1)} %get-tuple-element.26) | copy-start | bytes 393220
  71.2 20.1 %copy-start.5 = (bf16[4,512,256]{2,1,0:T(8,128)(2,1)}, bf16[4,512,256]{2,1,0:T(8,128)(2,1)S(1)}, u32[]{:S(2)}) copy-start(bf16[4,512,256]{2,1,0:T(8,128)(2,1)S(1)} %copy.52) | copy-start | bytes 3145732
  91.2 35.5 %all-to-all-start.4 = ((f32[8,32,2048]{2,1,0:T(8,128)}), f32[8,32,2048]{2,1,0:T(8,128)S(1)}, u32[]{:S(2)}, u32[]{:S(2)}) async-start(f32[8,32,2048]{2,1,0:T(8,128)} %bitcast.299), calls=%async_computation.4 | async-start | bytes 4194304 | tf_op jit(solution)/shard_map/all_to_all | solution.py:165
  98.4 21.0 %collective-permute-start = (bf16[3,2,256]{2,1,0:T(2,128)(2,1)S(1)}, bf16[3,2,256]{2,1,0:T(2,128)(2,1)S(1)}, u32[]{:S(2)}, u32[]{:S(2)}) collective-permute-start(bf16[3,2,256]{2,1,0:T(2,128)(2,1)S(1)} %pad_maximum_fusion), channel_id=1, source_target_pairs={{0,4},{4,8},{8,12},{12,16},{16,20},{20,24},{24,28},{1,5},{5,9},{9,... | collective-permute-start | bytes 9224 | tf_op jit(solution)/shard_map/ppermute | solution.py:14
  126.7 52.4 %all-to-all-start.3 = ((f32[8,32,2048]{2,1,0:T(8,128)}), f32[8,32,2048]{2,1,0:T(8,128)}, u32[]{:S(2)}, u32[]{:S(2)}) async-start(f32[8,32,2048]{2,1,0:T(8,128)} %bitcast.300), calls=%async_computation.3 | async-start | bytes 4194304 | tf_op jit(solution)/shard_map/all_to_all | solution.py:164
  224.2 5.6 %copy-start.4 = (f32[32,16,16,128]{3,2,1,0:T(8,128)S(1)}, f32[32,16,16,128]{3,2,1,0:T(8,128)}, u32[]{:S(2)}) copy-start(f32[32,16,16,128]{3,2,1,0:T(8,128)} %convolution_add_fusion.1) | copy-start | bytes 12582916
  249.7 14.4 %copy-start = (f32[32,16,16,128]{3,2,1,0:T(8,128)}, f32[32,16,16,128]{3,2,1,0:T(8,128)S(1)}, u32[]{:S(2)}) copy-start(f32[32,16,16,128]{3,2,1,0:T(8,128)S(1)} %convolution_subtract_fusion) | copy-start | bytes 12582916
  254.2 10.0 %copy-start.1 = (f32[32,16,16,128]{3,2,1,0:T(8,128)}, f32[32,16,16,128]{3,2,1,0:T(8,128)S(1)}, u32[]{:S(2)}) copy-start(f32[32,16,16,128]{3,2,1,0:T(8,128)S(1)} %convolution_add_fusion) | copy-start | bytes 12582916
  285.6 5.0 %copy-start.9 = (f32[16,2048]{1,0:T(8,128)S(1)}, f32[16,2048]{1,0:T(8,128)}, u32[]{:S(2)}) copy-start(f32[16,2048]{1,0:T(8,128)} %copy-done.8) | copy-start | bytes 393220
  285.6 5.0 %copy-start.10 = (f32[16,2048]{1,0:T(8,128)S(1)}, f32[16,2048]{1,0:T(8,128)}, u32[]{:S(2)}) copy-start(f32[16,2048]{1,0:T(8,128)} %fusion.114) | copy-start | bytes 393220
  290.6 5.4 %copy-start.2 = (f32[32,16,2048]{2,1,0:T(8,128)S(1)}, f32[32,16,2048]{2,1,0:T(8,128)}, u32[]{:S(2)}) copy-start(f32[32,16,2048]{2,1,0:T(8,128)} %reshape.167) | copy-start | bytes 12582916
  290.6 5.9 %copy-start.3 = (f32[32,16,2048]{2,1,0:T(8,128)S(1)}, f32[32,16,2048]{2,1,0:T(8,128)}, u32[]{:S(2)}) copy-start(f32[32,16,2048]{2,1,0:T(8,128)} %reshape.166) | copy-start | bytes 12582916
  299.7 6.9 %copy-start.6 = (bf16[4,512,256]{2,1,0:T(8,128)(2,1)S(1)}, bf16[4,512,256]{2,1,0:T(8,128)(2,1)}, u32[]{:S(2)}) copy-start(bf16[4,512,256]{2,1,0:T(8,128)(2,1)} %copy-done.5) | copy-start | bytes 3145732
  302.2 29.4 %all-to-all-start.5 = ((f32[32,8,2048]{2,0,1:T(8,128)}), f32[32,8,2048]{2,0,1:T(8,128)}, u32[]{:S(2)}, u32[]{:S(2)}) async-start(f32[32,8,2048]{2,0,1:T(8,128)} %copy.69), calls=%async_computation.5 | async-start | bytes 4194304 | tf_op jit(solution)/shard_map/all_to_all | solution.py:168
  306.5 28.0 %copy-start.13 = (f32[256]{0:T(256)S(1)}, f32[256]{0:T(256)}, u32[]{:S(2)}) copy-start(f32[256]{0:T(256)} %param.11) | copy-start | bytes 3076
where the time goes:
time: 399 us; the launch traced here: 394 us
  matrix products  154 us (39%)
  waiting for transfers between devices  109 us (27%)
  blocking collectives  51.2 us (13%)
  local copies, waits for them, and re-layouts  41.8 us (10%)
  starting transfers between devices  27.7 us (7%)
  other arithmetic  9.39 us (2%)
    dot_general x30, matrix products, product(): return jnp.einsum(formula, left, right, precision=highest)  154 us
    all_to_all x1, blocking collectives, local(): return lax.all_to_all(result, 'tp', split_axis=0, concat_axis=1, tiled=True)  51.2 us
    all_to_all x1, waiting for transfers between devices, local(): lax.all_to_all(convolved, 'ctx', split_axis=1, concat_axis=0, tiled=True)  24.8 us
    all_to_all x1, waiting for transfers between devices, local(): lax.all_to_all(query_proj, 'tp', split_axis=1, concat_axis=0, tiled=True)  24.4 us
    all_to_all x1, waiting for transfers between devices, local(): lax.all_to_all(key_proj, 'tp', split_axis=1, concat_axis=0, tiled=True)  22.9 us
    ppermute x1, waiting for transfers between devices, passed_along(): return lax.ppermute(value, axis, pairs)  18.9 us
    all_to_all x1, waiting for transfers between devices, local(): lax.all_to_all(value_proj, 'tp', split_axis=1, concat_axis=0, tiled=True)  18.2 us
    unnamed x36, local copies, waits for them, and re-layouts  13.3 us
  transfers between devices with their start and end apart: 7, of which 5 were waited for; matrix products, arithmetic and copies ran while one was open for 18% of the time, Pallas kernels for 0%

commit v1 on v0

v1 whole, which is shorter than its diff:
```python
import functools

import jax
import jax.numpy as jnp
import ml_dtypes
import numpy as np
from jax import lax
from jax.experimental import pallas as pl
from jax.experimental.pallas import tpu as pltpu
from jax.sharding import PartitionSpec as P

LANES = 128
PAD = 8
SPAN = 240.0
BOTH = ("ctx", "tp")
bf16, f32 = jnp.bfloat16, jnp.float32


def split_table(table):
    high = table.astype(ml_dtypes.bfloat16)
    low = (table - high.astype(np.float64)).astype(ml_dtypes.bfloat16)
    return np.stack([high, low])


@functools.lru_cache(maxsize=None)
def transform_tables(rows):
    m = np.arange(rows)
    k1 = np.arange(rows) + 0.5
    b = np.arange(LANES)
    outer = 2.0 * np.pi * np.outer(k1, m) / (2 * rows)
    inner = 2.0 * np.pi * (np.outer(b, b) % LANES) / LANES
    twist = 2.0 * np.pi * np.outer(k1, b) / (2 * LANES * rows)
    c, s = np.cos(inner), np.sin(inner)
    outer_forward = np.concatenate([np.cos(outer), -np.sin(outer)], 0)
    inner_forward = np.block([[c, -s], [s, c]])
    return (
        split_table(outer_forward),
        split_table(inner_forward),
        split_table(inner_forward.T),
        split_table(outer_forward.T),
        np.stack([np.cos(twist), -np.sin(twist)]).astype(np.float32),
    )


def halves(value):
    high = value.astype(bf16)
    return high, (value - high.astype(f32)).astype(bf16)


def mm(left, right):
    return jnp.dot(left, right, preferred_element_type=f32)


def product(left, right):
    return mm(left[0], right[0]) + (mm(left[1], right[0]) + mm(left[0], right[1]))


def pair(ref):
    return ref[0], ref[1]


def forward(signal, rows, outer, inner, twist):
    group = signal.shape[1] // LANES
    columns = product(pair(outer), halves(signal))
    cos, sin = twist[0], twist[1]
    stacked = []
    for p in range(group):
        re = columns[:rows, p * LANES : (p + 1) * LANES]
        im = columns[rows:, p * LANES : (p + 1) * LANES]
        stacked.append(jnp.concatenate([re * cos - im * sin, re * sin + im * cos], 1))
    return product(halves(jnp.concatenate(stacked, 0)), pair(inner))


def backward(spectrum, rows, inner, outer, twist):
    group = spectrum.shape[0] // rows
    lines = product(halves(spectrum), pair(inner))
    cos, sin = twist[0], twist[1]
    columns = []
    for p in range(group):
        re = lines[p * rows : (p + 1) * rows, :LANES]
        im = lines[p * rows : (p + 1) * rows, LANES:]
        columns.append(jnp.concatenate([re * cos + im * sin, im * cos - re * sin], 0))
    return product(pair(outer), halves(jnp.concatenate(columns, 1)))


def encode(value, inverse_scale):
    magnitude = jnp.exp2(jnp.abs(value) * inverse_scale * SPAN - SPAN / 2)
    return jnp.where(value < 0, -magnitude, magnitude)


def decode(code, scale):
    magnitude = (jnp.log2(jnp.abs(code)) + SPAN / 2) * (scale * (1.0 / SPAN))
    return jnp.where(code < 0, -magnitude, magnitude)


def block_scale(largest):
    return jnp.maximum(largest * 1.0078125, 1e-30).astype(bf16).astype(f32)


def short_conv(ext_ref, weights, length):
    return (
        weights[0:1] * ext_ref[8 : 8 + length]
        + weights[1:2] * ext_ref[7 : 7 + length]
        + weights[2:3] * ext_ref[6 : 6 + length]
    )


def fill(ext_ref, current, before):
    ext_ref[6:8] = before.astype(f32)
    ext_ref[8 : 8 + current.shape[0]] = current[...].astype(f32)


def lane_index(shape):
    return lax.broadcasted_iota(jnp.int32, shape, 1)


def rows_out_kernel(dims, idx_ref, k_ref, v_ref, halo_ref, w_ref, out_ref, k_ext, v_ext):
    length, per, parts = dims
    steps = length // LANES
    fill(k_ext, k_ref, halo_ref[2:4])
    fill(v_ext, v_ref, halo_ref[4:6])
    weights = w_ref[0]
    mixed = short_conv(k_ext, weights[3:6], length) * short_conv(v_ext, weights[6:9], length)
    codes, scales = [], []
    for step in range(steps):
        block = mixed[step * LANES : (step + 1) * LANES]
        scale = block_scale(jnp.max(jnp.abs(block), 0, keepdims=True))
        scales.append(jnp.broadcast_to(scale, (PAD, LANES)))
        codes.append(encode(block, 1.0 / scale).T)
    lane = lane_index((PAD, LANES))
    for g in range(parts):
        piece = [code[g * per : (g + 1) * per] for code in codes]
        line = jnp.ones((PAD, LANES), f32)
        for step in range(steps):
            moved = pltpu.roll(scales[step], ((step - g) * per) % LANES, 1)
            inside = (lane >= step * per) & (lane < (step + 1) * per)
            line = jnp.where(inside, moved, line)
        out_ref[g, 0] = jnp.concatenate(piece + [line], 0).astype(bf16)


def gate_parts_kernel(
    length, idx_ref, q_ref, k_ref, v_ref, halo_ref, w_ref, short_ref, skip_ref, q_ext, k_ext, v_ext
):
    fill(q_ext, q_ref, halo_ref[0:2])
    fill(k_ext, k_ref, halo_ref[2:4])
    fill(v_ext, v_ref, halo_ref[4:6])
    weights = w_ref[0]
    mixed = short_conv(k_ext, weights[3:6], length) * short_conv(v_ext, weights[6:9], length)
    short_ref[...] = short_conv(q_ext, weights[0:3], length)
    skip_ref[...] = weights[9:10] * mixed


def gate_kernel(dims, y_ref, short_ref, skip_ref, out_ref):
    length, per, parts = dims
    steps = length // LANES
    rows = steps * per
    tiles = [y_ref[g, 0].astype(f32) for g in range(parts)]
    lane = lane_index((PAD, LANES))
    for step in range(steps):
        code = jnp.concatenate([t[step * per : (step + 1) * per] for t in tiles], 0).T
        scale = jnp.ones((PAD, LANES), f32)
        for g in range(parts):
            moved = pltpu.roll(tiles[g][rows:], ((g - step) * per) % LANES, 1)
            inside = (lane >= g * per) & (lane < (g + 1) * per)
            scale = jnp.where(inside, moved, scale)
        here = pl.ds(step * LANES, LANES)
        out_ref[here, :] = short_ref[here, :] * (decode(code, scale[0:1]) + skip_ref[here, :])


def filter_rows_kernel(dims, idx_ref, h_ref, *refs):
    per, peers = dims
    outs, turned = refs[:-1], refs[-1]
    me = idx_ref[0]
    for r in range(h_ref.shape[0] // LANES):
        for c in range(h_ref.shape[1] // LANES):
            block = h_ref[r * LANES : (r + 1) * LANES, c * LANES : (c + 1) * LANES].T
            for g in range(LANES // per):
                turned[c * (LANES // per) + g] = block[g * per : (g + 1) * per]
        for s in range(peers):
            outs[s][r] = turned[lax.bitwise_xor(me, s)]


def filter_kernel(dims, idx_ref, *refs):
    rows, per, peers, group = dims
    pieces = refs[:peers]
    outer, inner, twist, out_ref, held, sems = refs[peers:]
    me = idx_ref[0]
    size = rows // peers * per
    copies = []
    for s in range(peers):
        start = pl.multiple_of(lax.bitwise_xor(me, s) * size, 8)
        copies.append(pltpu.make_async_copy(pieces[s], held.at[pl.ds(start, size)], sems.at[s]))
        copies[-1].start()
    for copy in copies:
        copy.wait()

    def body(i, carry):
        first = i * group
        signal = jnp.concatenate(
            [held[pl.ds(first + p, rows, stride=per), :] for p in range(group)], 1
        )
        spectrum = forward(signal, rows, outer, inner, twist) * (1.0 / (LANES * rows))
        for p in range(group):
            out_ref[first + p] = spectrum[p * rows : (p + 1) * rows]
        return carry

    lax.fori_loop(0, per // group, body, 0)


def conv_kernel(
    dims, x_ref, h_ref, outer, inner, inner_back, outer_back, twist, out_ref, held
):
    rows, per, lines, blocks, group = dims

    def unpack(i, carry):
        tile = x_ref[i].astype(f32)
        scale = jnp.broadcast_to(tile[lines : lines + 1], (LANES, LANES)).T[:lines]
        start = pl.multiple_of(i * lines, 8)
        held[pl.ds(start, lines), :] = decode(tile[:lines], scale)
        return carry

    lax.fori_loop(0, blocks, unpack, 0)

    def body(i, carry):
        first = i * group
        signal = jnp.concatenate(
            [held[pl.ds(first + p, rows, stride=per), :] for p in range(group)], 1
        )
        spectrum = forward(signal, rows, outer, inner, twist)
        joined = []
        for p in range(group):
            re = spectrum[p * rows : (p + 1) * rows, :LANES]
            im = spectrum[p * rows : (p + 1) * rows, LANES:]
            h_re, h_im = h_ref[first + p, :, :LANES], h_ref[first + p, :, LANES:]
            joined.append(jnp.concatenate([re * h_re - im * h_im, re * h_im + im * h_re], 1))
        result = backward(jnp.concatenate(joined, 0), rows, inner_back, outer_back, twist)
        for p in range(group):
            held[pl.ds(first + p, rows, stride=per), :] = result[:, p * LANES : (p + 1) * LANES]
        return carry

    lax.fori_loop(0, per // group, body, 0)

    def pack(i, carry):
        start = pl.multiple_of(i * lines, 8)
        tile = held[pl.ds(start, lines), :]
        scale = block_scale(jnp.max(jnp.abs(tile), 1, keepdims=True))
        code = encode(tile, 1.0 / scale)
        wide = jnp.broadcast_to(scale, (lines, LANES))
        if lines < LANES:
            wide = jnp.concatenate([wide, jnp.ones((LANES - lines, LANES), f32)], 0)
        out_ref[i] = jnp.concatenate([code, wide.T[:PAD]], 0).astype(bf16)
        return carry

    lax.fori_loop(0, blocks, pack, 0)


def whole(array):
    return pl.BlockSpec(array.shape, lambda *_: (0,) * len(array.shape))


PARAMS = dict(vmem_limit_bytes=48 * 1024 * 1024)


def local(sizes, query, key, value, long_filter, short_filter, skip_bias):
    peers, depth = sizes
    devices = peers * depth
    length, width = query.shape
    shard = long_filter.shape[1]
    per = shard // peers
    rows = length * devices // LANES
    lines = length // LANES * per
    parts = LANES // per
    tiles = shard // LANES
    group = 4
    me = jnp.stack([lax.axis_index("ctx"), lax.axis_index("tp")]).astype(jnp.int32)
    tables = transform_tables(rows)
    outer, inner, inner_back, outer_back, twist = (jnp.asarray(t) for t in tables)

    def crossed(array, axis, count):
        return [array[0]] + [
            lax.ppermute(array[s], axis, [(i, i ^ s) for i in range(count)])
            for s in range(1, count)
        ]

    edge = jnp.concatenate([query[-2:], key[-2:], value[-2:]], 0)
    halo = lax.ppermute(edge, BOTH, [(i, i + 1) for i in range(devices - 1)])
    own = jnp.concatenate([short_filter.reshape(9, shard), skip_bias[None]], 0)
    taps = jnp.stack(crossed([own] * depth, "tp", depth))

    chunk = long_filter.shape[0] // LANES
    step = min(4, chunk)
    pieces = pl.pallas_call(
        functools.partial(filter_rows_kernel, (per, peers)),
        grid_spec=pltpu.PrefetchScalarGridSpec(
            num_scalar_prefetch=1,
            grid=(chunk // step,),
            in_specs=[pl.BlockSpec((step * LANES, shard), lambda i, _: (i, 0))],
            out_specs=[pl.BlockSpec((step, per, LANES), lambda i, _: (i, 0, 0))] * peers,
            scratch_shapes=[pltpu.VMEM((peers, per, LANES), f32)],
        ),
        out_shape=[jax.ShapeDtypeStruct((chunk, per, LANES), f32)] * peers,
        compiler_params=pltpu.CompilerParams(**PARAMS),
        name="filter_rows",
    )(me, long_filter)
    pieces = crossed(pieces, "ctx", peers)
    pieces = [piece.reshape(chunk * per, LANES) for piece in pieces]

    row_spec = pl.BlockSpec((length, LANES), lambda j, _: (0, j))
    halo_spec = pl.BlockSpec((6, LANES), lambda j, _: (0, j))
    tap_spec = pl.BlockSpec(
        (1, 10, LANES), lambda j, idx: (lax.bitwise_xor(idx[1], j // tiles), 0, j % tiles)
    )
    wire_shape = jax.ShapeDtypeStruct((peers, depth, lines + PAD, LANES), bf16)
    ext = pltpu.VMEM((length + 8, LANES), f32)
    coded = pl.pallas_call(
        functools.partial(rows_out_kernel, (length, per, parts)),
        grid_spec=pltpu.PrefetchScalarGridSpec(
            num_scalar_prefetch=1,
            grid=(width // LANES,),
            in_specs=[row_spec, row_spec, halo_spec, tap_spec],
            out_specs=pl.BlockSpec(
                (parts, 1, lines + PAD, LANES), lambda j, _: (j % tiles, j // tiles, 0, 0)
            ),
            scratch_shapes=[ext] * 2,
        ),
        out_shape=wire_shape,
        compiler_params=pltpu.CompilerParams(**PARAMS),
        name="mixed_rows",
    )(me, key, value, halo, taps)
    coded = coded.reshape(devices, lines + PAD, LANES)
    arrived = lax.all_to_all(coded, BOTH, split_axis=0, concat_axis=0, tiled=True)

    spectrum = pl.pallas_call(
        functools.partial(filter_kernel, (rows, per, peers, group)),
        grid_spec=pltpu.PrefetchScalarGridSpec(
            num_scalar_prefetch=1,
            grid=(1,),
            in_specs=[pl.BlockSpec(memory_space=pl.ANY)] * peers
            + [whole(outer), whole(inner), whole(twist)],
            out_specs=pl.BlockSpec((per, rows, 2 * LANES), lambda *_: (0, 0, 0)),
            scratch_shapes=[
                pltpu.VMEM((rows * per, LANES), f32),
                pltpu.SemaphoreType.DMA((peers,)),
            ],
        ),
        out_shape=jax.ShapeDtypeStruct((per, rows, 2 * LANES), f32),
        compiler_params=pltpu.CompilerParams(**PARAMS),
        name="filter_spectrum",
    )(me, *pieces, outer, inner, twist)

    query_short, skip = pl.pallas_call(
        functools.partial(gate_parts_kernel, length),
        grid_spec=pltpu.PrefetchScalarGridSpec(
            num_scalar_prefetch=1,
            grid=(width // LANES,),
            in_specs=[row_spec, row_spec, row_spec, halo_spec, tap_spec],
            out_specs=[row_spec, row_spec],
            scratch_shapes=[ext] * 3,
        ),
        out_shape=[jax.ShapeDtypeStruct((length, width), f32)] * 2,
        compiler_params=pltpu.CompilerParams(**PARAMS),
        name="gate_parts",
    )(me, query, key, value, halo, taps)

    convolved = pl.pallas_call(
        functools.partial(conv_kernel, (rows, per, lines, devices, group)),
        out_shape=jax.ShapeDtypeStruct((devices, lines + PAD, LANES), bf16),
        scratch_shapes=[pltpu.VMEM((rows * per, LANES), f32)],
        compiler_params=pltpu.CompilerParams(**PARAMS),
        name="long_conv",
    )(arrived, spectrum, outer, inner, inner_back, outer_back, twist)
    returned = lax.all_to_all(convolved, BOTH, split_axis=0, concat_axis=0, tiled=True)
    returned = returned.reshape(peers, depth, lines + PAD, LANES)

    row_spec = pl.BlockSpec((length, LANES), lambda j: (0, j))
    return pl.pallas_call(
        functools.partial(gate_kernel, (length, per, parts)),
        grid=(width // LANES,),
        in_specs=[
            pl.BlockSpec(
                (parts, 1, lines + PAD, LANES), lambda j: (j % tiles, j // tiles, 0, 0)
            ),
            row_spec,
            row_spec,
        ],
        out_specs=row_spec,
        out_shape=jax.ShapeDtypeStruct((length, width), f32),
        compiler_params=pltpu.CompilerParams(**PARAMS),
        name="gate",
    )(returned, query_short, skip)


def solution(mesh):
    sizes = (mesh.shape["ctx"], mesh.shape["tp"])
    return jax.shard_map(
        functools.partial(local, sizes),
        mesh=mesh,
        in_specs=(
            P(BOTH, None),
            P(BOTH, None),
            P(BOTH, None),
            P("ctx", "tp"),
            P(None, None, "tp"),
            P("tp"),
        ),
        out_specs=P(BOTH, None),
        check_vma=False,
    )
```

time: 399 us -> 141 us (0.35)
  the two profiles are of different devices: /device:TPU:2 before, /device:TPU:1 now
where the time goes in v1:
time: 141 us; the launch traced here: 140 us
  waiting for transfers between devices  51.4 us (36%)
  Pallas kernels  51.4 us (36%)
  starting transfers between devices  24.2 us (17%)
  local copies, waits for them, and re-layouts  11.8 us (8%)
  other arithmetic  1.48 us (1%)
    ppermute x10, waiting for transfers between devices, crossed(): lax.ppermute(array[s], axis, [(i, i ^ s) for i in range(count)])  27 us
    pallas_call x1, Pallas kernels, local(): pl.pallas_call(functools.partial(conv_kernel, (rows, per, lines, devices,...  25.2 us
    all_to_all x1, waiting for transfers between devices, local(): lax.all_to_all(convolved, BOTH, split_axis=0, concat_axis=0, tiled=True)  19.4 us
    ppermute x10, starting transfers between devices, crossed(): lax.ppermute(array[s], axis, [(i, i ^ s) for i in range(count)])  13 us
    pallas_call x1, Pallas kernels, local(): pl.pallas_call(functools.partial(filter_kernel, (rows, per, peers, group)...  9.34 us
    unnamed x38, local copies, waits for them, and re-layouts  8.92 us
    pallas_call x1, Pallas kernels, local(): pl.pallas_call(functools.partial(gate_parts_kernel, length), grid_spec=pl...  5.7 us
    pallas_call x1, Pallas kernels, local(): pl.pallas_call(functools.partial(rows_out_kernel, (length, per, parts)),...  5.47 us
  transfers between devices with their start and end apart: 13, of which 6 were waited for; matrix products, arithmetic and copies ran while one was open for 2% of the time, Pallas kernels for 12%

profile of v1, /device:TPU:1, one launch (start us, length us, event | category | flops | bytes accessed | tf_op | source)
XLA Modules:
  0.0 140.4 jit_solution(10329403728681282634)
XLA Ops:
  0.0 0.7 reshape.33
  0.7 0.7 pad_maximum_fusion.2
  1.4 2.1 %collective-permute-start.1 = (f32[10,256]{1,0:T(8,128)S(1)}, f32[10,256]{1,0:T(8,128)S(1)}, u32[]{:S(2)}, u32[]{:S(2)}) collective-permute-start(f32[10,256]{1,0:T(8,128)S(1)} %pad_maximum_fusion.2), channel_id=1, source_target_pairs={{0,1},{1,0},{2,3},{3,2},{4,5},{5,4},{6,7},{7,6},{8,9},{9,8},{10,11... | collective-permute-start | bytes 30728 | tf_op jit(solution)/shard_map/ppermute | solution.py:281
  3.5 2.3 %collective-permute-start.2 = (f32[10,256]{1,0:T(8,128)S(1)}, f32[10,256]{1,0:T(8,128)S(1)}, u32[]{:S(2)}, u32[]{:S(2)}) collective-permute-start(f32[10,256]{1,0:T(8,128)S(1)} %pad_maximum_fusion.2), channel_id=1, source_target_pairs={{0,2},{1,3},{2,0},{3,1},{4,6},{5,7},{6,4},{7,5},{8,10},{9,11},{10,... | collective-permute-start | bytes 30728 | tf_op jit(solution)/shard_map/ppermute | solution.py:281
  5.8 0.0 collective-permute-start.3
  5.8 0.7 slice.10
  6.6 0.7 slice.11
  7.3 0.7 slice.9
  8.0 2.2 %collective-permute-start = (bf16[6,1024]{1,0:T(8,128)(2,1)S(1)}, bf16[6,1024]{1,0:T(8,128)(2,1)S(1)}, u32[]{:S(2)}, u32[]{:S(2)}) collective-permute-start(bf16[6,1024]{1,0:T(8,128)(2,1)S(1)} %pad_maximum_fusion.1), channel_id=1, source_target_pairs={{0,1},{1,2},{2,3},{3,4},{4,5},{5,6},{6,7},{7,8},{8,9},{9,10},{10,1... | collective-permute-start | bytes 36872 | tf_op jit(solution)/shard_map/ppermute | solution.py:286
  10.3 0.7 fusion
  11.0 0.1 pad_add_fusion.idx_ref
  11.1 0.0 collective-permute-done.1
  11.1 0.0 collective-permute-done.2
  11.1 0.0 collective-permute-done.3
  11.1 4.9 %collective-permute-done.halo_ref = bf16[6,1024]{1,0:T(8,128)(2,1)S(1)} collective-permute-done((bf16[6,1024]{1,0:T(8,128)(2,1)S(1)}, bf16[6,1024]{1,0:T(8,128)(2,1)S(1)}, u32[]{:S(2)}, u32[]{:S(2)}) %collective-permute-start) | collective-permute-done | bytes 12320 | tf_op jit(solution)/shard_map/ppermute | solution.py:286
  16.0 1.2 copy-done
  17.3 1.2 copy-done.2
  18.5 5.5 %mixed_rows.1 = bf16[8,4,136,128]{3,2,1,0:T(8,128)(2,1)} custom-call(s32[2]{0:T(128)S(1)} %pad_add_fusion.idx_ref, bf16[512,1024]{1,0:T(8,128)(2,1)S(1)} %copy-done, bf16[512,1024]{1,0:T(8,128)(2,1)S(1)} %copy-done.2, bf16[6,1024]{1,0:T(8,128)(2,1)S(1)} %collective-permute-done.halo_ref, f32[4,10,256]{2,1,0:T(8,128)S(1)} %pad_maximum_fusion.w_ref), custom_call_target="tpu_custom_call" | custom-call | tf_op jit(solution)/shard_map/mixed_rows/pallas_call | solution.py:315
  24.0 0.0 copy-done.16
  24.0 4.7 %all-to-all-start = ((bf16[32,136,128]{2,1,0:T(8,128)(2,1)}), bf16[32,136,128]{2,1,0:T(8,128)(2,1)S(1)}, u32[]{:S(2)}, u32[]{:S(2)}) async-start(bf16[32,136,128]{2,1,0:T(8,128)(2,1)} %bitcast.7), calls=%async_computation | async-start | bytes 2228224 | tf_op jit(solution)/shard_map/all_to_all | solution.py:331
  28.7 0.0 copy-done.7
  28.7 0.0 copy-start.17
  28.7 0.7 copy-done.17
  29.3 1.4 %filter_rows.1 = (f32[16,32,128]{2,1,0:T(8,128)S(1)}, f32[16,32,128]{2,1,0:T(8,128)S(1)}, f32[16,32,128]{2,1,0:T(8,128)S(1)}, f32[16,32,128]{2,1,0:T(8,128)S(1)}...) custom-call(s32[2]{0:T(128)S(1)} %copy-done.17, ...), custom_call_target="tpu_custom_call" | custom-call | tf_op jit(solution)/shard_map/filter_rows/pallas_call | solution.py:292
  30.8 1.5 %collective-permute-start.5 = (f32[16,32,128]{2,1,0:T(8,128)S(1)}, f32[16,32,128]{2,1,0:T(8,128)S(1)}, u32[]{:S(2)}, u32[]{:S(2)}) collective-permute-start(f32[16,32,128]{2,1,0:T(8,128)S(1)} %get-tuple-element.17), channel_id=1, source_target_pairs={{0,8},{4,12},{8,0},{12,4},{16,24},{20,28},{24,16},{28,20},{1,9},{5... | collective-permute-start | bytes 786440 | tf_op jit(solution)/shard_map/ppermute | solution.py:281
  32.3 0.5 collective-permute-start.6
  32.8 1.5 %collective-permute-start.7 = (f32[16,32,128]{2,1,0:T(8,128)S(1)}, f32[16,32,128]{2,1,0:T(8,128)S(1)}, u32[]{:S(2)}, u32[]{:S(2)}) collective-permute-start(f32[16,32,128]{2,1,0:T(8,128)S(1)} %get-tuple-element.19), channel_id=1, source_target_pairs={{0,16},{4,20},{8,24},{12,28},{16,0},{20,4},{24,8},{28,12},{1,17},{... | collective-permute-start | bytes 786440 | tf_op jit(solution)/shard_map/ppermute | solution.py:281
  34.2 0.3 collective-permute-start.8
  34.5 2.1 %collective-permute-start.9 = (f32[16,32,128]{2,1,0:T(8,128)S(1)}, f32[16,32,128]{2,1,0:T(8,128)S(1)}, u32[]{:S(2)}, u32[]{:S(2)}) collective-permute-start(f32[16,32,128]{2,1,0:T(8,128)S(1)} %get-tuple-element.21), channel_id=1, source_target_pairs={{0,24},{4,28},{8,16},{12,20},{16,8},{20,12},{24,0},{28,4},{1,25},{... | collective-permute-start | bytes 786440 | tf_op jit(solution)/shard_map/ppermute | solution.py:281
  36.7 8.5 %collective-permute-done.5 = f32[16,32,128]{2,1,0:T(8,128)S(1)} collective-permute-done((f32[16,32,128]{2,1,0:T(8,128)S(1)}, f32[16,32,128]{2,1,0:T(8,128)S(1)}, u32[]{:S(2)}, u32[]{:S(2)}) %collective-permute-start.5) | collective-permute-done | bytes 262176 | tf_op jit(solution)/shard_map/ppermute | solution.py:281
  45.2 2.7 %collective-permute-start.10 = (f32[16,32,128]{2,1,0:T(8,128)S(1)}, f32[16,32,128]{2,1,0:T(8,128)S(1)}, u32[]{:S(2)}, u32[]{:S(2)}) collective-permute-start(f32[16,32,128]{2,1,0:T(8,128)S(1)} %get-tuple-element.22), channel_id=1, source_target_pairs={{0,28},{4,24},{8,20},{12,16},{16,12},{20,8},{24,4},{28,0},{1,29},{... | collective-permute-start | bytes 786440 | tf_op jit(solution)/shard_map/ppermute | solution.py:281
  47.9 6.7 %collective-permute-done.6 = f32[16,32,128]{2,1,0:T(8,128)S(1)} collective-permute-done((f32[16,32,128]{2,1,0:T(8,128)S(1)}, f32[16,32,128]{2,1,0:T(8,128)S(1)}, u32[]{:S(2)}, u32[]{:S(2)}) %collective-permute-start.6) | collective-permute-done | bytes 262176 | tf_op jit(solution)/shard_map/ppermute | solution.py:281
  54.7 0.0 collective-permute-start.4
  54.7 0.0 collective-permute-done.7
  54.7 0.0 collective-permute-done.8
  54.7 5.9 %collective-permute-done.9 = f32[16,32,128]{2,1,0:T(8,128)S(1)} collective-permute-done((f32[16,32,128]{2,1,0:T(8,128)S(1)}, f32[16,32,128]{2,1,0:T(8,128)S(1)}, u32[]{:S(2)}, u32[]{:S(2)}) %collective-permute-start.9) | collective-permute-done | bytes 262176 | tf_op jit(solution)/shard_map/ppermute | solution.py:281
  60.6 5.8 %collective-permute-done.10 = f32[16,32,128]{2,1,0:T(8,128)S(1)} collective-permute-done((f32[16,32,128]{2,1,0:T(8,128)S(1)}, f32[16,32,128]{2,1,0:T(8,128)S(1)}, u32[]{:S(2)}, u32[]{:S(2)}) %collective-permute-start.10) | collective-permute-done | bytes 262176 | tf_op jit(solution)/shard_map/ppermute | solution.py:281
  66.4 0.0 collective-permute-done.4
  66.4 0.0 copy-done.9
  66.4 0.0 copy-done.10
  66.4 0.0 copy-done.12
  66.4 0.0 copy-start.11
  66.4 0.0 copy-start.13
  66.4 0.0 copy-start.14
  66.5 0.0 copy-start.15
  66.5 9.3 %filter_spectrum.1.h_ref = f32[32,128,256]{2,1,0:T(8,128)} custom-call(s32[2]{0:T(128)S(1)} %copy-done.17, f32[512,128]{1,0:T(8,128)S(1)} %bitcast.19, f32[512,128]{1,0:T(8,128)S(1)} %bitcast.26, f32[512,128]{1,0:T(8,128)S(1)} %bitcast.20, f32[512,128]{1,0:T(8,128)S(1)} %bitcast.21, f32[512,128]{1,0:T(8,128)S(1)} %bitcast.22, f32[512,128]{1,0:T(8,128)S(1)} %bitcast.23, ...), custom_call_target="tpu_custom_call" | custom-call | tf_op jit(solution)/shard_map/filter_spectrum/pallas_call | solution.py:333
  75.8 0.0 all-to-all-done.x_ref
  75.8 0.0 copy-done.11
  75.8 0.0 copy-done.13
  75.8 0.0 copy-done.14
  75.9 0.0 copy-done.15
  75.9 25.2 %long_conv.1 = bf16[32,136,128]{2,1,0:T(8,128)(2,1)} custom-call(bf16[32,136,128]{2,1,0:T(8,128)(2,1)S(1)} %all-to-all-done.x_ref, f32[32,128,256]{2,1,0:T(8,128)} %filter_spectrum.1.h_ref, bf16[2,256,128]{2,1,0:T(8,128)(2,1)S(1)} %copy-done.11, bf16[2,256,256]{2,1,0:T(8,128)(2,1)S(1)} %copy-done.9, bf16[2,256,256]{2,1,0:T(8,128)(2,1)S(1)} %copy-done.14, ...), custom_call_target="tpu_custom_call" | custom-call | tf_op jit(solution)/shard_map/long_conv/pallas_call | solution.py:365
  101.1 4.2 %all-to-all-start.1 = ((bf16[32,136,128]{2,1,0:T(8,128)(2,1)}), bf16[32,136,128]{2,1,0:T(8,128)(2,1)S(1)}, u32[]{:S(2)}, u32[]{:S(2)}) async-start(bf16[32,136,128]{2,1,0:T(8,128)(2,1)} %long_conv.1), calls=%async_computation.1 | async-start | bytes 2228224 | tf_op jit(solution)/shard_map/all_to_all | solution.py:372
  105.3 0.0 copy-done.1
  105.3 0.0 copy-done.3
  105.3 0.0 copy-done.18
  105.3 0.0 copy-start.8
  105.3 1.2 copy-done.8
  106.5 5.7 %gate_parts.1 = (f32[512,1024]{1,0:T(8,128)S(1)}, f32[512,1024]{1,0:T(8,128)}) custom-call(s32[2]{0:T(128)S(1)} %copy-done.18, bf16[512,1024]{1,0:T(8,128)(2,1)S(1)} %copy-done.8, bf16[512,1024]{1,0:T(8,128)(2,1)S(1)} %copy-done.1, bf16[512,1024]{1,0:T(8,128)(2,1)S(1)} %copy-done.3, bf16[6,1024]{1,0:T(8,128)(2,1)S(1)} %collective-permute-done.halo_ref, ...), custom_call_target="tpu_custom_call" | custom-call | tf_op jit(solution)/shard_map/gate_parts/pallas_call | solution.py:351
  112.2 1.3 copy-done.4
  113.6 19.4 %all-to-all-done.1 = bf16[32,136,128]{2,1,0:T(8,128)(2,1)S(1)} async-done(((bf16[32,136,128]{2,1,0:T(8,128)(2,1)}), bf16[32,136,128]{2,1,0:T(8,128)(2,1)S(1)}, u32[]{:S(2)}, u32[]{:S(2)}) %all-to-all-start.1) | async-done | bytes 1114144 | tf_op jit(solution)/shard_map/all_to_all | solution.py:372
  133.0 1.6 %copy-done.5 = f32[512,1024]{1,0:T(8,128)S(1)} copy-done((f32[512,1024]{1,0:T(8,128)S(1)}, f32[512,1024]{1,0:T(8,128)}, u32[]{:S(2)}) %copy-start.5) | copy-done | bytes 2097176
  134.6 1.6 %copy-done.6 = f32[512,1024]{1,0:T(8,128)S(1)} copy-done((f32[512,1024]{1,0:T(8,128)S(1)}, f32[512,1024]{1,0:T(8,128)}, u32[]{:S(2)}) %copy-start.6) | copy-done | bytes 2097176
  136.2 4.2 %gate.1 = f32[512,1024]{1,0:T(8,128)} custom-call(bf16[8,4,136,128]{3,2,1,0:T(8,128)(2,1)S(1)} %bitcast.18, f32[512,1024]{1,0:T(8,128)S(1)} %copy-done.5, f32[512,1024]{1,0:T(8,128)S(1)} %copy-done.6), custom_call_target="tpu_custom_call" | custom-call | tf_op jit(solution)/shard_map/gate/pallas_call | solution.py:376
  (15 shorter events, 0.0 us)
Async XLA Ops:
  1.4 9.7 %collective-permute-start.1 = (f32[10,256]{1,0:T(8,128)S(1)}, f32[10,256]{1,0:T(8,128)S(1)}, u32[]{:S(2)}, u32[]{:S(2)}) collective-permute-start(f32[10,256]{1,0:T(8,128)S(1)} %pad_maximum_fusion.2), channel_id=1, source_target_pairs={{0,1},{1,0},{2,3},{3,2},{4,5},{5,4},{6,7},{7,6},{8,9},{9,8},{10,11... | collective-permute-start | bytes 30728 | tf_op jit(solution)/shard_map/ppermute | solution.py:281
  3.5 7.5 %collective-permute-start.2 = (f32[10,256]{1,0:T(8,128)S(1)}, f32[10,256]{1,0:T(8,128)S(1)}, u32[]{:S(2)}, u32[]{:S(2)}) collective-permute-start(f32[10,256]{1,0:T(8,128)S(1)} %pad_maximum_fusion.2), channel_id=1, source_target_pairs={{0,2},{1,3},{2,0},{3,1},{4,6},{5,7},{6,4},{7,5},{8,10},{9,11},{10,... | collective-permute-start | bytes 30728 | tf_op jit(solution)/shard_map/ppermute | solution.py:281
  5.8 5.2 %collective-permute-start.3 = (f32[10,256]{1,0:T(8,128)S(1)}, f32[10,256]{1,0:T(8,128)S(1)}, u32[]{:S(2)}, u32[]{:S(2)}) collective-permute-start(f32[10,256]{1,0:T(8,128)S(1)} %pad_maximum_fusion.2), channel_id=1, source_target_pairs={{0,3},{1,2},{2,1},{3,0},{4,7},{5,6},{6,5},{7,4},{8,11},{9,10},{10,... | collective-permute-start | bytes 30728 | tf_op jit(solution)/shard_map/ppermute | solution.py:281
  8.0 8.0 %collective-permute-start = (bf16[6,1024]{1,0:T(8,128)(2,1)S(1)}, bf16[6,1024]{1,0:T(8,128)(2,1)S(1)}, u32[]{:S(2)}, u32[]{:S(2)}) collective-permute-start(bf16[6,1024]{1,0:T(8,128)(2,1)S(1)} %pad_maximum_fusion.1), channel_id=1, source_target_pairs={{0,1},{1,2},{2,3},{3,4},{4,5},{5,6},{6,7},{7,8},{8,9},{9,10},{10,1... | collective-permute-start | bytes 36872 | tf_op jit(solution)/shard_map/ppermute | solution.py:286
  11.1 12.9 %copy-start.16 = (s32[2]{0:T(128)}, s32[2]{0:T(128)S(1)}, u32[]{:S(2)}) copy-start(s32[2]{0:T(128)S(1)} %pad_add_fusion.idx_ref) | copy-start | bytes 28
  16.0 1.2 copy-start
  17.2 1.2 copy-start.2
  18.5 10.2 %copy-start.7 = (f32[2048,256]{1,0:T(8,128)S(1)}, f32[2048,256]{1,0:T(8,128)}, u32[]{:S(2)}) copy-start(f32[2048,256]{1,0:T(8,128)} %h_ref.1) | copy-start | bytes 6291460
  24.0 42.4 %copy-start.9 = (bf16[2,256,256]{2,1,0:T(8,128)(2,1)S(1)}, bf16[2,256,256]{2,1,0:T(8,128)(2,1)}, u32[]{:S(2)}) copy-start(bf16[2,256,256]{2,1,0:T(8,128)(2,1)} %constant.20.clone.refs_9_.inner) | copy-start | bytes 786436
  24.0 51.9 %all-to-all-start = ((bf16[32,136,128]{2,1,0:T(8,128)(2,1)}), bf16[32,136,128]{2,1,0:T(8,128)(2,1)S(1)}, u32[]{:S(2)}, u32[]{:S(2)}) async-start(bf16[32,136,128]{2,1,0:T(8,128)(2,1)} %bitcast.7), calls=%async_computation | async-start | bytes 2228224 | tf_op jit(solution)/shard_map/all_to_all | solution.py:331
  28.7 0.7 copy-start.17
  29.3 37.1 %copy-start.10 = (bf16[2,256,128]{2,1,0:T(8,128)(2,1)S(1)}, bf16[2,256,128]{2,1,0:T(8,128)(2,1)}, u32[]{:S(2)}) copy-start(bf16[2,256,128]{2,1,0:T(8,128)(2,1)} %constant.19.clone.refs_8_.outer) | copy-start | bytes 393220
  29.3 37.1 %copy-start.12 = (f32[2,128,128]{2,1,0:T(8,128)S(1)}, f32[2,128,128]{2,1,0:T(8,128)}, u32[]{:S(2)}) copy-start(f32[2,128,128]{2,1,0:T(8,128)} %constant.23.clone.refs_10_.twist) | copy-start | bytes 393220
  30.8 14.4 %collective-permute-start.5 = (f32[16,32,128]{2,1,0:T(8,128)S(1)}, f32[16,32,128]{2,1,0:T(8,128)S(1)}, u32[]{:S(2)}, u32[]{:S(2)}) collective-permute-start(f32[16,32,128]{2,1,0:T(8,128)S(1)} %get-tuple-element.17), channel_id=1, source_target_pairs={{0,8},{4,12},{8,0},{12,4},{16,24},{20,28},{24,16},{28,20},{1,9},{5... | collective-permute-start | bytes 786440 | tf_op jit(solution)/shard_map/ppermute | solution.py:281
  32.3 22.4 %collective-permute-start.6 = (f32[16,32,128]{2,1,0:T(8,128)S(1)}, f32[16,32,128]{2,1,0:T(8,128)S(1)}, u32[]{:S(2)}, u32[]{:S(2)}) collective-permute-start(f32[16,32,128]{2,1,0:T(8,128)S(1)} %get-tuple-element.18), channel_id=1, source_target_pairs={{0,12},{4,8},{8,4},{12,0},{16,28},{20,24},{24,20},{28,16},{1,13},{... | collective-permute-start | bytes 786440 | tf_op jit(solution)/shard_map/ppermute | solution.py:281
  32.8 21.9 %collective-permute-start.7 = (f32[16,32,128]{2,1,0:T(8,128)S(1)}, f32[16,32,128]{2,1,0:T(8,128)S(1)}, u32[]{:S(2)}, u32[]{:S(2)}) collective-permute-start(f32[16,32,128]{2,1,0:T(8,128)S(1)} %get-tuple-element.19), channel_id=1, source_target_pairs={{0,16},{4,20},{8,24},{12,28},{16,0},{20,4},{24,8},{28,12},{1,17},{... | collective-permute-start | bytes 786440 | tf_op jit(solution)/shard_map/ppermute | solution.py:281
  34.2 20.4 %collective-permute-start.8 = (f32[16,32,128]{2,1,0:T(8,128)S(1)}, f32[16,32,128]{2,1,0:T(8,128)S(1)}, u32[]{:S(2)}, u32[]{:S(2)}) collective-permute-start(f32[16,32,128]{2,1,0:T(8,128)S(1)} %get-tuple-element.20), channel_id=1, source_target_pairs={{0,20},{4,16},{8,28},{12,24},{16,4},{20,0},{24,12},{28,8},{1,21},{... | collective-permute-start | bytes 786440 | tf_op jit(solution)/shard_map/ppermute | solution.py:281
  34.5 26.1 %collective-permute-start.9 = (f32[16,32,128]{2,1,0:T(8,128)S(1)}, f32[16,32,128]{2,1,0:T(8,128)S(1)}, u32[]{:S(2)}, u32[]{:S(2)}) collective-permute-start(f32[16,32,128]{2,1,0:T(8,128)S(1)} %get-tuple-element.21), channel_id=1, source_target_pairs={{0,24},{4,28},{8,16},{12,20},{16,8},{20,12},{24,0},{28,4},{1,25},{... | collective-permute-start | bytes 786440 | tf_op jit(solution)/shard_map/ppermute | solution.py:281
  45.2 21.2 %collective-permute-start.10 = (f32[16,32,128]{2,1,0:T(8,128)S(1)}, f32[16,32,128]{2,1,0:T(8,128)S(1)}, u32[]{:S(2)}, u32[]{:S(2)}) collective-permute-start(f32[16,32,128]{2,1,0:T(8,128)S(1)} %get-tuple-element.22), channel_id=1, source_target_pairs={{0,28},{4,24},{8,20},{12,16},{16,12},{20,8},{24,4},{28,0},{1,29},{... | collective-permute-start | bytes 786440 | tf_op jit(solution)/shard_map/ppermute | solution.py:281
  54.7 11.7 %collective-permute-start.4 = (f32[16,32,128]{2,1,0:T(8,128)S(1)}, f32[16,32,128]{2,1,0:T(8,128)S(1)}, u32[]{:S(2)}, u32[]{:S(2)}) collective-permute-start(f32[16,32,128]{2,1,0:T(8,128)S(1)} %get-tuple-element.16), channel_id=1, source_target_pairs={{0,4},{4,0},{8,12},{12,8},{16,20},{20,16},{24,28},{28,24},{1,5},{5... | collective-permute-start | bytes 786440 | tf_op jit(solution)/shard_map/ppermute | solution.py:281
  66.4 9.4 %copy-start.11 = (bf16[2,256,128]{2,1,0:T(8,128)(2,1)S(1)}, bf16[2,256,128]{2,1,0:T(8,128)(2,1)}, u32[]{:S(2)}) copy-start(bf16[2,256,128]{2,1,0:T(8,128)(2,1)} %constant.19.clone.refs_8_.outer) | copy-start | bytes 393220
  66.4 9.4 %copy-start.13 = (f32[2,128,128]{2,1,0:T(8,128)S(1)}, f32[2,128,128]{2,1,0:T(8,128)}, u32[]{:S(2)}) copy-start(f32[2,128,128]{2,1,0:T(8,128)} %constant.23.clone.refs_10_.twist) | copy-start | bytes 393220
  66.4 9.4 %copy-start.14 = (bf16[2,256,256]{2,1,0:T(8,128)(2,1)S(1)}, bf16[2,256,256]{2,1,0:T(8,128)(2,1)}, u32[]{:S(2)}) copy-start(bf16[2,256,256]{2,1,0:T(8,128)(2,1)} %constant.21.clone.inner_back) | copy-start | bytes 786436
  66.5 9.4 %copy-start.15 = (bf16[2,128,256]{2,1,0:T(8,128)(2,1)S(1)}, bf16[2,128,256]{2,1,0:T(8,128)(2,1)}, u32[]{:S(2)}) copy-start(bf16[2,128,256]{2,1,0:T(8,128)(2,1)} %constant.22.clone.outer_back) | copy-start | bytes 393220
  101.1 4.2 %copy-start.1 = (bf16[512,1024]{1,0:T(8,128)(2,1)S(1)}, bf16[512,1024]{1,0:T(8,128)(2,1)}, u32[]{:S(2)}) copy-start(bf16[512,1024]{1,0:T(8,128)(2,1)} %k_ref.3) | copy-start | bytes 3145732
  101.1 4.2 %copy-start.3 = (bf16[512,1024]{1,0:T(8,128)(2,1)S(1)}, bf16[512,1024]{1,0:T(8,128)(2,1)}, u32[]{:S(2)}) copy-start(bf16[512,1024]{1,0:T(8,128)(2,1)} %v_ref.3) | copy-start | bytes 3145732
  101.1 4.2 %copy-start.18 = (s32[2]{0:T(128)S(1)}, s32[2]{0:T(128)}, u32[]{:S(2)}) copy-start(s32[2]{0:T(128)} %copy-done.16) | copy-start | bytes 28
  101.1 32.0 %all-to-all-start.1 = ((bf16[32,136,128]{2,1,0:T(8,128)(2,1)}), bf16[32,136,128]{2,1,0:T(8,128)(2,1)S(1)}, u32[]{:S(2)}, u32[]{:S(2)}) async-start(bf16[32,136,128]{2,1,0:T(8,128)(2,1)} %long_conv.1), calls=%async_computation.1 | async-start | bytes 2228224 | tf_op jit(solution)/shard_map/all_to_all | solution.py:372
  105.3 1.2 copy-start.8
  112.2 1.3 copy-start.4
  133.0 1.6 %copy-start.5 = (f32[512,1024]{1,0:T(8,128)S(1)}, f32[512,1024]{1,0:T(8,128)}, u32[]{:S(2)}) copy-start(f32[512,1024]{1,0:T(8,128)} %copy-done.4) | copy-start | bytes 6291460
  134.6 1.6 %copy-start.6 = (f32[512,1024]{1,0:T(8,128)S(1)}, f32[512,1024]{1,0:T(8,128)}, u32[]{:S(2)}) copy-start(f32[512,1024]{1,0:T(8,128)} %get-tuple-element.24.skip_ref) | copy-start | bytes 6291460

commit v2 on v1

v2 whole, which is shorter than its diff:
```python
import functools

import jax
import jax.numpy as jnp
import ml_dtypes
import numpy as np
from jax import lax
from jax.experimental import pallas as pl
from jax.experimental.pallas import tpu as pltpu
from jax.sharding import PartitionSpec as P

LANES = 128
PAD = 8
SPAN = 240.0
BOTH = ("ctx", "tp")
bf16, f32 = jnp.bfloat16, jnp.float32


def split_table(table, axis):
    high = table.astype(ml_dtypes.bfloat16)
    low = (table - high.astype(np.float64)).astype(ml_dtypes.bfloat16)
    parts = [high, low, high] if axis == 1 else [high, high, low]
    return np.concatenate(parts, axis)


@functools.lru_cache(maxsize=None)
def transform_tables(rows):
    m = np.arange(rows)
    k1 = np.arange(rows) + 0.5
    b = np.arange(LANES)
    outer = 2.0 * np.pi * np.outer(k1, m) / (2 * rows)
    inner = 2.0 * np.pi * (np.outer(b, b) % LANES) / LANES
    twist = 2.0 * np.pi * np.outer(k1, b) / (2 * LANES * rows)
    c, s = np.cos(inner), np.sin(inner)
    outer_forward = np.concatenate([np.cos(outer), -np.sin(outer)], 0)
    inner_forward = np.block([[c, -s], [s, c]])
    return (
        split_table(outer_forward, 1),
        split_table(inner_forward, 0),
        split_table(inner_forward.T, 0),
        split_table(outer_forward.T, 1),
        np.stack([np.cos(twist), -np.sin(twist)]).astype(np.float32),
    )


def halves(value):
    high = value.astype(bf16)
    return high, (value - high.astype(f32)).astype(bf16)


def from_left(table, value):
    high, low = halves(value)
    return jnp.dot(table[...], jnp.concatenate([high, high, low], 0), preferred_element_type=f32)


def from_right(value, table):
    high, low = halves(value)
    return jnp.dot(jnp.concatenate([high, low, high], 1), table[...], preferred_element_type=f32)


def forward(signal, rows, outer, inner, twist):
    group = signal.shape[1] // LANES
    columns = from_left(outer, signal)
    cos, sin = twist[0], twist[1]
    stacked = []
    for p in range(group):
        re = columns[:rows, p * LANES : (p + 1) * LANES]
        im = columns[rows:, p * LANES : (p + 1) * LANES]
        stacked.append(jnp.concatenate([re * cos - im * sin, re * sin + im * cos], 1))
    return from_right(jnp.concatenate(stacked, 0), inner)


def backward(spectrum, rows, inner, outer, twist):
    group = spectrum.shape[0] // rows
    lines = from_right(spectrum, inner)
    cos, sin = twist[0], twist[1]
    columns = []
    for p in range(group):
        re = lines[p * rows : (p + 1) * rows, :LANES]
        im = lines[p * rows : (p + 1) * rows, LANES:]
        columns.append(jnp.concatenate([re * cos + im * sin, im * cos - re * sin], 0))
    return from_left(outer, jnp.concatenate(columns, 1))


def encode(value, inverse_scale):
    magnitude = jnp.exp2(jnp.abs(value) * inverse_scale * SPAN - SPAN / 2)
    return jnp.where(value < 0, -magnitude, magnitude)


def decode(code, scale):
    magnitude = (jnp.log2(jnp.abs(code)) + SPAN / 2) * (scale * (1.0 / SPAN))
    return jnp.where(code < 0, -magnitude, magnitude)


def block_scale(largest):
    return jnp.maximum(largest * 1.0078125, 1e-30).astype(bf16).astype(f32)


def short_conv(ext_ref, weights, length):
    return (
        weights[0:1] * ext_ref[8 : 8 + length]
        + weights[1:2] * ext_ref[7 : 7 + length]
        + weights[2:3] * ext_ref[6 : 6 + length]
    )


def fill(ext_ref, current, before):
    ext_ref[6:8] = before
    ext_ref[8 : 8 + current.shape[0]] = current.astype(f32)


def columns(j):
    return pl.ds(pl.multiple_of(j * LANES, LANES), LANES)


def lane_index(shape):
    return lax.broadcasted_iota(jnp.int32, shape, 1)


def edges_kernel(q_ref, k_ref, v_ref, short_ref, skip_ref, edge_ref, own_ref):
    last = q_ref.shape[0]
    shard = own_ref.shape[1]
    edge_ref[...] = jnp.zeros_like(edge_ref)
    own_ref[...] = jnp.zeros_like(own_ref)
    for i, ref in enumerate((q_ref, k_ref, v_ref)):
        edge_ref[2 * i : 2 * i + 2] = ref[...].astype(f32)[last - 2 : last]
        for ref_out in (edge_ref, own_ref):
            ref_out[6 + 3 * i : 9 + 3 * i, :shard] = short_ref[i]
    for ref_out in (edge_ref, own_ref):
        ref_out[15:16, :shard] = skip_ref[...]


def taps_and_edge(idx_ref, refs, tiles, j):
    edge_ref, *held = refs
    depth = len(held)
    behind = lax.rem(idx_ref[1] - j // tiles + depth, depth)
    here = columns(lax.rem(j, tiles))
    taps = held[0][:, here]
    for s in range(1, depth):
        taps = jnp.where(behind == s, held[s][:, here], taps)
    first = (idx_ref[0] == 0) & (idx_ref[1] == 0)
    return taps[6:15], taps[15:16], jnp.where(first, 0.0, edge_ref[0:6, columns(j)])


def column_copies(sources, targets, sems, j):
    return [
        pltpu.make_async_copy(s.at[:, columns(j)], t.at[:, columns(j)], sems.at[i, j])
        for i, (s, t) in enumerate(zip(sources, targets))
    ]


def start_all(copies_of, count):
    def step(j, carry):
        for copy in copies_of(j):
            copy.start()
        return carry

    lax.fori_loop(0, count, step, 0)


def wait_all(copies_of, count):
    def step(j, carry):
        for copy in copies_of(j):
            copy.wait()
        return carry

    lax.fori_loop(0, count, step, 0)


def rows_out_kernel(dims, idx_ref, k_hbm, v_hbm, *refs):
    length, per, parts, tiles, count = dims
    out_hbm, k_ref, v_ref, out_ref, k_ext, v_ext, sems, out_sems = refs[-8:]
    steps = length // LANES
    into = lambda j: column_copies((k_hbm, v_hbm), (k_ref, v_ref), sems, j)
    start_all(into, count)

    def out_of(j):
        where = (pl.ds(lax.rem(j, tiles) * parts, parts), pl.ds(j // tiles, 1))
        return [pltpu.make_async_copy(out_ref.at[where], out_hbm.at[where], out_sems.at[j])]

    def tile(j, carry):
        weights, _, before = taps_and_edge(idx_ref, refs[:-8], tiles, j)
        for copy in into(j):
            copy.wait()
        fill(k_ext, k_ref[:, columns(j)], before[2:4])
        fill(v_ext, v_ref[:, columns(j)], before[4:6])
        mixed = short_conv(k_ext, weights[3:6], length) * short_conv(v_ext, weights[6:9], length)
        codes, scales = [], []
        for step in range(steps):
            block = mixed[step * LANES : (step + 1) * LANES]
            scale = block_scale(jnp.max(jnp.abs(block), 0, keepdims=True))
            scales.append(jnp.broadcast_to(scale, (PAD, LANES)))
            codes.append(encode(block, 1.0 / scale).T)
        lane = lane_index((PAD, LANES))
        for g in range(parts):
            piece = [code[g * per : (g + 1) * per] for code in codes]
            line = jnp.ones((PAD, LANES), f32)
            for step in range(steps):
                moved = pltpu.roll(scales[step], ((step - g) * per) % LANES, 1)
                inside = (lane >= step * per) & (lane < (step + 1) * per)
                line = jnp.where(inside, moved, line)
            whole_piece = jnp.concatenate(piece + [line], 0).astype(bf16)
            out_ref[lax.rem(j, tiles) * parts + g, j // tiles] = whole_piece
        for copy in out_of(j):
            copy.start()
        return carry

    lax.fori_loop(0, count, tile, 0)
    wait_all(out_of, count)


def gate_parts_kernel(dims, idx_ref, q_ref, k_ref, v_ref, *refs):
    length, tiles = dims
    short_ref, skip_ref, q_ext, k_ext, v_ext = refs[-5:]
    weights, bias, before = taps_and_edge(idx_ref, refs[:-5], tiles, pl.program_id(0))
    fill(q_ext, q_ref[...], before[0:2])
    fill(k_ext, k_ref[...], before[2:4])
    fill(v_ext, v_ref[...], before[4:6])
    mixed = short_conv(k_ext, weights[3:6], length) * short_conv(v_ext, weights[6:9], length)
    short_ref[...] = short_conv(q_ext, weights[0:3], length)
    skip_ref[...] = bias * mixed


def gate_kernel(dims, y_ref, short_hbm, skip_hbm, out_hbm, short_ref, skip_ref, out_ref, sems):
    length, per, parts, tiles, count = dims
    steps = length // LANES
    rows = steps * per
    into = lambda j: column_copies((short_hbm, skip_hbm), (short_ref, skip_ref), sems, j)
    out_of = lambda j: column_copies((out_ref,), (out_hbm,), sems.at[pl.ds(2, 1)], j)
    start_all(into, count)

    def tile(j, carry):
        pieces = [
            y_ref[lax.rem(j, tiles) * parts + g, j // tiles].astype(f32) for g in range(parts)
        ]
        lane = lane_index((PAD, LANES))
        values = []
        for step in range(steps):
            code = jnp.concatenate([t[step * per : (step + 1) * per] for t in pieces], 0).T
            scale = jnp.ones((PAD, LANES), f32)
            for g in range(parts):
                moved = pltpu.roll(pieces[g][rows:], ((g - step) * per) % LANES, 1)
                inside = (lane >= g * per) & (lane < (g + 1) * per)
                scale = jnp.where(inside, moved, scale)
            values.append(decode(code, scale[0:1]))
        for copy in into(j):
            copy.wait()
        for step in range(steps):
            here = pl.ds(step * LANES, LANES)
            out_ref[here, columns(j)] = short_ref[here, columns(j)] * (
                values[step] + skip_ref[here, columns(j)]
            )
        for copy in out_of(j):
            copy.start()
        return carry

    lax.fori_loop(0, count, tile, 0)
    wait_all(out_of, count)


def filter_rows_kernel(dims, idx_ref, h_ref, *refs):
    per, peers, chunk = dims
    outs, turned, lines = refs[:peers], refs[-2], refs[-1]
    me = idx_ref[0]
    parts = LANES // per
    for r in range(chunk):
        for c in range(h_ref.shape[1] // LANES):
            block = h_ref[r * LANES : (r + 1) * LANES, c * LANES : (c + 1) * LANES]
            scale = block_scale(jnp.max(jnp.abs(block), 0, keepdims=True))
            code = encode(block, 1.0 / scale).T.astype(bf16)
            wide = jnp.broadcast_to(scale, (PAD, LANES))
            for g in range(parts):
                turned[c * parts + g, r] = code[g * per : (g + 1) * per]
                lines[c * parts + g, r : r + 1] = pltpu.roll(wide, (-g * per) % LANES, 1)[0:1]
    for s in range(peers):
        peer = lax.bitwise_xor(me, s)
        outs[s][0 : chunk * per] = turned[peer].reshape(chunk * per, LANES)
        outs[s][chunk * per :] = lines[peer].astype(bf16)


def filter_kernel(dims, idx_ref, *refs):
    rows, per, peers, group = dims
    pieces = refs[:peers]
    outer, inner, twist, out_hbm, out_ref, coded, scales, held, wide, sems, out_sems = refs[peers:]
    me = idx_ref[0]
    chunk = rows // peers
    size = chunk * per
    copies = []
    for s in range(peers):
        peer = lax.bitwise_xor(me, s)
        copies.append(
            pltpu.make_async_copy(
                pieces[s].at[pl.ds(0, size)],
                coded.at[pl.ds(pl.multiple_of(peer * size, 16), size)],
                sems.at[0, s],
            )
        )
        copies.append(
            pltpu.make_async_copy(
                pieces[s].at[pl.ds(size, chunk)],
                scales.at[pl.ds(pl.multiple_of(peer * chunk, 16), chunk)],
                sems.at[1, s],
            )
        )
    for copy in copies:
        copy.start()
    for copy in copies:
        copy.wait()
    wide[...] = scales[...].astype(f32)

    def out_of(i):
        where = pl.ds(i * group, group)
        return [pltpu.make_async_copy(out_ref.at[where], out_hbm.at[where], out_sems.at[i])]

    def widen(i, carry):
        here = pl.ds(pl.multiple_of(i * size, 16), size)
        held[here, :] = coded[here, :].astype(f32)
        return carry

    lax.fori_loop(0, peers, widen, 0)

    def body(i, carry):
        first = i * group
        near = pltpu.roll(wide[...], LANES - first, 1)
        signal = jnp.concatenate(
            [
                decode(held[pl.ds(first + p, rows, stride=per), :], near[:, p : p + 1])
                for p in range(group)
            ],
            1,
        )
        spectrum = forward(signal, rows, outer, inner, twist) * (1.0 / (LANES * rows))
        for p in range(group):
            out_ref[first + p] = spectrum[p * rows : (p + 1) * rows]
        for copy in out_of(i):
            copy.start()
        return carry

    lax.fori_loop(0, per // group, body, 0)
    wait_all(out_of, per // group)


def conv_kernel(
    dims, x_ref, h_hbm, outer, inner, inner_back, outer_back, twist, out_ref, held, h_ref, sem
):
    rows, per, lines, blocks, group, batch = dims
    fetch = pltpu.make_async_copy(h_hbm, h_ref, sem)
    fetch.start()

    def unpack(i, carry):
        for j in range(batch):
            tile = x_ref[i * batch + j].astype(f32)
            scale = jnp.broadcast_to(tile[lines : lines + 1], (LANES, LANES)).T[:lines]
            start = pl.multiple_of((i * batch + j) * lines, 8)
            held[pl.ds(start, lines), :] = decode(tile[:lines], scale)
        return carry

    lax.fori_loop(0, blocks // batch, unpack, 0)
    fetch.wait()

    def body(i, carry):
        first = i * group
        signal = jnp.concatenate(
            [held[pl.ds(first + p, rows, stride=per), :] for p in range(group)], 1
        )
        spectrum = forward(signal, rows, outer, inner, twist)
        joined = []
        for p in range(group):
            re = spectrum[p * rows : (p + 1) * rows, :LANES]
            im = spectrum[p * rows : (p + 1) * rows, LANES:]
            h_re, h_im = h_ref[first + p, :, :LANES], h_ref[first + p, :, LANES:]
            joined.append(jnp.concatenate([re * h_re - im * h_im, re * h_im + im * h_re], 1))
        result = backward(jnp.concatenate(joined, 0), rows, inner_back, outer_back, twist)
        for p in range(group):
            held[pl.ds(first + p, rows, stride=per), :] = result[:, p * LANES : (p + 1) * LANES]
        return carry

    lax.fori_loop(0, per // group, body, 0)

    def pack(i, carry):
        for j in range(batch):
            start = pl.multiple_of((i * batch + j) * lines, 8)
            tile = held[pl.ds(start, lines), :]
            scale = block_scale(jnp.max(jnp.abs(tile), 1, keepdims=True))
            code = encode(tile, 1.0 / scale)
            wide = jnp.broadcast_to(scale, (lines, LANES))
            if lines < LANES:
                wide = jnp.concatenate([wide, jnp.ones((LANES - lines, LANES), f32)], 0)
            out_ref[i * batch + j] = jnp.concatenate([code, wide.T[:PAD]], 0).astype(bf16)
        return carry

    lax.fori_loop(0, blocks // batch, pack, 0)


def whole(array):
    return pl.BlockSpec(array.shape, lambda *_: (0,) * len(array.shape))


def vmem_limit(mebibytes):
    return pltpu.CompilerParams(vmem_limit_bytes=mebibytes * 1024 * 1024)


def local(sizes, query, key, value, long_filter, short_filter, skip_bias):
    peers, depth = sizes
    devices = peers * depth
    length, width = query.shape
    shard = long_filter.shape[1]
    per = shard // peers
    rows = length * devices // LANES
    lines = length // LANES * per
    parts = LANES // per
    tiles = shard // LANES
    group = min(8, per)
    me = jnp.stack([lax.axis_index(axis) for axis in BOTH]).astype(jnp.int32)
    tables = transform_tables(rows)
    outer, inner, inner_back, outer_back, twist = (jnp.asarray(t) for t in tables)

    def crossed(array, axis, count):
        return [array[0]] + [
            lax.ppermute(array[s], axis, [(i, i ^ s) for i in range(count)])
            for s in range(1, count)
        ]

    query, key, value = (pltpu.with_memory_space_constraint(a, pltpu.HBM) for a in (query, key, value))
    last = pl.BlockSpec((16, width), lambda i: (length // 16 - 1, 0))
    edge, own = pl.pallas_call(
        edges_kernel,
        grid=(1,),
        in_specs=[last] * 3 + [whole(short_filter), pl.BlockSpec((1, shard), lambda i: (0, 0))],
        out_specs=[
            pl.BlockSpec((16, width), lambda i: (0, 0)),
            pl.BlockSpec((16, shard), lambda i: (0, 0)),
        ],
        out_shape=[
            jax.ShapeDtypeStruct((16, width), f32),
            jax.ShapeDtypeStruct((16, shard), f32),
        ],
        compiler_params=vmem_limit(8),
        name="edges",
    )(query, key, value, short_filter, skip_bias.reshape(1, shard))

    def shifted(array, by):
        return lax.ppermute(array, BOTH, [(i, (i + by) % devices) for i in range(devices)])

    edge = shifted(edge, 1)
    taps = [own, edge] + [shifted(own, s) for s in range(2, depth)]

    chunk = long_filter.shape[0] // LANES
    pieces = pl.pallas_call(
        functools.partial(filter_rows_kernel, (per, peers, chunk)),
        grid_spec=pltpu.PrefetchScalarGridSpec(
            num_scalar_prefetch=1,
            grid=(1,),
            in_specs=[whole(long_filter)],
            out_specs=[pl.BlockSpec((chunk * per + chunk, LANES), lambda *_: (0, 0))] * peers,
            scratch_shapes=[
                pltpu.VMEM((peers, chunk, per, LANES), bf16),
                pltpu.VMEM((peers, chunk, LANES), f32),
            ],
        ),
        out_shape=[jax.ShapeDtypeStruct((chunk * per + chunk, LANES), bf16)] * peers,
        compiler_params=vmem_limit(16),
        name="filter_rows",
    )(me, long_filter)
    edge, *taps = lax.optimization_barrier((edge, *taps, *pieces))
    taps, pieces = taps[:depth], taps[depth:]
    pieces = crossed(pieces, "ctx", peers)

    row_spec = pl.BlockSpec((length, LANES), lambda j, _: (0, j))
    wire_shape = jax.ShapeDtypeStruct((peers, depth, lines + PAD, LANES), bf16)
    ext = pltpu.VMEM((length + 8, LANES), f32)
    vmem, hbm = pl.BlockSpec(memory_space=pltpu.VMEM), pl.BlockSpec(memory_space=pltpu.HBM)
    count = width // LANES
    coded = pl.pallas_call(
        functools.partial(rows_out_kernel, (length, per, parts, tiles, count)),
        in_specs=[pl.BlockSpec(memory_space=pltpu.SMEM), hbm, hbm] + [vmem] * (depth + 1),
        out_specs=hbm,
        out_shape=wire_shape,
        scratch_shapes=[
            pltpu.VMEM((length, width), bf16),
            pltpu.VMEM((length, width), bf16),
            pltpu.VMEM(wire_shape.shape, bf16),
            ext,
            ext,
            pltpu.SemaphoreType.DMA((2, count)),
            pltpu.SemaphoreType.DMA((count,)),
        ],
        compiler_params=vmem_limit(16),
        name="mixed_rows",
    )(me, key, value, edge, *taps)
    coded = coded.reshape(devices, lines + PAD, LANES)
    arrived = lax.all_to_all(coded, BOTH, split_axis=0, concat_axis=0, tiled=True)

    spectrum = pl.pallas_call(
        functools.partial(filter_kernel, (rows, per, peers, group)),
        grid_spec=pltpu.PrefetchScalarGridSpec(
            num_scalar_prefetch=1,
            grid=(1,),
            in_specs=[pl.BlockSpec(memory_space=pltpu.HBM)] * peers
            + [whole(outer), whole(inner), whole(twist)],
            out_specs=hbm,
            scratch_shapes=[
                pltpu.VMEM((per, rows, 2 * LANES), f32),
                pltpu.VMEM((rows * per, LANES), bf16),
                pltpu.VMEM((rows, LANES), bf16),
                pltpu.VMEM((rows * per, LANES), f32),
                pltpu.VMEM((rows, LANES), f32),
                pltpu.SemaphoreType.DMA((2, peers)),
                pltpu.SemaphoreType.DMA((per // group,)),
            ],
        ),
        out_shape=pltpu.HBM((per, rows, 2 * LANES), f32),
        compiler_params=vmem_limit(28),
        name="filter_spectrum",
    )(me, *pieces, outer, inner, twist)

    query_short, skip = pl.pallas_call(
        functools.partial(gate_parts_kernel, (length, tiles)),
        grid_spec=pltpu.PrefetchScalarGridSpec(
            num_scalar_prefetch=1,
            grid=(width // LANES,),
            in_specs=[row_spec] * 3 + [whole(edge)] + [whole(tap) for tap in taps],
            out_specs=[row_spec, row_spec],
            scratch_shapes=[ext] * 3,
        ),
        out_shape=[pltpu.HBM((length, width), f32)] * 2,
        compiler_params=vmem_limit(12),
        name="gate_parts",
    )(me, query, key, value, edge, *taps)

    query_short, skip, spectrum = (
        pltpu.with_memory_space_constraint(a, pltpu.HBM) for a in (query_short, skip, spectrum)
    )

    convolved = pl.pallas_call(
        functools.partial(conv_kernel, (rows, per, lines, devices, group, 4)),
        in_specs=[vmem, hbm] + [vmem] * 5,
        out_specs=vmem,
        out_shape=jax.ShapeDtypeStruct((devices, lines + PAD, LANES), bf16),
        scratch_shapes=[
            pltpu.VMEM((rows * per, LANES), f32),
            pltpu.VMEM((per, rows, 2 * LANES), f32),
            pltpu.SemaphoreType.DMA,
        ],
        compiler_params=vmem_limit(28),
        name="long_conv",
    )(arrived, spectrum, outer, inner, inner_back, outer_back, twist)
    returned = lax.all_to_all(convolved, BOTH, split_axis=0, concat_axis=0, tiled=True)
    returned = returned.reshape(peers, depth, lines + PAD, LANES)

    return pl.pallas_call(
        functools.partial(gate_kernel, (length, per, parts, tiles, count)),
        in_specs=[vmem, hbm, hbm],
        out_specs=hbm,
        out_shape=jax.ShapeDtypeStruct((length, width), f32),
        scratch_shapes=[pltpu.VMEM((length, width), f32)] * 3
        + [pltpu.SemaphoreType.DMA((3, count))],
        compiler_params=vmem_limit(20),
        name="gate",
    )(returned, query_short, skip)


def solution(mesh):
    sizes = (mesh.shape["ctx"], mesh.shape["tp"])
    return jax.shard_map(
        functools.partial(local, sizes),
        mesh=mesh,
        in_specs=(
            P(BOTH, None),
            P(BOTH, None),
            P(BOTH, None),
            P("ctx", "tp"),
            P(None, None, "tp"),
            P("tp"),
        ),
        out_specs=P(BOTH, None),
        check_vma=False,
    )
```

time: 141 us -> 110 us (0.78)
  waiting for transfers between devices: 51.4 us -> 39.9 us
  local copies, waits for them, and re-layouts: 11.8 us -> 2.2 us
  Pallas kernels: 51.4 us -> 43.3 us
  other arithmetic: 1.48 us -> 0.07 us
    pallas_call x1, Pallas kernels: 25.2 us -> 14.9 us  [local(): pl.pallas_call(functools.partial(conv_kernel, (rows, per, lines, devices,...]
    ppermute x10 -> x7, waiting for transfers between devices: 27 us -> 18.1 us  [crossed(): lax.ppermute(array[s], axis, [(i, i ^ s) for i in range(count)])]
    unnamed x38 -> x18, local copies, waits for them, and re-layouts: 8.92 us -> 2.2 us
    ppermute x10 -> x7, starting transfers between devices: 13 us -> 8.86 us  [crossed(): lax.ppermute(array[s], axis, [(i, i ^ s) for i in range(count)])]
    ppermute x1 -> x3, starting transfers between devices: 2.24 us -> 6.15 us  [shifted(): lax.ppermute(array, BOTH, [(i, (i + by) % devices) for i in range(devices)])]
    pallas_call x4 -> x5, Pallas kernels: 16.9 us -> 19.9 us  [the longest x1 8.12 us: local(): pl.pallas_call(functools.partial(gate_parts_kernel, (length, tiles)), gri...]
    ppermute x1 -> x3, waiting for transfers between devices: 4.93 us -> 2.19 us  [shifted(): lax.ppermute(array, BOTH, [(i, (i + by) % devices) for i in range(devices)])]
    slice x3 -> x0, local copies, waits for them, and re-layouts: 2.17 us -> none  [local(): edge = jnp.concatenate([query[-2:], key[-2:], value[-2:]], 0)]
  transfers between devices with their start and end apart: 13 -> 12, of which waited for: 6 -> 6; matrix products, arithmetic and copies ran while one was open for 2% -> 0% of each run, Pallas kernels for 12% -> 17%
where the time goes in v2:
time: 110 us
  Pallas kernels  43.3 us (39%)
  waiting for transfers between devices  39.9 us (36%)
  starting transfers between devices  24.2 us (22%)
  local copies, waits for them, and re-layouts  2.2 us (2%)
    all_to_all x1, waiting for transfers between devices, local(): lax.all_to_all(convolved, BOTH, split_axis=0, concat_axis=0, tiled=True)  19.6 us
    ppermute x7, waiting for transfers between devices, crossed(): lax.ppermute(array[s], axis, [(i, i ^ s) for i in range(count)])  18.1 us
    pallas_call x1, Pallas kernels, local(): pl.pallas_call(functools.partial(conv_kernel, (rows, per, lines, devices,...  14.9 us
    ppermute x7, starting transfers between devices, crossed(): lax.ppermute(array[s], axis, [(i, i ^ s) for i in range(count)])  8.86 us
    pallas_call x1, Pallas kernels, local(): pl.pallas_call(functools.partial(filter_kernel, (rows, per, peers, group)...  8.45 us
    pallas_call x1, Pallas kernels, local(): pl.pallas_call(functools.partial(gate_parts_kernel, (length, tiles)), gri...  8.12 us
    ppermute x3, starting transfers between devices, shifted(): lax.ppermute(array, BOTH, [(i, (i + by) % devices) for i in range(devices)])  6.15 us
    pallas_call x1, Pallas kernels, local(): pl.pallas_call(functools.partial(rows_out_kernel, (length, per, parts, ti...  5.44 us
  transfers between devices with their start and end apart: 12, of which 6 were waited for; matrix products, arithmetic and copies ran while one was open for 0% of the time, Pallas kernels for 17%

profile of v2, /device:TPU:1, one launch (start us, length us, event | category | flops | bytes accessed | tf_op | source)
XLA Modules:
  0.0 109.8 jit_solution(10555201932217287097)
XLA Ops:
  0.0 0.0 copy-start
  0.0 0.0 copy-start.6
  0.0 0.9 copy-done.6
  0.9 0.0 copy-start.7
  0.9 0.7 copy-done.7
  1.5 0.8 edges.1
  2.3 4.2 %collective-permute-start.2 = (f32[16,256]{1,0:T(8,128)S(1)}, f32[16,256]{1,0:T(8,128)S(1)}, u32[]{:S(2)}, u32[]{:S(2)}) collective-permute-start(f32[16,256]{1,0:T(8,128)S(1)} %get-tuple-element.41.refs_1_), channel_id=1, source_target_pairs={{0,3},{1,4},{2,5},{3,6},{4,7},{5,8},{6,9},{7,10},{8,11},{9,12},{10... | collective-permute-start | bytes 49160 | tf_op jit(solution)/shard_map/ppermute | solution.py:443
  6.6 0.6 collective-permute-start.1
  7.2 1.3 %collective-permute-start = (f32[16,1024]{1,0:T(8,128)S(1)}, f32[16,1024]{1,0:T(8,128)S(1)}, u32[]{:S(2)}, u32[]{:S(2)}) collective-permute-start(f32[16,1024]{1,0:T(8,128)S(1)} %get-tuple-element.30), channel_id=1, source_target_pairs={{0,1},{1,2},{2,3},{3,4},{4,5},{5,6},{6,7},{7,8},{8,9},{9,10},{10,1... | collective-permute-start | bytes 196616 | tf_op jit(solution)/shard_map/ppermute | solution.py:443
  8.5 0.1 pad_add_fusion.idx_ref
  8.6 0.0 copy-done
  8.6 1.6 %filter_rows.1 = (bf16[528,128]{1,0:T(8,128)(2,1)S(1)}, bf16[528,128]{1,0:T(8,128)(2,1)S(1)}, bf16[528,128]{1,0:T(8,128)(2,1)S(1)}, bf16[528,128]{1,0:T(8,128)(2...) custom-call(s32[2]{0:T(128)S(1)} %pad_add_fusion.idx_ref, ...), custom_call_target="tpu_custom_call" | custom-call | tf_op jit(solution)/shard_map/filter_rows/pallas_call | solution.py:449
  10.1 0.0 copy-start.8
  10.1 0.6 copy-done.8
  10.8 0.0 collective-permute-done.2.refs_4_
  10.8 0.0 collective-permute-done.1.refs_3_
  10.8 2.2 %collective-permute-done.refs_0_.refs_2_ = f32[16,1024]{1,0:T(8,128)S(1)} collective-permute-done((f32[16,1024]{1,0:T(8,128)S(1)}, f32[16,1024]{1,0:T(8,128)S(1)}, u32[]{:S(2)}, u32[]{:S(2)}) %collective-permute-start) | collective-permute-done | bytes 65568 | tf_op jit(solution)/shard_map/ppermute | solution.py:443
  13.0 0.0 copy-start.1
  13.0 0.0 copy-start.2
  13.0 0.0 copy-start.3
  13.0 5.4 %mixed_rows.1 = bf16[8,4,136,128]{3,2,1,0:T(8,128)(2,1)} custom-call(s32[2]{0:T(128)S(1)} %pad_add_fusion.idx_ref, bf16[512,1024]{1,0:T(8,128)(2,1)} %k_ref.3, bf16[512,1024]{1,0:T(8,128)(2,1)} %v_ref.3, f32[16,1024]{1,0:T(8,128)S(1)} %collective-permute-done.refs_0_.refs_2_, f32[16,256]{1,0:T(8,128)S(1)} %get-tuple-element.41.refs_1_, ...), custom_call_target="tpu_custom_call" | custom-call | tf_op jit(solution)/shard_map/mixed_rows/pallas_call | solution.py:474
  18.4 4.6 %all-to-all-start = ((bf16[32,136,128]{2,1,0:T(8,128)(2,1)}), bf16[32,136,128]{2,1,0:T(8,128)(2,1)S(1)}, u32[]{:S(2)}, u32[]{:S(2)}) async-start(bf16[32,136,128]{2,1,0:T(8,128)(2,1)} %bitcast.3), calls=%async_computation | async-start | bytes 2228224 | tf_op jit(solution)/shard_map/all_to_all | solution.py:492
  23.1 0.0 copy-start.4
  23.1 0.0 copy-start.5
  23.1 0.5 collective-permute-start.3
  23.5 1.4 %collective-permute-start.4 = (bf16[528,128]{1,0:T(8,128)(2,1)S(1)}, bf16[528,128]{1,0:T(8,128)(2,1)S(1)}, u32[]{:S(2)}, u32[]{:S(2)}) collective-permute-start(bf16[528,128]{1,0:T(8,128)(2,1)S(1)} %get-tuple-element.47), channel_id=1, source_target_pairs={{0,8},{4,12},{8,0},{12,4},{16,24},{20,28},{24,16},{28,20},{1,9},{5... | collective-permute-start | bytes 405512 | tf_op jit(solution)/shard_map/ppermute | solution.py:420
  24.9 0.4 collective-permute-start.5
  25.3 1.4 %collective-permute-start.6 = (bf16[528,128]{1,0:T(8,128)(2,1)S(1)}, bf16[528,128]{1,0:T(8,128)(2,1)S(1)}, u32[]{:S(2)}, u32[]{:S(2)}) collective-permute-start(bf16[528,128]{1,0:T(8,128)(2,1)S(1)} %get-tuple-element.49), channel_id=1, source_target_pairs={{0,16},{4,20},{8,24},{12,28},{16,0},{20,4},{24,8},{28,12},{1,17},{... | collective-permute-start | bytes 405512 | tf_op jit(solution)/shard_map/ppermute | solution.py:420
  26.7 0.4 collective-permute-start.7
  27.1 0.0 collective-permute-done.3.refs_1_
  27.1 2.2 %collective-permute-start.8 = (bf16[528,128]{1,0:T(8,128)(2,1)S(1)}, bf16[528,128]{1,0:T(8,128)(2,1)S(1)}, u32[]{:S(2)}, u32[]{:S(2)}) collective-permute-start(bf16[528,128]{1,0:T(8,128)(2,1)S(1)} %get-tuple-element.51), channel_id=1, source_target_pairs={{0,24},{4,28},{8,16},{12,20},{16,8},{20,12},{24,0},{28,4},{1,25},{... | collective-permute-start | bytes 405512 | tf_op jit(solution)/shard_map/ppermute | solution.py:420
  29.3 6.5 %collective-permute-done.4.refs_2_ = bf16[528,128]{1,0:T(8,128)(2,1)S(1)} collective-permute-done((bf16[528,128]{1,0:T(8,128)(2,1)S(1)}, bf16[528,128]{1,0:T(8,128)(2,1)S(1)}, u32[]{:S(2)}, u32[]{:S(2)}) %collective-permute-start.4) | collective-permute-done | bytes 135200 | tf_op jit(solution)/shard_map/ppermute | solution.py:420
  35.9 2.6 %collective-permute-start.9 = (bf16[528,128]{1,0:T(8,128)(2,1)S(1)}, bf16[528,128]{1,0:T(8,128)(2,1)S(1)}, u32[]{:S(2)}, u32[]{:S(2)}) collective-permute-start(bf16[528,128]{1,0:T(8,128)(2,1)S(1)} %get-tuple-element.52), channel_id=1, source_target_pairs={{0,28},{4,24},{8,20},{12,16},{16,12},{20,8},{24,4},{28,0},{1,29},{... | collective-permute-start | bytes 405512 | tf_op jit(solution)/shard_map/ppermute | solution.py:420
  38.5 2.6 %collective-permute-done.5.refs_3_ = bf16[528,128]{1,0:T(8,128)(2,1)S(1)} collective-permute-done((bf16[528,128]{1,0:T(8,128)(2,1)S(1)}, bf16[528,128]{1,0:T(8,128)(2,1)S(1)}, u32[]{:S(2)}, u32[]{:S(2)}) %collective-permute-start.5) | collective-permute-done | bytes 135200 | tf_op jit(solution)/shard_map/ppermute | solution.py:420
  41.1 0.0 collective-permute-done.6.refs_4_
  41.1 0.0 collective-permute-done.7.refs_5_
  41.1 4.3 %collective-permute-done.8.refs_6_ = bf16[528,128]{1,0:T(8,128)(2,1)S(1)} collective-permute-done((bf16[528,128]{1,0:T(8,128)(2,1)S(1)}, bf16[528,128]{1,0:T(8,128)(2,1)S(1)}, u32[]{:S(2)}, u32[]{:S(2)}) %collective-permute-start.8) | collective-permute-done | bytes 135200 | tf_op jit(solution)/shard_map/ppermute | solution.py:420
  45.4 4.6 %collective-permute-done.9.refs_7_ = bf16[528,128]{1,0:T(8,128)(2,1)S(1)} collective-permute-done((bf16[528,128]{1,0:T(8,128)(2,1)S(1)}, bf16[528,128]{1,0:T(8,128)(2,1)S(1)}, u32[]{:S(2)}, u32[]{:S(2)}) %collective-permute-start.9) | collective-permute-done | bytes 135200 | tf_op jit(solution)/shard_map/ppermute | solution.py:420
  50.0 0.0 copy-done.1
  50.0 0.0 copy-done.2
  50.0 0.0 copy-done.3
  50.1 8.4 %filter_spectrum.1.h_hbm = f32[32,128,256]{2,1,0:T(8,128)} custom-call(s32[2]{0:T(128)S(1)} %pad_add_fusion.idx_ref, bf16[528,128]{1,0:T(8,128)(2,1)S(1)} %get-tuple-element.45.refs_0_, bf16[528,128]{1,0:T(8,128)(2,1)S(1)} %collective-permute-done.3.refs_1_, bf16[528,128]{1,0:T(8,128)(2,1)S(1)} %collective-permute-done.4.refs_2_, ...), custom_call_target="tpu_custom_call" | custom-call | tf_op jit(solution)/shard_map/filter_spectrum/pallas_call | solution.py:494
  58.5 0.0 all-to-all-done.x_ref
  58.5 0.0 copy-done.4
  58.5 0.0 copy-done.5
  58.5 14.9 %long_conv.1 = bf16[32,136,128]{2,1,0:T(8,128)(2,1)} custom-call(bf16[32,136,128]{2,1,0:T(8,128)(2,1)S(1)} %all-to-all-done.x_ref, f32[32,128,256]{2,1,0:T(8,128)} %filter_spectrum.1.h_hbm, bf16[256,384]{1,0:T(8,128)(2,1)S(1)} %copy-done.2, bf16[768,256]{1,0:T(8,128)(2,1)S(1)} %copy-done.1, bf16[768,256]{1,0:T(8,128)(2,1)S(1)} %copy-done.4, ...), custom_call_target="tpu_custom_call" | custom-call | tf_op jit(solution)/shard_map/long_conv/pallas_call | solution.py:535
  73.5 4.6 %all-to-all-start.1 = ((bf16[32,136,128]{2,1,0:T(8,128)(2,1)}), bf16[32,136,128]{2,1,0:T(8,128)(2,1)S(1)}, u32[]{:S(2)}, u32[]{:S(2)}) async-start(bf16[32,136,128]{2,1,0:T(8,128)(2,1)} %long_conv.1), calls=%async_computation.1 | async-start | bytes 2228224 | tf_op jit(solution)/shard_map/all_to_all | solution.py:548
  78.1 8.1 %gate_parts.1 = (f32[512,1024]{1,0:T(8,128)}, f32[512,1024]{1,0:T(8,128)}) custom-call(s32[2]{0:T(128)S(1)} %pad_add_fusion.idx_ref, bf16[512,1024]{1,0:T(8,128)(2,1)} %q_ref.3, bf16[512,1024]{1,0:T(8,128)(2,1)} %k_ref.3, bf16[512,1024]{1,0:T(8,128)(2,1)} %v_ref.3, f32[16,1024]{1,0:T(8,128)S(1)} %collective-permute-done.refs_0_.refs_2_, ...), custom_call_target="tpu_custom_call" | custom-call | tf_op jit(solution)/shard_map/gate_parts/pallas_call | solution.py:517
  86.2 19.6 %all-to-all-done.1 = bf16[32,136,128]{2,1,0:T(8,128)(2,1)S(1)} async-done(((bf16[32,136,128]{2,1,0:T(8,128)(2,1)}), bf16[32,136,128]{2,1,0:T(8,128)(2,1)S(1)}, u32[]{:S(2)}, u32[]{:S(2)}) %all-to-all-start.1) | async-done | bytes 1114144 | tf_op jit(solution)/shard_map/all_to_all | solution.py:548
  105.8 4.0 %gate.1 = f32[512,1024]{1,0:T(8,128)} custom-call(bf16[8,4,136,128]{3,2,1,0:T(8,128)(2,1)S(1)} %bitcast.5, f32[512,1024]{1,0:T(8,128)} %get-tuple-element.53.short_hbm, f32[512,1024]{1,0:T(8,128)} %get-tuple-element.54.skip_hbm), custom_call_target="tpu_custom_call" | custom-call | tf_op jit(solution)/shard_map/gate/pallas_call | solution.py:551
Async XLA Ops:
  0.0 8.6 %copy-start = (f32[2048,256]{1,0:T(8,128)S(1)}, f32[2048,256]{1,0:T(8,128)}, u32[]{:S(2)}) copy-start(f32[2048,256]{1,0:T(8,128)} %h_ref.1) | copy-start | bytes 6291460
  0.0 0.9 copy-start.6
  0.9 0.7 copy-start.7
  2.3 8.4 %collective-permute-start.2 = (f32[16,256]{1,0:T(8,128)S(1)}, f32[16,256]{1,0:T(8,128)S(1)}, u32[]{:S(2)}, u32[]{:S(2)}) collective-permute-start(f32[16,256]{1,0:T(8,128)S(1)} %get-tuple-element.41.refs_1_), channel_id=1, source_target_pairs={{0,3},{1,4},{2,5},{3,6},{4,7},{5,8},{6,9},{7,10},{8,11},{9,12},{10... | collective-permute-start | bytes 49160 | tf_op jit(solution)/shard_map/ppermute | solution.py:443
  6.6 4.2 %collective-permute-start.1 = (f32[16,256]{1,0:T(8,128)S(1)}, f32[16,256]{1,0:T(8,128)S(1)}, u32[]{:S(2)}, u32[]{:S(2)}) collective-permute-start(f32[16,256]{1,0:T(8,128)S(1)} %get-tuple-element.41.refs_1_), channel_id=1, source_target_pairs={{0,2},{1,3},{2,4},{3,5},{4,6},{5,7},{6,8},{7,9},{8,10},{9,11},{10,... | collective-permute-start | bytes 49160 | tf_op jit(solution)/shard_map/ppermute | solution.py:443
  7.2 5.8 %collective-permute-start = (f32[16,1024]{1,0:T(8,128)S(1)}, f32[16,1024]{1,0:T(8,128)S(1)}, u32[]{:S(2)}, u32[]{:S(2)}) collective-permute-start(f32[16,1024]{1,0:T(8,128)S(1)} %get-tuple-element.30), channel_id=1, source_target_pairs={{0,1},{1,2},{2,3},{3,4},{4,5},{5,6},{6,7},{7,8},{8,9},{9,10},{10,1... | collective-permute-start | bytes 196616 | tf_op jit(solution)/shard_map/ppermute | solution.py:443
  10.1 0.6 copy-start.8
  13.0 37.1 %copy-start.1 = (bf16[768,256]{1,0:T(8,128)(2,1)S(1)}, bf16[768,256]{1,0:T(8,128)(2,1)}, u32[]{:S(2)}) copy-start(bf16[768,256]{1,0:T(8,128)(2,1)} %constant.20.clone.refs_9_.inner) | copy-start | bytes 1179652
  13.0 37.1 %copy-start.2 = (bf16[256,384]{1,0:T(8,128)(2,1)S(1)}, bf16[256,384]{1,0:T(8,128)(2,1)}, u32[]{:S(2)}) copy-start(bf16[256,384]{1,0:T(8,128)(2,1)} %constant.19.clone.refs_8_.outer) | copy-start | bytes 589828
  13.0 37.1 %copy-start.3 = (f32[2,128,128]{2,1,0:T(8,128)S(1)}, f32[2,128,128]{2,1,0:T(8,128)}, u32[]{:S(2)}) copy-start(f32[2,128,128]{2,1,0:T(8,128)} %constant.23.clone.refs_10_.twist) | copy-start | bytes 393220
  18.4 40.1 %all-to-all-start = ((bf16[32,136,128]{2,1,0:T(8,128)(2,1)}), bf16[32,136,128]{2,1,0:T(8,128)(2,1)S(1)}, u32[]{:S(2)}, u32[]{:S(2)}) async-start(bf16[32,136,128]{2,1,0:T(8,128)(2,1)} %bitcast.3), calls=%async_computation | async-start | bytes 2228224 | tf_op jit(solution)/shard_map/all_to_all | solution.py:492
  23.1 35.5 %copy-start.4 = (bf16[768,256]{1,0:T(8,128)(2,1)S(1)}, bf16[768,256]{1,0:T(8,128)(2,1)}, u32[]{:S(2)}) copy-start(bf16[768,256]{1,0:T(8,128)(2,1)} %constant.21.clone.inner_back) | copy-start | bytes 1179652
  23.1 35.5 %copy-start.5 = (bf16[128,768]{1,0:T(8,128)(2,1)S(1)}, bf16[128,768]{1,0:T(8,128)(2,1)}, u32[]{:S(2)}) copy-start(bf16[128,768]{1,0:T(8,128)(2,1)} %constant.22.clone.outer_back) | copy-start | bytes 589828
  23.1 4.0 %collective-permute-start.3 = (bf16[528,128]{1,0:T(8,128)(2,1)}, bf16[528,128]{1,0:T(8,128)(2,1)S(1)}, u32[]{:S(2)}, u32[]{:S(2)}) collective-permute-start(bf16[528,128]{1,0:T(8,128)(2,1)} %copy-done.8), channel_id=1, source_target_pairs={{0,4},{4,0},{8,12},{12,8},{16,20},{20,16},{24,28},{28,24},{1,5},{5... | collective-permute-start | bytes 405512 | tf_op jit(solution)/shard_map/ppermute | solution.py:420
  23.5 12.3 %collective-permute-start.4 = (bf16[528,128]{1,0:T(8,128)(2,1)S(1)}, bf16[528,128]{1,0:T(8,128)(2,1)S(1)}, u32[]{:S(2)}, u32[]{:S(2)}) collective-permute-start(bf16[528,128]{1,0:T(8,128)(2,1)S(1)} %get-tuple-element.47), channel_id=1, source_target_pairs={{0,8},{4,12},{8,0},{12,4},{16,24},{20,28},{24,16},{28,20},{1,9},{5... | collective-permute-start | bytes 405512 | tf_op jit(solution)/shard_map/ppermute | solution.py:420
  24.9 16.2 %collective-permute-start.5 = (bf16[528,128]{1,0:T(8,128)(2,1)S(1)}, bf16[528,128]{1,0:T(8,128)(2,1)S(1)}, u32[]{:S(2)}, u32[]{:S(2)}) collective-permute-start(bf16[528,128]{1,0:T(8,128)(2,1)S(1)} %get-tuple-element.48), channel_id=1, source_target_pairs={{0,12},{4,8},{8,4},{12,0},{16,28},{20,24},{24,20},{28,16},{1,13},{... | collective-permute-start | bytes 405512 | tf_op jit(solution)/shard_map/ppermute | solution.py:420
  25.3 15.8 %collective-permute-start.6 = (bf16[528,128]{1,0:T(8,128)(2,1)S(1)}, bf16[528,128]{1,0:T(8,128)(2,1)S(1)}, u32[]{:S(2)}, u32[]{:S(2)}) collective-permute-start(bf16[528,128]{1,0:T(8,128)(2,1)S(1)} %get-tuple-element.49), channel_id=1, source_target_pairs={{0,16},{4,20},{8,24},{12,28},{16,0},{20,4},{24,8},{28,12},{1,17},{... | collective-permute-start | bytes 405512 | tf_op jit(solution)/shard_map/ppermute | solution.py:420
  26.7 14.4 %collective-permute-start.7 = (bf16[528,128]{1,0:T(8,128)(2,1)S(1)}, bf16[528,128]{1,0:T(8,128)(2,1)S(1)}, u32[]{:S(2)}, u32[]{:S(2)}) collective-permute-start(bf16[528,128]{1,0:T(8,128)(2,1)S(1)} %get-tuple-element.50), channel_id=1, source_target_pairs={{0,20},{4,16},{8,28},{12,24},{16,4},{20,0},{24,12},{28,8},{1,21},{... | collective-permute-start | bytes 405512 | tf_op jit(solution)/shard_map/ppermute | solution.py:420
  27.1 18.3 %collective-permute-start.8 = (bf16[528,128]{1,0:T(8,128)(2,1)S(1)}, bf16[528,128]{1,0:T(8,128)(2,1)S(1)}, u32[]{:S(2)}, u32[]{:S(2)}) collective-permute-start(bf16[528,128]{1,0:T(8,128)(2,1)S(1)} %get-tuple-element.51), channel_id=1, source_target_pairs={{0,24},{4,28},{8,16},{12,20},{16,8},{20,12},{24,0},{28,4},{1,25},{... | collective-permute-start | bytes 405512 | tf_op jit(solution)/shard_map/ppermute | solution.py:420
  35.9 14.2 %collective-permute-start.9 = (bf16[528,128]{1,0:T(8,128)(2,1)S(1)}, bf16[528,128]{1,0:T(8,128)(2,1)S(1)}, u32[]{:S(2)}, u32[]{:S(2)}) collective-permute-start(bf16[528,128]{1,0:T(8,128)(2,1)S(1)} %get-tuple-element.52), channel_id=1, source_target_pairs={{0,28},{4,24},{8,20},{12,16},{16,12},{20,8},{24,4},{28,0},{1,29},{... | collective-permute-start | bytes 405512 | tf_op jit(solution)/shard_map/ppermute | solution.py:420
  73.5 32.4 %all-to-all-start.1 = ((bf16[32,136,128]{2,1,0:T(8,128)(2,1)}), bf16[32,136,128]{2,1,0:T(8,128)(2,1)S(1)}, u32[]{:S(2)}, u32[]{:S(2)}) async-start(bf16[32,136,128]{2,1,0:T(8,128)(2,1)} %long_conv.1), calls=%async_computation.1 | async-start | bytes 2228224 | tf_op jit(solution)/shard_map/all_to_all | solution.py:548

commit v3 on v2

--- a/solution.py
+++ b/solution.py
@@ -117,29 +117,35 @@
     return lax.broadcasted_iota(jnp.int32, shape, 1)
 
 
-def edges_kernel(q_ref, k_ref, v_ref, short_ref, skip_ref, edge_ref, own_ref):
+def edges_kernel(q_ref, k_ref, v_ref, short_ref, skip_ref, edge_ref, own_ref, rows_ref):
     last = q_ref.shape[0]
     shard = own_ref.shape[1]
-    edge_ref[...] = jnp.zeros_like(edge_ref)
-    own_ref[...] = jnp.zeros_like(own_ref)
+    rows_ref[...] = jnp.zeros_like(rows_ref)
+    own_ref[0:6] = jnp.zeros((6, shard), f32)
     for i, ref in enumerate((q_ref, k_ref, v_ref)):
-        edge_ref[2 * i : 2 * i + 2] = ref[...].astype(f32)[last - 2 : last]
-        for ref_out in (edge_ref, own_ref):
-            ref_out[6 + 3 * i : 9 + 3 * i, :shard] = short_ref[i]
-    for ref_out in (edge_ref, own_ref):
-        ref_out[15:16, :shard] = skip_ref[...]
+        rows_ref[2 * i : 2 * i + 2] = ref[...].astype(f32)[last - 2 : last]
+        own_ref[6 + 3 * i : 9 + 3 * i] = short_ref[i]
+    own_ref[15:16] = skip_ref[...]
+    rest = own_ref[6:16]
+    for i in range(3):
+        part = rest.astype(bf16).astype(f32)
+        rows_ref[6:16, i * shard : (i + 1) * shard] = part
+        rest = rest - part
+    edge_ref[...] = rows_ref[...].astype(bf16)
 
 
 def taps_and_edge(idx_ref, refs, tiles, j):
     edge_ref, *held = refs
-    depth = len(held)
+    depth = len(held) + 1
     behind = lax.rem(idx_ref[1] - j // tiles + depth, depth)
-    here = columns(lax.rem(j, tiles))
-    taps = held[0][:, here]
-    for s in range(1, depth):
-        taps = jnp.where(behind == s, held[s][:, here], taps)
+    tile = lax.rem(j, tiles)
+    parts = [edge_ref[:, columns(tile + i * tiles)].astype(f32) for i in range(3)]
+    taps = jnp.where(behind == 1, parts[0] + parts[1] + parts[2], held[0][:, columns(tile)])
+    for s in range(2, depth):
+        taps = jnp.where(behind == s, held[s - 1][:, columns(tile)], taps)
     first = (idx_ref[0] == 0) & (idx_ref[1] == 0)
-    return taps[6:15], taps[15:16], jnp.where(first, 0.0, edge_ref[0:6, columns(j)])
+    before = edge_ref[:, columns(j)].astype(f32)[0:6]
+    return taps[6:15], taps[15:16], jnp.where(first, 0.0, before)
 
 
 def column_copies(sources, targets, sems, j):
@@ -190,7 +196,7 @@
             block = mixed[step * LANES : (step + 1) * LANES]
             scale = block_scale(jnp.max(jnp.abs(block), 0, keepdims=True))
             scales.append(jnp.broadcast_to(scale, (PAD, LANES)))
-            codes.append(encode(block, 1.0 / scale).T)
+            codes.append(encode(block, 1.0 / scale).astype(bf16).T.astype(f32))
         lane = lane_index((PAD, LANES))
         for g in range(parts):
             piece = [code[g * per : (g + 1) * per] for code in codes]
@@ -423,6 +429,10 @@
 
     query, key, value = (pltpu.with_memory_space_constraint(a, pltpu.HBM) for a in (query, key, value))
     last = pl.BlockSpec((16, width), lambda i: (length // 16 - 1, 0))
+    taps_hbm, bias_hbm = (
+        pltpu.with_memory_space_constraint(a, pltpu.HBM)
+        for a in (short_filter, skip_bias.reshape(1, shard))
+    )
     edge, own = pl.pallas_call(
         edges_kernel,
         grid=(1,),
@@ -432,18 +442,19 @@
             pl.BlockSpec((16, shard), lambda i: (0, 0)),
         ],
         out_shape=[
-            jax.ShapeDtypeStruct((16, width), f32),
+            jax.ShapeDtypeStruct((16, width), bf16),
             jax.ShapeDtypeStruct((16, shard), f32),
         ],
+        scratch_shapes=[pltpu.VMEM((16, width), f32)],
         compiler_params=vmem_limit(8),
         name="edges",
-    )(query, key, value, short_filter, skip_bias.reshape(1, shard))
+    )(query, key, value, taps_hbm, bias_hbm)
 
     def shifted(array, by):
         return lax.ppermute(array, BOTH, [(i, (i + by) % devices) for i in range(devices)])
 
     edge = shifted(edge, 1)
-    taps = [own, edge] + [shifted(own, s) for s in range(2, depth)]
+    taps = [own] + [shifted(own, s) for s in range(2, depth)]
 
     chunk = long_filter.shape[0] // LANES
     pieces = pl.pallas_call(
@@ -458,12 +469,16 @@
                 pltpu.VMEM((peers, chunk, LANES), f32),
             ],
         ),
-        out_shape=[jax.ShapeDtypeStruct((chunk * per + chunk, LANES), bf16)] * peers,
+        out_shape=[pltpu.HBM((chunk * per + chunk, LANES), bf16)] * peers,
         compiler_params=vmem_limit(16),
         name="filter_rows",
     )(me, long_filter)
-    edge, *taps = lax.optimization_barrier((edge, *taps, *pieces))
-    taps, pieces = taps[:depth], taps[depth:]
+    pieces = list(pieces)
+    early = [s for s in (2, 4) if s < peers]
+    edge, *ready = lax.optimization_barrier((edge, *taps[1:], *(pieces[s] for s in early)))
+    taps[1:] = ready[: depth - 2]
+    for s, piece in zip(early, ready[depth - 2 :]):
+        pieces[s] = piece
     pieces = crossed(pieces, "ctx", peers)
 
     row_spec = pl.BlockSpec((length, LANES), lambda j, _: (0, j))
@@ -473,7 +488,7 @@
     count = width // LANES
     coded = pl.pallas_call(
         functools.partial(rows_out_kernel, (length, per, parts, tiles, count)),
-        in_specs=[pl.BlockSpec(memory_space=pltpu.SMEM), hbm, hbm] + [vmem] * (depth + 1),
+        in_specs=[pl.BlockSpec(memory_space=pltpu.SMEM), hbm, hbm] + [vmem] * depth,
         out_specs=hbm,
         out_shape=wire_shape,
         scratch_shapes=[
@@ -488,6 +503,9 @@
         compiler_params=vmem_limit(16),
         name="mixed_rows",
     )(me, key, value, edge, *taps)
+    coded, *ready = lax.optimization_barrier((coded, *(pieces[s] for s in early)))
+    for s, piece in zip(early, ready):
+        pieces[s] = piece
     coded = coded.reshape(devices, lines + PAD, LANES)
     arrived = lax.all_to_all(coded, BOTH, split_axis=0, concat_axis=0, tiled=True)
 

time: 110 us -> 106 us (0.964)
  local copies, waits for them, and re-layouts: 2.2 us -> 0.06 us
  waiting for transfers between devices: 39.9 us -> 38.1 us
  starting transfers between devices: 24.2 us -> 23 us
    unnamed x18 -> x24, local copies, waits for them, and re-layouts: 2.2 us -> 0.06 us
  transfers between devices with their start and end apart: 12 -> 12, of which waited for: 6 -> 6; matrix products, arithmetic and copies ran while one was open for 0% -> 0% of each run, Pallas kernels for 17% -> 23%
where the time goes in v3:
time: 106 us
  Pallas kernels  44.3 us (42%)
  waiting for transfers between devices  38.1 us (36%)
  starting transfers between devices  23 us (22%)
    all_to_all x1, waiting for transfers between devices, local(): lax.all_to_all(convolved, BOTH, split_axis=0, concat_axis=0, tiled=True)  19.6 us
    ppermute x7, waiting for transfers between devices, crossed(): lax.ppermute(array[s], axis, [(i, i ^ s) for i in range(count)])  17 us
    pallas_call x1, Pallas kernels, local(): pl.pallas_call(functools.partial(conv_kernel, (rows, per, lines, devices,...  14.9 us
    pallas_call x1, Pallas kernels, local(): pl.pallas_call(functools.partial(filter_kernel, (rows, per, peers, group)...  8.43 us
    pallas_call x1, Pallas kernels, local(): pl.pallas_call(functools.partial(gate_parts_kernel, (length, tiles)), gri...  8.17 us
    ppermute x7, starting transfers between devices, crossed(): lax.ppermute(array[s], axis, [(i, i ^ s) for i in range(count)])  7.97 us
    ppermute x3, starting transfers between devices, shifted(): lax.ppermute(array, BOTH, [(i, (i + by) % devices) for i in range(devices)])  6.15 us
    pallas_call x1, Pallas kernels, local(): pl.pallas_call(functools.partial(rows_out_kernel, (length, per, parts, ti...  5.24 us
  transfers between devices with their start and end apart: 12, of which 6 were waited for; matrix products, arithmetic and copies ran while one was open for 0% of the time, Pallas kernels for 23%

profile of v3, /device:TPU:1, one launch (start us, length us, event | category | flops | bytes accessed | tf_op | source)
XLA Modules:
  0.0 105.7 jit_solution(3811146588938458922)
XLA Ops:
  0.0 0.0 copy-start
  0.0 1.0 edges.1
  1.0 4.2 %collective-permute-start.2 = (f32[16,256]{1,0:T(8,128)S(1)}, f32[16,256]{1,0:T(8,128)S(1)}, u32[]{:S(2)}, u32[]{:S(2)}) collective-permute-start(f32[16,256]{1,0:T(8,128)S(1)} %get-tuple-element.26.refs_1_), channel_id=1, source_target_pairs={{0,3},{1,4},{2,5},{3,6},{4,7},{5,8},{6,9},{7,10},{8,11},{9,12},{10... | collective-permute-start | bytes 49160 | tf_op jit(solution)/shard_map/ppermute | solution.py:454
  5.2 0.6 collective-permute-start.1
  5.8 1.3 %collective-permute-start = (bf16[16,1024]{1,0:T(8,128)(2,1)S(1)}, bf16[16,1024]{1,0:T(8,128)(2,1)S(1)}, u32[]{:S(2)}, u32[]{:S(2)}) collective-permute-start(bf16[16,1024]{1,0:T(8,128)(2,1)S(1)} %get-tuple-element.25), channel_id=1, source_target_pairs={{0,1},{1,2},{2,3},{3,4},{4,5},{5,6},{6,7},{7,8},{8,9},{9,10},{10,1... | collective-permute-start | bytes 98312 | tf_op jit(solution)/shard_map/ppermute | solution.py:454
  7.1 0.1 pad_add_fusion.idx_ref
  7.2 0.0 copy-done
  7.2 2.6 %filter_rows.1 = (bf16[528,128]{1,0:T(8,128)(2,1)}, bf16[528,128]{1,0:T(8,128)(2,1)}, bf16[528,128]{1,0:T(8,128)(2,1)}, bf16[528,128]{1,0:T(8,128)(2,1)}, bf16[5...) custom-call(s32[2]{0:T(128)S(1)} %pad_add_fusion.idx_ref, ...), custom_call_target="tpu_custom_call" | custom-call | tf_op jit(solution)/shard_map/filter_rows/pallas_call | solution.py:460
  9.8 0.0 collective-permute-done.2.refs_3_
  9.8 0.0 collective-permute-done.1.refs_2_
  9.8 1.5 %collective-permute-done.refs_0_ = bf16[16,1024]{1,0:T(8,128)(2,1)S(1)} collective-permute-done((bf16[16,1024]{1,0:T(8,128)(2,1)S(1)}, bf16[16,1024]{1,0:T(8,128)(2,1)S(1)}, u32[]{:S(2)}, u32[]{:S(2)}) %collective-permute-start) | collective-permute-done | bytes 32800 | tf_op jit(solution)/shard_map/ppermute | solution.py:454
  11.3 0.0 copy-start.11
  11.3 0.0 copy-start.10
  11.3 0.0 copy-start.9
  11.3 0.0 copy-start.8
  11.3 0.0 copy-start.7
  11.3 0.0 copy-start.1
  11.3 0.0 copy-start.2
  11.3 0.0 copy-start.3
  11.3 0.0 copy-start.6
  11.4 1.0 collective-permute-start.3
  12.3 1.0 collective-permute-start.4
  13.3 5.2 %mixed_rows.1 = bf16[8,4,136,128]{3,2,1,0:T(8,128)(2,1)} custom-call(s32[2]{0:T(128)S(1)} %pad_add_fusion.idx_ref, bf16[512,1024]{1,0:T(8,128)(2,1)} %k_ref.3, bf16[512,1024]{1,0:T(8,128)(2,1)} %v_ref.3, bf16[16,1024]{1,0:T(8,128)(2,1)S(1)} %collective-permute-done.refs_0_, f32[16,256]{1,0:T(8,128)S(1)} %get-tuple-element.26.refs_1_, ...), custom_call_target="tpu_custom_call" | custom-call | tf_op jit(solution)/shard_map/mixed_rows/pallas_call | solution.py:489
  18.6 0.0 collective-permute-done.3.refs_2_
  18.6 0.0 collective-permute-done.4.refs_4_
  18.6 4.3 %all-to-all-start = ((bf16[32,136,128]{2,1,0:T(8,128)(2,1)}), bf16[32,136,128]{2,1,0:T(8,128)(2,1)S(1)}, u32[]{:S(2)}, u32[]{:S(2)}) async-start(bf16[32,136,128]{2,1,0:T(8,128)(2,1)} %bitcast.3), calls=%async_computation | async-start | bytes 2228224 | tf_op jit(solution)/shard_map/all_to_all | solution.py:510
  22.9 0.0 copy-done.11
  22.9 0.5 collective-permute-start.5
  23.4 0.0 copy-done.10
  23.4 1.4 %collective-permute-start.6 = (bf16[528,128]{1,0:T(8,128)(2,1)S(1)}, bf16[528,128]{1,0:T(8,128)(2,1)S(1)}, u32[]{:S(2)}, u32[]{:S(2)}) collective-permute-start(bf16[528,128]{1,0:T(8,128)(2,1)S(1)} %copy-done.10), channel_id=1, source_target_pairs={{0,12},{4,8},{8,4},{12,0},{16,28},{20,24},{24,20},{28,16},{1,13},{... | collective-permute-start | bytes 405512 | tf_op jit(solution)/shard_map/ppermute | solution.py:426
  24.8 0.0 copy-done.9
  24.8 1.4 %collective-permute-start.7 = (bf16[528,128]{1,0:T(8,128)(2,1)S(1)}, bf16[528,128]{1,0:T(8,128)(2,1)S(1)}, u32[]{:S(2)}, u32[]{:S(2)}) collective-permute-start(bf16[528,128]{1,0:T(8,128)(2,1)S(1)} %copy-done.9), channel_id=1, source_target_pairs={{0,20},{4,16},{8,28},{12,24},{16,4},{20,0},{24,12},{28,8},{1,21},{... | collective-permute-start | bytes 405512 | tf_op jit(solution)/shard_map/ppermute | solution.py:426
  26.2 0.0 copy-done.8
  26.2 0.1 collective-permute-start.8
  26.4 0.0 copy-done.7
  26.4 2.6 %collective-permute-start.9 = (bf16[528,128]{1,0:T(8,128)(2,1)S(1)}, bf16[528,128]{1,0:T(8,128)(2,1)S(1)}, u32[]{:S(2)}, u32[]{:S(2)}) collective-permute-start(bf16[528,128]{1,0:T(8,128)(2,1)S(1)} %copy-done.7), channel_id=1, source_target_pairs={{0,28},{4,24},{8,20},{12,16},{16,12},{20,8},{24,4},{28,0},{1,29},{... | collective-permute-start | bytes 405512 | tf_op jit(solution)/shard_map/ppermute | solution.py:426
  28.9 0.0 collective-permute-done.5.refs_1_
  28.9 7.9 %collective-permute-done.6.refs_3_ = bf16[528,128]{1,0:T(8,128)(2,1)S(1)} collective-permute-done((bf16[528,128]{1,0:T(8,128)(2,1)S(1)}, bf16[528,128]{1,0:T(8,128)(2,1)S(1)}, u32[]{:S(2)}, u32[]{:S(2)}) %collective-permute-start.6) | collective-permute-done | bytes 135200 | tf_op jit(solution)/shard_map/ppermute | solution.py:426
  36.8 1.6 %collective-permute-done.7.refs_5_ = bf16[528,128]{1,0:T(8,128)(2,1)S(1)} collective-permute-done((bf16[528,128]{1,0:T(8,128)(2,1)S(1)}, bf16[528,128]{1,0:T(8,128)(2,1)S(1)}, u32[]{:S(2)}, u32[]{:S(2)}) %collective-permute-start.7) | collective-permute-done | bytes 135200 | tf_op jit(solution)/shard_map/ppermute | solution.py:426
  38.4 2.1 %collective-permute-done.8.refs_6_ = bf16[528,128]{1,0:T(8,128)(2,1)S(1)} collective-permute-done((bf16[528,128]{1,0:T(8,128)(2,1)S(1)}, bf16[528,128]{1,0:T(8,128)(2,1)S(1)}, u32[]{:S(2)}, u32[]{:S(2)}) %collective-permute-start.8) | collective-permute-done | bytes 135200 | tf_op jit(solution)/shard_map/ppermute | solution.py:426
  40.6 5.4 %collective-permute-done.9.refs_7_ = bf16[528,128]{1,0:T(8,128)(2,1)S(1)} collective-permute-done((bf16[528,128]{1,0:T(8,128)(2,1)S(1)}, bf16[528,128]{1,0:T(8,128)(2,1)S(1)}, u32[]{:S(2)}, u32[]{:S(2)}) %collective-permute-start.9) | collective-permute-done | bytes 135200 | tf_op jit(solution)/shard_map/ppermute | solution.py:426
  46.0 0.0 copy-done.1
  46.0 0.0 copy-done.2
  46.0 0.0 copy-done.3
  46.0 0.0 copy-done.6
  46.0 0.0 copy-start.4
  46.0 0.0 copy-start.5
  46.0 8.4 %filter_spectrum.1.h_hbm = f32[32,128,256]{2,1,0:T(8,128)} custom-call(s32[2]{0:T(128)S(1)} %pad_add_fusion.idx_ref, bf16[528,128]{1,0:T(8,128)(2,1)S(1)} %copy-done.6, bf16[528,128]{1,0:T(8,128)(2,1)S(1)} %collective-permute-done.5.refs_1_, bf16[528,128]{1,0:T(8,128)(2,1)S(1)} %collective-permute-done.3.refs_2_, ...), custom_call_target="tpu_custom_call" | custom-call | tf_op jit(solution)/shard_map/filter_spectrum/pallas_call | solution.py:512
  54.4 0.0 all-to-all-done.x_ref
  54.5 0.0 copy-done.4
  54.5 0.0 copy-done.5
  54.5 14.9 %long_conv.1 = bf16[32,136,128]{2,1,0:T(8,128)(2,1)} custom-call(bf16[32,136,128]{2,1,0:T(8,128)(2,1)S(1)} %all-to-all-done.x_ref, f32[32,128,256]{2,1,0:T(8,128)} %filter_spectrum.1.h_hbm, bf16[256,384]{1,0:T(8,128)(2,1)S(1)} %copy-done.2, bf16[768,256]{1,0:T(8,128)(2,1)S(1)} %copy-done.1, bf16[768,256]{1,0:T(8,128)(2,1)S(1)} %copy-done.4, ...), custom_call_target="tpu_custom_call" | custom-call | tf_op jit(solution)/shard_map/long_conv/pallas_call | solution.py:553
  69.4 4.6 %all-to-all-start.1 = ((bf16[32,136,128]{2,1,0:T(8,128)(2,1)}), bf16[32,136,128]{2,1,0:T(8,128)(2,1)S(1)}, u32[]{:S(2)}, u32[]{:S(2)}) async-start(bf16[32,136,128]{2,1,0:T(8,128)(2,1)} %long_conv.1), calls=%async_computation.1 | async-start | bytes 2228224 | tf_op jit(solution)/shard_map/all_to_all | solution.py:566
  74.1 8.2 %gate_parts.1 = (f32[512,1024]{1,0:T(8,128)}, f32[512,1024]{1,0:T(8,128)}) custom-call(s32[2]{0:T(128)S(1)} %pad_add_fusion.idx_ref, bf16[512,1024]{1,0:T(8,128)(2,1)} %q_ref.3, bf16[512,1024]{1,0:T(8,128)(2,1)} %k_ref.3, bf16[512,1024]{1,0:T(8,128)(2,1)} %v_ref.3, bf16[16,1024]{1,0:T(8,128)(2,1)S(1)} %collective-permute-done.refs_0_, ...), custom_call_target="tpu_custom_call" | custom-call | tf_op jit(solution)/shard_map/gate_parts/pallas_call | solution.py:535
  82.2 19.6 %all-to-all-done.1 = bf16[32,136,128]{2,1,0:T(8,128)(2,1)S(1)} async-done(((bf16[32,136,128]{2,1,0:T(8,128)(2,1)}), bf16[32,136,128]{2,1,0:T(8,128)(2,1)S(1)}, u32[]{:S(2)}, u32[]{:S(2)}) %all-to-all-start.1) | async-done | bytes 1114144 | tf_op jit(solution)/shard_map/all_to_all | solution.py:566
  101.8 4.0 %gate.1 = f32[512,1024]{1,0:T(8,128)} custom-call(bf16[8,4,136,128]{3,2,1,0:T(8,128)(2,1)S(1)} %bitcast.5, f32[512,1024]{1,0:T(8,128)} %get-tuple-element.43.short_hbm, f32[512,1024]{1,0:T(8,128)} %get-tuple-element.44.skip_hbm), custom_call_target="tpu_custom_call" | custom-call | tf_op jit(solution)/shard_map/gate/pallas_call | solution.py:569
Async XLA Ops:
  0.0 7.2 %copy-start = (f32[2048,256]{1,0:T(8,128)S(1)}, f32[2048,256]{1,0:T(8,128)}, u32[]{:S(2)}) copy-start(f32[2048,256]{1,0:T(8,128)} %h_ref.1) | copy-start | bytes 6291460
  1.0 8.8 %collective-permute-start.2 = (f32[16,256]{1,0:T(8,128)S(1)}, f32[16,256]{1,0:T(8,128)S(1)}, u32[]{:S(2)}, u32[]{:S(2)}) collective-permute-start(f32[16,256]{1,0:T(8,128)S(1)} %get-tuple-element.26.refs_1_), channel_id=1, source_target_pairs={{0,3},{1,4},{2,5},{3,6},{4,7},{5,8},{6,9},{7,10},{8,11},{9,12},{10... | collective-permute-start | bytes 49160 | tf_op jit(solution)/shard_map/ppermute | solution.py:454
  5.2 4.6 %collective-permute-start.1 = (f32[16,256]{1,0:T(8,128)S(1)}, f32[16,256]{1,0:T(8,128)S(1)}, u32[]{:S(2)}, u32[]{:S(2)}) collective-permute-start(f32[16,256]{1,0:T(8,128)S(1)} %get-tuple-element.26.refs_1_), channel_id=1, source_target_pairs={{0,2},{1,3},{2,4},{3,5},{4,6},{5,7},{6,8},{7,9},{8,10},{9,11},{10,... | collective-permute-start | bytes 49160 | tf_op jit(solution)/shard_map/ppermute | solution.py:454
  5.8 5.4 %collective-permute-start = (bf16[16,1024]{1,0:T(8,128)(2,1)S(1)}, bf16[16,1024]{1,0:T(8,128)(2,1)S(1)}, u32[]{:S(2)}, u32[]{:S(2)}) collective-permute-start(bf16[16,1024]{1,0:T(8,128)(2,1)S(1)} %get-tuple-element.25), channel_id=1, source_target_pairs={{0,1},{1,2},{2,3},{3,4},{4,5},{5,6},{6,7},{7,8},{8,9},{9,10},{10,1... | collective-permute-start | bytes 98312 | tf_op jit(solution)/shard_map/ppermute | solution.py:454
  11.3 11.6 %copy-start.11 = (bf16[528,128]{1,0:T(8,128)(2,1)S(1)}, bf16[528,128]{1,0:T(8,128)(2,1)}, u32[]{:S(2)}) copy-start(bf16[528,128]{1,0:T(8,128)(2,1)} %get-tuple-element.36) | copy-start | bytes 405508
  11.3 12.1 %copy-start.10 = (bf16[528,128]{1,0:T(8,128)(2,1)S(1)}, bf16[528,128]{1,0:T(8,128)(2,1)}, u32[]{:S(2)}) copy-start(bf16[528,128]{1,0:T(8,128)(2,1)} %get-tuple-element.38) | copy-start | bytes 405508
  11.3 13.5 %copy-start.9 = (bf16[528,128]{1,0:T(8,128)(2,1)S(1)}, bf16[528,128]{1,0:T(8,128)(2,1)}, u32[]{:S(2)}) copy-start(bf16[528,128]{1,0:T(8,128)(2,1)} %get-tuple-element.40) | copy-start | bytes 405508
  11.3 14.9 %copy-start.8 = (bf16[528,128]{1,0:T(8,128)(2,1)S(1)}, bf16[528,128]{1,0:T(8,128)(2,1)}, u32[]{:S(2)}) copy-start(bf16[528,128]{1,0:T(8,128)(2,1)} %get-tuple-element.41) | copy-start | bytes 405508
  11.3 15.1 %copy-start.7 = (bf16[528,128]{1,0:T(8,128)(2,1)S(1)}, bf16[528,128]{1,0:T(8,128)(2,1)}, u32[]{:S(2)}) copy-start(bf16[528,128]{1,0:T(8,128)(2,1)} %get-tuple-element.42) | copy-start | bytes 405508
  11.3 34.7 %copy-start.1 = (bf16[768,256]{1,0:T(8,128)(2,1)S(1)}, bf16[768,256]{1,0:T(8,128)(2,1)}, u32[]{:S(2)}) copy-start(bf16[768,256]{1,0:T(8,128)(2,1)} %constant.20.clone.refs_9_.inner) | copy-start | bytes 1179652
  11.3 34.6 %copy-start.2 = (bf16[256,384]{1,0:T(8,128)(2,1)S(1)}, bf16[256,384]{1,0:T(8,128)(2,1)}, u32[]{:S(2)}) copy-start(bf16[256,384]{1,0:T(8,128)(2,1)} %constant.19.clone.refs_8_.outer) | copy-start | bytes 589828
  11.3 34.6 %copy-start.3 = (f32[2,128,128]{2,1,0:T(8,128)S(1)}, f32[2,128,128]{2,1,0:T(8,128)}, u32[]{:S(2)}) copy-start(f32[2,128,128]{2,1,0:T(8,128)} %constant.23.clone.refs_10_.twist) | copy-start | bytes 393220
  11.3 34.6 %copy-start.6 = (bf16[528,128]{1,0:T(8,128)(2,1)S(1)}, bf16[528,128]{1,0:T(8,128)(2,1)}, u32[]{:S(2)}) copy-start(bf16[528,128]{1,0:T(8,128)(2,1)} %get-tuple-element.35.refs_0_) | copy-start | bytes 405508
  11.4 7.2 %collective-permute-start.3 = (bf16[528,128]{1,0:T(8,128)(2,1)}, bf16[528,128]{1,0:T(8,128)(2,1)S(1)}, u32[]{:S(2)}, u32[]{:S(2)}) collective-permute-start(bf16[528,128]{1,0:T(8,128)(2,1)} %get-tuple-element.32), channel_id=1, source_target_pairs={{0,8},{4,12},{8,0},{12,4},{16,24},{20,28},{24,16},{28,20},{1,9},{5... | collective-permute-start | bytes 405512 | tf_op jit(solution)/shard_map/ppermute | solution.py:426
  12.3 6.2 %collective-permute-start.4 = (bf16[528,128]{1,0:T(8,128)(2,1)}, bf16[528,128]{1,0:T(8,128)(2,1)S(1)}, u32[]{:S(2)}, u32[]{:S(2)}) collective-permute-start(bf16[528,128]{1,0:T(8,128)(2,1)} %get-tuple-element.33), channel_id=1, source_target_pairs={{0,16},{4,20},{8,24},{12,28},{16,0},{20,4},{24,8},{28,12},{1,17},{... | collective-permute-start | bytes 405512 | tf_op jit(solution)/shard_map/ppermute | solution.py:426
  18.6 35.9 %all-to-all-start = ((bf16[32,136,128]{2,1,0:T(8,128)(2,1)}), bf16[32,136,128]{2,1,0:T(8,128)(2,1)S(1)}, u32[]{:S(2)}, u32[]{:S(2)}) async-start(bf16[32,136,128]{2,1,0:T(8,128)(2,1)} %bitcast.3), calls=%async_computation | async-start | bytes 2228224 | tf_op jit(solution)/shard_map/all_to_all | solution.py:510
  22.9 6.0 %collective-permute-start.5 = (bf16[528,128]{1,0:T(8,128)(2,1)S(1)}, bf16[528,128]{1,0:T(8,128)(2,1)S(1)}, u32[]{:S(2)}, u32[]{:S(2)}) collective-permute-start(bf16[528,128]{1,0:T(8,128)(2,1)S(1)} %copy-done.11), channel_id=1, source_target_pairs={{0,4},{4,0},{8,12},{12,8},{16,20},{20,16},{24,28},{28,24},{1,5},{5... | collective-permute-start | bytes 405512 | tf_op jit(solution)/shard_map/ppermute | solution.py:426
  23.4 13.5 %collective-permute-start.6 = (bf16[528,128]{1,0:T(8,128)(2,1)S(1)}, bf16[528,128]{1,0:T(8,128)(2,1)S(1)}, u32[]{:S(2)}, u32[]{:S(2)}) collective-permute-start(bf16[528,128]{1,0:T(8,128)(2,1)S(1)} %copy-done.10), channel_id=1, source_target_pairs={{0,12},{4,8},{8,4},{12,0},{16,28},{20,24},{24,20},{28,16},{1,13},{... | collective-permute-start | bytes 405512 | tf_op jit(solution)/shard_map/ppermute | solution.py:426
  24.8 13.7 %collective-permute-start.7 = (bf16[528,128]{1,0:T(8,128)(2,1)S(1)}, bf16[528,128]{1,0:T(8,128)(2,1)S(1)}, u32[]{:S(2)}, u32[]{:S(2)}) collective-permute-start(bf16[528,128]{1,0:T(8,128)(2,1)S(1)} %copy-done.9), channel_id=1, source_target_pairs={{0,20},{4,16},{8,28},{12,24},{16,4},{20,0},{24,12},{28,8},{1,21},{... | collective-permute-start | bytes 405512 | tf_op jit(solution)/shard_map/ppermute | solution.py:426
  26.2 14.3 %collective-permute-start.8 = (bf16[528,128]{1,0:T(8,128)(2,1)S(1)}, bf16[528,128]{1,0:T(8,128)(2,1)S(1)}, u32[]{:S(2)}, u32[]{:S(2)}) collective-permute-start(bf16[528,128]{1,0:T(8,128)(2,1)S(1)} %copy-done.8), channel_id=1, source_target_pairs={{0,24},{4,28},{8,16},{12,20},{16,8},{20,12},{24,0},{28,4},{1,25},{... | collective-permute-start | bytes 405512 | tf_op jit(solution)/shard_map/ppermute | solution.py:426
  26.4 19.6 %collective-permute-start.9 = (bf16[528,128]{1,0:T(8,128)(2,1)S(1)}, bf16[528,128]{1,0:T(8,128)(2,1)S(1)}, u32[]{:S(2)}, u32[]{:S(2)}) collective-permute-start(bf16[528,128]{1,0:T(8,128)(2,1)S(1)} %copy-done.7), channel_id=1, source_target_pairs={{0,28},{4,24},{8,20},{12,16},{16,12},{20,8},{24,4},{28,0},{1,29},{... | collective-permute-start | bytes 405512 | tf_op jit(solution)/shard_map/ppermute | solution.py:426
  46.0 8.5 %copy-start.4 = (bf16[768,256]{1,0:T(8,128)(2,1)S(1)}, bf16[768,256]{1,0:T(8,128)(2,1)}, u32[]{:S(2)}) copy-start(bf16[768,256]{1,0:T(8,128)(2,1)} %constant.21.clone.inner_back) | copy-start | bytes 1179652
  46.0 8.5 %copy-start.5 = (bf16[128,768]{1,0:T(8,128)(2,1)S(1)}, bf16[128,768]{1,0:T(8,128)(2,1)}, u32[]{:S(2)}) copy-start(bf16[128,768]{1,0:T(8,128)(2,1)} %constant.22.clone.outer_back) | copy-start | bytes 589828
  69.4 32.4 %all-to-all-start.1 = ((bf16[32,136,128]{2,1,0:T(8,128)(2,1)}), bf16[32,136,128]{2,1,0:T(8,128)(2,1)S(1)}, u32[]{:S(2)}, u32[]{:S(2)}) async-start(bf16[32,136,128]{2,1,0:T(8,128)(2,1)} %long_conv.1), calls=%async_computation.1 | async-start | bytes 2228224 | tf_op jit(solution)/shard_map/all_to_all | solution.py:566

commit v4 on v3

--- a/solution.py
+++ b/solution.py
@@ -195,16 +195,13 @@
         for step in range(steps):
             block = mixed[step * LANES : (step + 1) * LANES]
             scale = block_scale(jnp.max(jnp.abs(block), 0, keepdims=True))
-            scales.append(jnp.broadcast_to(scale, (PAD, LANES)))
+            scales.append(scale)
             codes.append(encode(block, 1.0 / scale).astype(bf16).T.astype(f32))
-        lane = lane_index((PAD, LANES))
+        unused = [jnp.ones((PAD - steps, LANES), f32)]
+        lines = jnp.concatenate([*scales, *unused], 0)
         for g in range(parts):
             piece = [code[g * per : (g + 1) * per] for code in codes]
-            line = jnp.ones((PAD, LANES), f32)
-            for step in range(steps):
-                moved = pltpu.roll(scales[step], ((step - g) * per) % LANES, 1)
-                inside = (lane >= step * per) & (lane < (step + 1) * per)
-                line = jnp.where(inside, moved, line)
+            line = pltpu.roll(lines, (-g * per) % LANES, 1)
             whole_piece = jnp.concatenate(piece + [line], 0).astype(bf16)
             out_ref[lax.rem(j, tiles) * parts + g, j // tiles] = whole_piece
         for copy in out_of(j):
@@ -240,15 +237,15 @@
             y_ref[lax.rem(j, tiles) * parts + g, j // tiles].astype(f32) for g in range(parts)
         ]
         lane = lane_index((PAD, LANES))
+        moved = [pltpu.roll(pieces[g][rows:], g * per, 1) for g in range(parts)]
         values = []
         for step in range(steps):
             code = jnp.concatenate([t[step * per : (step + 1) * per] for t in pieces], 0).T
             scale = jnp.ones((PAD, LANES), f32)
             for g in range(parts):
-                moved = pltpu.roll(pieces[g][rows:], ((g - step) * per) % LANES, 1)
                 inside = (lane >= g * per) & (lane < (g + 1) * per)
-                scale = jnp.where(inside, moved, scale)
-            values.append(decode(code, scale[0:1]))
+                scale = jnp.where(inside, moved[g], scale)
+            values.append(decode(code, scale[step : step + 1]))
         for copy in into(j):
             copy.wait()
         for step in range(steps):
@@ -325,7 +322,7 @@
 
     lax.fori_loop(0, peers, widen, 0)
 
-    def body(i, carry):
+    def body(i):
         first = i * group
         near = pltpu.roll(wide[...], LANES - first, 1)
         signal = jnp.concatenate(
@@ -340,36 +337,46 @@
             out_ref[first + p] = spectrum[p * rows : (p + 1) * rows]
         for copy in out_of(i):
             copy.start()
-        return carry
-
-    lax.fori_loop(0, per // group, body, 0)
+
+    for i in range(per // group):
+        body(i)
     wait_all(out_of, per // group)
 
 
 def conv_kernel(
-    dims, x_ref, h_hbm, outer, inner, inner_back, outer_back, twist, out_ref, held, h_ref, sem
+    dims, x_ref, h_hbm, outer, inner, inner_back, outer_back, twist, out_ref, *scratch
 ):
     rows, per, lines, blocks, group, batch = dims
-    fetch = pltpu.make_async_copy(h_hbm, h_ref, sem)
-    fetch.start()
+    held, h_ref, scales, found, sems = scratch
+    steps = lines // per
+    fetches = []
+    for i in range(per // group):
+        part = pl.ds(i * group, group)
+        fetches.append(pltpu.make_async_copy(h_hbm.at[part], h_ref.at[part], sems.at[i]))
+        fetches[-1].start()
 
     def unpack(i, carry):
         for j in range(batch):
             tile = x_ref[i * batch + j].astype(f32)
-            scale = jnp.broadcast_to(tile[lines : lines + 1], (LANES, LANES)).T[:lines]
-            start = pl.multiple_of((i * batch + j) * lines, 8)
-            held[pl.ds(start, lines), :] = decode(tile[:lines], scale)
+            held[pl.ds(pl.multiple_of((i * batch + j) * lines, 8), lines), :] = tile[:lines]
+            scales[i * batch + j] = tile[lines : lines + steps]
         return carry
 
     lax.fori_loop(0, blocks // batch, unpack, 0)
-    fetch.wait()
-
-    def body(i, carry):
+    lane = lane_index((rows, LANES))
+
+    def body(i):
         first = i * group
+        near = pltpu.roll(scales[...].reshape(rows, LANES), LANES - first, 1)
         signal = jnp.concatenate(
-            [held[pl.ds(first + p, rows, stride=per), :] for p in range(group)], 1
+            [
+                decode(held[pl.ds(first + p, rows, stride=per), :], near[:, p : p + 1])
+                for p in range(group)
+            ],
+            1,
         )
         spectrum = forward(signal, rows, outer, inner, twist)
+        fetches[i].wait()
         joined = []
         for p in range(group):
             re = spectrum[p * rows : (p + 1) * rows, :LANES]
@@ -378,21 +385,22 @@
             joined.append(jnp.concatenate([re * h_re - im * h_im, re * h_im + im * h_re], 1))
         result = backward(jnp.concatenate(joined, 0), rows, inner_back, outer_back, twist)
         for p in range(group):
-            held[pl.ds(first + p, rows, stride=per), :] = result[:, p * LANES : (p + 1) * LANES]
-        return carry
-
-    lax.fori_loop(0, per // group, body, 0)
+            value = result[:, p * LANES : (p + 1) * LANES]
+            scale = block_scale(jnp.max(jnp.abs(value), 1, keepdims=True))
+            held[pl.ds(first + p, rows, stride=per), :] = encode(value, 1.0 / scale)
+            found[...] = jnp.where(lane == first + p, scale, found[...])
+
+    found[...] = jnp.ones_like(found)
+    for i in range(per // group):
+        body(i)
+    scales[...] = found[...].reshape(scales.shape)
 
     def pack(i, carry):
         for j in range(batch):
             start = pl.multiple_of((i * batch + j) * lines, 8)
-            tile = held[pl.ds(start, lines), :]
-            scale = block_scale(jnp.max(jnp.abs(tile), 1, keepdims=True))
-            code = encode(tile, 1.0 / scale)
-            wide = jnp.broadcast_to(scale, (lines, LANES))
-            if lines < LANES:
-                wide = jnp.concatenate([wide, jnp.ones((LANES - lines, LANES), f32)], 0)
-            out_ref[i * batch + j] = jnp.concatenate([code, wide.T[:PAD]], 0).astype(bf16)
+            line = jnp.concatenate([scales[i * batch + j], jnp.ones((PAD - steps, LANES), f32)], 0)
+            tile = jnp.concatenate([held[pl.ds(start, lines), :], line], 0)
+            out_ref[i * batch + j] = tile.astype(bf16)
         return carry
 
     lax.fori_loop(0, blocks // batch, pack, 0)
@@ -551,14 +559,16 @@
     )
 
     convolved = pl.pallas_call(
-        functools.partial(conv_kernel, (rows, per, lines, devices, group, 4)),
+        functools.partial(conv_kernel, (rows, per, lines, devices, group, 8)),
         in_specs=[vmem, hbm] + [vmem] * 5,
         out_specs=vmem,
         out_shape=jax.ShapeDtypeStruct((devices, lines + PAD, LANES), bf16),
         scratch_shapes=[
             pltpu.VMEM((rows * per, LANES), f32),
             pltpu.VMEM((per, rows, 2 * LANES), f32),
-            pltpu.SemaphoreType.DMA,
+            pltpu.VMEM((devices, length // LANES, LANES), f32),
+            pltpu.VMEM((rows, LANES), f32),
+            pltpu.SemaphoreType.DMA((per // group,)),
         ],
         compiler_params=vmem_limit(28),
         name="long_conv",

time: 106 us -> 105 us (level)
  Pallas kernels: 44.3 us -> 42.5 us
    pallas_call x1, Pallas kernels: 14.9 us -> 13.7 us  [local(): pl.pallas_call(functools.partial(conv_kernel, (rows, per, lines, devices,...]
where the time goes in v4:
time: 105 us; the launch traced here: 104 us
  Pallas kernels  42.5 us (40%)
  waiting for transfers between devices  38.1 us (36%)
  starting transfers between devices  23 us (22%)
    all_to_all x1, waiting for transfers between devices, local(): lax.all_to_all(convolved, BOTH, split_axis=0, concat_axis=0, tiled=True)  19.6 us
    ppermute x7, waiting for transfers between devices, crossed(): lax.ppermute(array[s], axis, [(i, i ^ s) for i in range(count)])  17 us
    pallas_call x1, Pallas kernels, local(): pl.pallas_call(functools.partial(conv_kernel, (rows, per, lines, devices,...  13.7 us
    pallas_call x1, Pallas kernels, local(): pl.pallas_call(functools.partial(gate_parts_kernel, (length, tiles)), gri...  8.17 us
    ppermute x7, starting transfers between devices, crossed(): lax.ppermute(array[s], axis, [(i, i ^ s) for i in range(count)])  7.97 us
    pallas_call x1, Pallas kernels, local(): pl.pallas_call(functools.partial(filter_kernel, (rows, per, peers, group)...  7.83 us
    ppermute x3, starting transfers between devices, shifted(): lax.ppermute(array, BOTH, [(i, (i + by) % devices) for i in range(devices)])  6.15 us
    pallas_call x1, Pallas kernels, local(): pl.pallas_call(functools.partial(rows_out_kernel, (length, per, parts, ti...  5.39 us
  transfers between devices with their start and end apart: 12, of which 6 were waited for; matrix products, arithmetic and copies ran while one was open for 0% of the time, Pallas kernels for 23%

profile of v4, /device:TPU:1, one launch (start us, length us, event | category | flops | bytes accessed | tf_op | source)
XLA Modules:
  0.0 104.2 jit_solution(18218127775590684283)
XLA Ops:
  0.0 0.0 copy-start
  0.0 1.0 edges.1
  1.0 4.2 %collective-permute-start.2 = (f32[16,256]{1,0:T(8,128)S(1)}, f32[16,256]{1,0:T(8,128)S(1)}, u32[]{:S(2)}, u32[]{:S(2)}) collective-permute-start(f32[16,256]{1,0:T(8,128)S(1)} %get-tuple-element.26.refs_1_), channel_id=1, source_target_pairs={{0,3},{1,4},{2,5},{3,6},{4,7},{5,8},{6,9},{7,10},{8,11},{9,12},{10... | collective-permute-start | bytes 49160 | tf_op jit(solution)/shard_map/ppermute | solution.py:462
  5.2 0.6 collective-permute-start.1
  5.8 1.3 %collective-permute-start = (bf16[16,1024]{1,0:T(8,128)(2,1)S(1)}, bf16[16,1024]{1,0:T(8,128)(2,1)S(1)}, u32[]{:S(2)}, u32[]{:S(2)}) collective-permute-start(bf16[16,1024]{1,0:T(8,128)(2,1)S(1)} %get-tuple-element.25), channel_id=1, source_target_pairs={{0,1},{1,2},{2,3},{3,4},{4,5},{5,6},{6,7},{7,8},{8,9},{9,10},{10,1... | collective-permute-start | bytes 98312 | tf_op jit(solution)/shard_map/ppermute | solution.py:462
  7.1 0.1 pad_add_fusion.idx_ref
  7.2 0.0 copy-done
  7.2 2.6 %filter_rows.1 = (bf16[528,128]{1,0:T(8,128)(2,1)}, bf16[528,128]{1,0:T(8,128)(2,1)}, bf16[528,128]{1,0:T(8,128)(2,1)}, bf16[528,128]{1,0:T(8,128)(2,1)}, bf16[5...) custom-call(s32[2]{0:T(128)S(1)} %pad_add_fusion.idx_ref, ...), custom_call_target="tpu_custom_call" | custom-call | tf_op jit(solution)/shard_map/filter_rows/pallas_call | solution.py:468
  9.8 0.0 collective-permute-done.2.refs_3_
  9.8 0.0 collective-permute-done.1.refs_2_
  9.8 1.5 %collective-permute-done.refs_0_ = bf16[16,1024]{1,0:T(8,128)(2,1)S(1)} collective-permute-done((bf16[16,1024]{1,0:T(8,128)(2,1)S(1)}, bf16[16,1024]{1,0:T(8,128)(2,1)S(1)}, u32[]{:S(2)}, u32[]{:S(2)}) %collective-permute-start) | collective-permute-done | bytes 32800 | tf_op jit(solution)/shard_map/ppermute | solution.py:462
  11.3 0.0 copy-start.11
  11.3 0.0 copy-start.10
  11.3 0.0 copy-start.9
  11.3 0.0 copy-start.8
  11.3 0.0 copy-start.7
  11.3 0.0 copy-start.1
  11.3 0.0 copy-start.2
  11.3 0.0 copy-start.3
  11.3 0.0 copy-start.6
  11.4 1.0 collective-permute-start.3
  12.3 1.0 collective-permute-start.4
  13.3 5.4 %mixed_rows.1 = bf16[8,4,136,128]{3,2,1,0:T(8,128)(2,1)} custom-call(s32[2]{0:T(128)S(1)} %pad_add_fusion.idx_ref, bf16[512,1024]{1,0:T(8,128)(2,1)} %k_ref.3, bf16[512,1024]{1,0:T(8,128)(2,1)} %v_ref.3, bf16[16,1024]{1,0:T(8,128)(2,1)S(1)} %collective-permute-done.refs_0_, f32[16,256]{1,0:T(8,128)S(1)} %get-tuple-element.26.refs_1_, ...), custom_call_target="tpu_custom_call" | custom-call | tf_op jit(solution)/shard_map/mixed_rows/pallas_call | solution.py:497
  18.7 0.0 collective-permute-done.3.refs_2_
  18.7 0.0 collective-permute-done.4.refs_4_
  18.7 4.3 %all-to-all-start = ((bf16[32,136,128]{2,1,0:T(8,128)(2,1)}), bf16[32,136,128]{2,1,0:T(8,128)(2,1)S(1)}, u32[]{:S(2)}, u32[]{:S(2)}) async-start(bf16[32,136,128]{2,1,0:T(8,128)(2,1)} %bitcast.3), calls=%async_computation | async-start | bytes 2228224 | tf_op jit(solution)/shard_map/all_to_all | solution.py:518
  23.0 0.0 copy-done.11
  23.1 0.5 collective-permute-start.5
  23.5 0.0 copy-done.10
  23.5 1.4 %collective-permute-start.6 = (bf16[528,128]{1,0:T(8,128)(2,1)S(1)}, bf16[528,128]{1,0:T(8,128)(2,1)S(1)}, u32[]{:S(2)}, u32[]{:S(2)}) collective-permute-start(bf16[528,128]{1,0:T(8,128)(2,1)S(1)} %copy-done.10), channel_id=1, source_target_pairs={{0,12},{4,8},{8,4},{12,0},{16,28},{20,24},{24,20},{28,16},{1,13},{... | collective-permute-start | bytes 405512 | tf_op jit(solution)/shard_map/ppermute | solution.py:434
  24.9 0.0 copy-done.9
  24.9 1.4 %collective-permute-start.7 = (bf16[528,128]{1,0:T(8,128)(2,1)S(1)}, bf16[528,128]{1,0:T(8,128)(2,1)S(1)}, u32[]{:S(2)}, u32[]{:S(2)}) collective-permute-start(bf16[528,128]{1,0:T(8,128)(2,1)S(1)} %copy-done.9), channel_id=1, source_target_pairs={{0,20},{4,16},{8,28},{12,24},{16,4},{20,0},{24,12},{28,8},{1,21},{... | collective-permute-start | bytes 405512 | tf_op jit(solution)/shard_map/ppermute | solution.py:434
  26.4 0.0 copy-done.8
  26.4 0.1 collective-permute-start.8
  26.5 0.0 copy-done.7
  26.5 2.6 %collective-permute-start.9 = (bf16[528,128]{1,0:T(8,128)(2,1)S(1)}, bf16[528,128]{1,0:T(8,128)(2,1)S(1)}, u32[]{:S(2)}, u32[]{:S(2)}) collective-permute-start(bf16[528,128]{1,0:T(8,128)(2,1)S(1)} %copy-done.7), channel_id=1, source_target_pairs={{0,28},{4,24},{8,20},{12,16},{16,12},{20,8},{24,4},{28,0},{1,29},{... | collective-permute-start | bytes 405512 | tf_op jit(solution)/shard_map/ppermute | solution.py:434
  29.1 0.0 collective-permute-done.5.refs_1_
  29.1 7.9 %collective-permute-done.6.refs_3_ = bf16[528,128]{1,0:T(8,128)(2,1)S(1)} collective-permute-done((bf16[528,128]{1,0:T(8,128)(2,1)S(1)}, bf16[528,128]{1,0:T(8,128)(2,1)S(1)}, u32[]{:S(2)}, u32[]{:S(2)}) %collective-permute-start.6) | collective-permute-done | bytes 135200 | tf_op jit(solution)/shard_map/ppermute | solution.py:434
  37.0 1.6 %collective-permute-done.7.refs_5_ = bf16[528,128]{1,0:T(8,128)(2,1)S(1)} collective-permute-done((bf16[528,128]{1,0:T(8,128)(2,1)S(1)}, bf16[528,128]{1,0:T(8,128)(2,1)S(1)}, u32[]{:S(2)}, u32[]{:S(2)}) %collective-permute-start.7) | collective-permute-done | bytes 135200 | tf_op jit(solution)/shard_map/ppermute | solution.py:434
  38.6 2.1 %collective-permute-done.8.refs_6_ = bf16[528,128]{1,0:T(8,128)(2,1)S(1)} collective-permute-done((bf16[528,128]{1,0:T(8,128)(2,1)S(1)}, bf16[528,128]{1,0:T(8,128)(2,1)S(1)}, u32[]{:S(2)}, u32[]{:S(2)}) %collective-permute-start.8) | collective-permute-done | bytes 135200 | tf_op jit(solution)/shard_map/ppermute | solution.py:434
  40.7 5.4 %collective-permute-done.9.refs_7_ = bf16[528,128]{1,0:T(8,128)(2,1)S(1)} collective-permute-done((bf16[528,128]{1,0:T(8,128)(2,1)S(1)}, bf16[528,128]{1,0:T(8,128)(2,1)S(1)}, u32[]{:S(2)}, u32[]{:S(2)}) %collective-permute-start.9) | collective-permute-done | bytes 135200 | tf_op jit(solution)/shard_map/ppermute | solution.py:434
  46.1 0.0 copy-done.1
  46.1 0.0 copy-done.2
  46.1 0.0 copy-done.3
  46.1 0.0 copy-done.6
  46.1 0.0 copy-start.4
  46.1 0.0 copy-start.5
  46.1 7.8 %filter_spectrum.1.h_hbm = f32[32,128,256]{2,1,0:T(8,128)} custom-call(s32[2]{0:T(128)S(1)} %pad_add_fusion.idx_ref, bf16[528,128]{1,0:T(8,128)(2,1)S(1)} %copy-done.6, bf16[528,128]{1,0:T(8,128)(2,1)S(1)} %collective-permute-done.5.refs_1_, bf16[528,128]{1,0:T(8,128)(2,1)S(1)} %collective-permute-done.3.refs_2_, ...), custom_call_target="tpu_custom_call" | custom-call | tf_op jit(solution)/shard_map/filter_spectrum/pallas_call | solution.py:520
  54.0 0.0 all-to-all-done.x_ref
  54.0 0.0 copy-done.4
  54.0 0.0 copy-done.5
  54.0 13.7 %long_conv.1 = bf16[32,136,128]{2,1,0:T(8,128)(2,1)} custom-call(bf16[32,136,128]{2,1,0:T(8,128)(2,1)S(1)} %all-to-all-done.x_ref, f32[32,128,256]{2,1,0:T(8,128)} %filter_spectrum.1.h_hbm, bf16[256,384]{1,0:T(8,128)(2,1)S(1)} %copy-done.2, bf16[768,256]{1,0:T(8,128)(2,1)S(1)} %copy-done.1, bf16[768,256]{1,0:T(8,128)(2,1)S(1)} %copy-done.4, ...), custom_call_target="tpu_custom_call" | custom-call | tf_op jit(solution)/shard_map/long_conv/pallas_call | solution.py:561
  67.7 4.6 %all-to-all-start.1 = ((bf16[32,136,128]{2,1,0:T(8,128)(2,1)}), bf16[32,136,128]{2,1,0:T(8,128)(2,1)S(1)}, u32[]{:S(2)}, u32[]{:S(2)}) async-start(bf16[32,136,128]{2,1,0:T(8,128)(2,1)} %long_conv.1), calls=%async_computation.1 | async-start | bytes 2228224 | tf_op jit(solution)/shard_map/all_to_all | solution.py:576
  72.3 8.2 %gate_parts.1 = (f32[512,1024]{1,0:T(8,128)}, f32[512,1024]{1,0:T(8,128)}) custom-call(s32[2]{0:T(128)S(1)} %pad_add_fusion.idx_ref, bf16[512,1024]{1,0:T(8,128)(2,1)} %q_ref.3, bf16[512,1024]{1,0:T(8,128)(2,1)} %k_ref.3, bf16[512,1024]{1,0:T(8,128)(2,1)} %v_ref.3, bf16[16,1024]{1,0:T(8,128)(2,1)S(1)} %collective-permute-done.refs_0_, ...), custom_call_target="tpu_custom_call" | custom-call | tf_op jit(solution)/shard_map/gate_parts/pallas_call | solution.py:543
  80.5 19.6 %all-to-all-done.1 = bf16[32,136,128]{2,1,0:T(8,128)(2,1)S(1)} async-done(((bf16[32,136,128]{2,1,0:T(8,128)(2,1)}), bf16[32,136,128]{2,1,0:T(8,128)(2,1)S(1)}, u32[]{:S(2)}, u32[]{:S(2)}) %all-to-all-start.1) | async-done | bytes 1114144 | tf_op jit(solution)/shard_map/all_to_all | solution.py:576
  100.1 3.9 %gate.1 = f32[512,1024]{1,0:T(8,128)} custom-call(bf16[8,4,136,128]{3,2,1,0:T(8,128)(2,1)S(1)} %bitcast.5, f32[512,1024]{1,0:T(8,128)} %get-tuple-element.43.short_hbm, f32[512,1024]{1,0:T(8,128)} %get-tuple-element.44.skip_hbm), custom_call_target="tpu_custom_call" | custom-call | tf_op jit(solution)/shard_map/gate/pallas_call | solution.py:579
Async XLA Ops:
  0.0 7.2 %copy-start = (f32[2048,256]{1,0:T(8,128)S(1)}, f32[2048,256]{1,0:T(8,128)}, u32[]{:S(2)}) copy-start(f32[2048,256]{1,0:T(8,128)} %h_ref.1) | copy-start | bytes 6291460
  1.0 8.8 %collective-permute-start.2 = (f32[16,256]{1,0:T(8,128)S(1)}, f32[16,256]{1,0:T(8,128)S(1)}, u32[]{:S(2)}, u32[]{:S(2)}) collective-permute-start(f32[16,256]{1,0:T(8,128)S(1)} %get-tuple-element.26.refs_1_), channel_id=1, source_target_pairs={{0,3},{1,4},{2,5},{3,6},{4,7},{5,8},{6,9},{7,10},{8,11},{9,12},{10... | collective-permute-start | bytes 49160 | tf_op jit(solution)/shard_map/ppermute | solution.py:462
  5.2 4.6 %collective-permute-start.1 = (f32[16,256]{1,0:T(8,128)S(1)}, f32[16,256]{1,0:T(8,128)S(1)}, u32[]{:S(2)}, u32[]{:S(2)}) collective-permute-start(f32[16,256]{1,0:T(8,128)S(1)} %get-tuple-element.26.refs_1_), channel_id=1, source_target_pairs={{0,2},{1,3},{2,4},{3,5},{4,6},{5,7},{6,8},{7,9},{8,10},{9,11},{10,... | collective-permute-start | bytes 49160 | tf_op jit(solution)/shard_map/ppermute | solution.py:462
  5.8 5.4 %collective-permute-start = (bf16[16,1024]{1,0:T(8,128)(2,1)S(1)}, bf16[16,1024]{1,0:T(8,128)(2,1)S(1)}, u32[]{:S(2)}, u32[]{:S(2)}) collective-permute-start(bf16[16,1024]{1,0:T(8,128)(2,1)S(1)} %get-tuple-element.25), channel_id=1, source_target_pairs={{0,1},{1,2},{2,3},{3,4},{4,5},{5,6},{6,7},{7,8},{8,9},{9,10},{10,1... | collective-permute-start | bytes 98312 | tf_op jit(solution)/shard_map/ppermute | solution.py:462
  11.3 11.8 %copy-start.11 = (bf16[528,128]{1,0:T(8,128)(2,1)S(1)}, bf16[528,128]{1,0:T(8,128)(2,1)}, u32[]{:S(2)}) copy-start(bf16[528,128]{1,0:T(8,128)(2,1)} %get-tuple-element.36) | copy-start | bytes 405508
  11.3 12.2 %copy-start.10 = (bf16[528,128]{1,0:T(8,128)(2,1)S(1)}, bf16[528,128]{1,0:T(8,128)(2,1)}, u32[]{:S(2)}) copy-start(bf16[528,128]{1,0:T(8,128)(2,1)} %get-tuple-element.38) | copy-start | bytes 405508
  11.3 13.6 %copy-start.9 = (bf16[528,128]{1,0:T(8,128)(2,1)S(1)}, bf16[528,128]{1,0:T(8,128)(2,1)}, u32[]{:S(2)}) copy-start(bf16[528,128]{1,0:T(8,128)(2,1)} %get-tuple-element.40) | copy-start | bytes 405508
  11.3 15.1 %copy-start.8 = (bf16[528,128]{1,0:T(8,128)(2,1)S(1)}, bf16[528,128]{1,0:T(8,128)(2,1)}, u32[]{:S(2)}) copy-start(bf16[528,128]{1,0:T(8,128)(2,1)} %get-tuple-element.41) | copy-start | bytes 405508
  11.3 15.2 %copy-start.7 = (bf16[528,128]{1,0:T(8,128)(2,1)S(1)}, bf16[528,128]{1,0:T(8,128)(2,1)}, u32[]{:S(2)}) copy-start(bf16[528,128]{1,0:T(8,128)(2,1)} %get-tuple-element.42) | copy-start | bytes 405508
  11.3 34.8 %copy-start.1 = (bf16[768,256]{1,0:T(8,128)(2,1)S(1)}, bf16[768,256]{1,0:T(8,128)(2,1)}, u32[]{:S(2)}) copy-start(bf16[768,256]{1,0:T(8,128)(2,1)} %constant.20.clone.refs_9_.inner) | copy-start | bytes 1179652
  11.3 34.8 %copy-start.2 = (bf16[256,384]{1,0:T(8,128)(2,1)S(1)}, bf16[256,384]{1,0:T(8,128)(2,1)}, u32[]{:S(2)}) copy-start(bf16[256,384]{1,0:T(8,128)(2,1)} %constant.19.clone.refs_8_.outer) | copy-start | bytes 589828
  11.3 34.8 %copy-start.3 = (f32[2,128,128]{2,1,0:T(8,128)S(1)}, f32[2,128,128]{2,1,0:T(8,128)}, u32[]{:S(2)}) copy-start(f32[2,128,128]{2,1,0:T(8,128)} %constant.23.clone.refs_10_.twist) | copy-start | bytes 393220
  11.3 34.8 %copy-start.6 = (bf16[528,128]{1,0:T(8,128)(2,1)S(1)}, bf16[528,128]{1,0:T(8,128)(2,1)}, u32[]{:S(2)}) copy-start(bf16[528,128]{1,0:T(8,128)(2,1)} %get-tuple-element.35.refs_0_) | copy-start | bytes 405508
  11.4 7.4 %collective-permute-start.3 = (bf16[528,128]{1,0:T(8,128)(2,1)}, bf16[528,128]{1,0:T(8,128)(2,1)S(1)}, u32[]{:S(2)}, u32[]{:S(2)}) collective-permute-start(bf16[528,128]{1,0:T(8,128)(2,1)} %get-tuple-element.32), channel_id=1, source_target_pairs={{0,8},{4,12},{8,0},{12,4},{16,24},{20,28},{24,16},{28,20},{1,9},{5... | collective-permute-start | bytes 405512 | tf_op jit(solution)/shard_map/ppermute | solution.py:434
  12.3 6.4 %collective-permute-start.4 = (bf16[528,128]{1,0:T(8,128)(2,1)}, bf16[528,128]{1,0:T(8,128)(2,1)S(1)}, u32[]{:S(2)}, u32[]{:S(2)}) collective-permute-start(bf16[528,128]{1,0:T(8,128)(2,1)} %get-tuple-element.33), channel_id=1, source_target_pairs={{0,16},{4,20},{8,24},{12,28},{16,0},{20,4},{24,8},{28,12},{1,17},{... | collective-permute-start | bytes 405512 | tf_op jit(solution)/shard_map/ppermute | solution.py:434
  18.7 35.3 %all-to-all-start = ((bf16[32,136,128]{2,1,0:T(8,128)(2,1)}), bf16[32,136,128]{2,1,0:T(8,128)(2,1)S(1)}, u32[]{:S(2)}, u32[]{:S(2)}) async-start(bf16[32,136,128]{2,1,0:T(8,128)(2,1)} %bitcast.3), calls=%async_computation | async-start | bytes 2228224 | tf_op jit(solution)/shard_map/all_to_all | solution.py:518
  23.1 6.0 %collective-permute-start.5 = (bf16[528,128]{1,0:T(8,128)(2,1)S(1)}, bf16[528,128]{1,0:T(8,128)(2,1)S(1)}, u32[]{:S(2)}, u32[]{:S(2)}) collective-permute-start(bf16[528,128]{1,0:T(8,128)(2,1)S(1)} %copy-done.11), channel_id=1, source_target_pairs={{0,4},{4,0},{8,12},{12,8},{16,20},{20,16},{24,28},{28,24},{1,5},{5... | collective-permute-start | bytes 405512 | tf_op jit(solution)/shard_map/ppermute | solution.py:434
  23.5 13.5 %collective-permute-start.6 = (bf16[528,128]{1,0:T(8,128)(2,1)S(1)}, bf16[528,128]{1,0:T(8,128)(2,1)S(1)}, u32[]{:S(2)}, u32[]{:S(2)}) collective-permute-start(bf16[528,128]{1,0:T(8,128)(2,1)S(1)} %copy-done.10), channel_id=1, source_target_pairs={{0,12},{4,8},{8,4},{12,0},{16,28},{20,24},{24,20},{28,16},{1,13},{... | collective-permute-start | bytes 405512 | tf_op jit(solution)/shard_map/ppermute | solution.py:434
  24.9 13.7 %collective-permute-start.7 = (bf16[528,128]{1,0:T(8,128)(2,1)S(1)}, bf16[528,128]{1,0:T(8,128)(2,1)S(1)}, u32[]{:S(2)}, u32[]{:S(2)}) collective-permute-start(bf16[528,128]{1,0:T(8,128)(2,1)S(1)} %copy-done.9), channel_id=1, source_target_pairs={{0,20},{4,16},{8,28},{12,24},{16,4},{20,0},{24,12},{28,8},{1,21},{... | collective-permute-start | bytes 405512 | tf_op jit(solution)/shard_map/ppermute | solution.py:434
  26.4 14.3 %collective-permute-start.8 = (bf16[528,128]{1,0:T(8,128)(2,1)S(1)}, bf16[528,128]{1,0:T(8,128)(2,1)S(1)}, u32[]{:S(2)}, u32[]{:S(2)}) collective-permute-start(bf16[528,128]{1,0:T(8,128)(2,1)S(1)} %copy-done.8), channel_id=1, source_target_pairs={{0,24},{4,28},{8,16},{12,20},{16,8},{20,12},{24,0},{28,4},{1,25},{... | collective-permute-start | bytes 405512 | tf_op jit(solution)/shard_map/ppermute | solution.py:434
  26.5 19.6 %collective-permute-start.9 = (bf16[528,128]{1,0:T(8,128)(2,1)S(1)}, bf16[528,128]{1,0:T(8,128)(2,1)S(1)}, u32[]{:S(2)}, u32[]{:S(2)}) collective-permute-start(bf16[528,128]{1,0:T(8,128)(2,1)S(1)} %copy-done.7), channel_id=1, source_target_pairs={{0,28},{4,24},{8,20},{12,16},{16,12},{20,8},{24,4},{28,0},{1,29},{... | collective-permute-start | bytes 405512 | tf_op jit(solution)/shard_map/ppermute | solution.py:434
  46.1 7.9 %copy-start.4 = (bf16[768,256]{1,0:T(8,128)(2,1)S(1)}, bf16[768,256]{1,0:T(8,128)(2,1)}, u32[]{:S(2)}) copy-start(bf16[768,256]{1,0:T(8,128)(2,1)} %constant.21.clone.inner_back) | copy-start | bytes 1179652
  46.1 7.9 %copy-start.5 = (bf16[128,768]{1,0:T(8,128)(2,1)S(1)}, bf16[128,768]{1,0:T(8,128)(2,1)}, u32[]{:S(2)}) copy-start(bf16[128,768]{1,0:T(8,128)(2,1)} %constant.22.clone.outer_back) | copy-start | bytes 589828
  67.7 32.4 %all-to-all-start.1 = ((bf16[32,136,128]{2,1,0:T(8,128)(2,1)}), bf16[32,136,128]{2,1,0:T(8,128)(2,1)S(1)}, u32[]{:S(2)}, u32[]{:S(2)}) async-start(bf16[32,136,128]{2,1,0:T(8,128)(2,1)} %long_conv.1), calls=%async_computation.1 | async-start | bytes 2228224 | tf_op jit(solution)/shard_map/all_to_all | solution.py:576

commit v5 on v4

--- a/solution.py
+++ b/solution.py
@@ -173,21 +173,17 @@
     lax.fori_loop(0, count, step, 0)
 
 
-def rows_out_kernel(dims, idx_ref, k_hbm, v_hbm, *refs):
+def rows_out_kernel(dims, idx_ref, k_ref, v_ref, *refs):
     length, per, parts, tiles, count = dims
-    out_hbm, k_ref, v_ref, out_ref, k_ext, v_ext, sems, out_sems = refs[-8:]
+    out_hbm, out_ref, k_ext, v_ext, out_sems = refs[-5:]
     steps = length // LANES
-    into = lambda j: column_copies((k_hbm, v_hbm), (k_ref, v_ref), sems, j)
-    start_all(into, count)
 
     def out_of(j):
         where = (pl.ds(lax.rem(j, tiles) * parts, parts), pl.ds(j // tiles, 1))
         return [pltpu.make_async_copy(out_ref.at[where], out_hbm.at[where], out_sems.at[j])]
 
     def tile(j, carry):
-        weights, _, before = taps_and_edge(idx_ref, refs[:-8], tiles, j)
-        for copy in into(j):
-            copy.wait()
+        weights, _, before = taps_and_edge(idx_ref, refs[:-5], tiles, j)
         fill(k_ext, k_ref[:, columns(j)], before[2:4])
         fill(v_ext, v_ref[:, columns(j)], before[4:6])
         mixed = short_conv(k_ext, weights[3:6], length) * short_conv(v_ext, weights[6:9], length)
@@ -224,12 +220,12 @@
     skip_ref[...] = bias * mixed
 
 
-def gate_kernel(dims, y_ref, short_hbm, skip_hbm, out_hbm, short_ref, skip_ref, out_ref, sems):
+def gate_kernel(dims, y_ref, short_ref, skip_hbm, out_hbm, skip_ref, out_ref, sems, out_sems):
     length, per, parts, tiles, count = dims
     steps = length // LANES
     rows = steps * per
-    into = lambda j: column_copies((short_hbm, skip_hbm), (short_ref, skip_ref), sems, j)
-    out_of = lambda j: column_copies((out_ref,), (out_hbm,), sems.at[pl.ds(2, 1)], j)
+    into = lambda j: column_copies((skip_hbm,), (skip_ref,), sems, j)
+    out_of = lambda j: column_copies((out_ref,), (out_hbm,), out_sems, j)
     start_all(into, count)
 
     def tile(j, carry):
@@ -261,9 +257,15 @@
     wait_all(out_of, count)
 
 
-def filter_rows_kernel(dims, idx_ref, h_ref, *refs):
+def filter_rows_kernel(dims, idx_ref, h_ref, k_hbm, v_hbm, *refs):
     per, peers, chunk = dims
-    outs, turned, lines = refs[:peers], refs[-2], refs[-1]
+    outs, (k_ref, v_ref, turned, lines, sems) = refs[:peers], refs[peers:]
+    fetches = [
+        pltpu.make_async_copy(k_hbm, k_ref, sems.at[0]),
+        pltpu.make_async_copy(v_hbm, v_ref, sems.at[1]),
+    ]
+    for fetch in fetches:
+        fetch.start()
     me = idx_ref[0]
     parts = LANES // per
     for r in range(chunk):
@@ -279,6 +281,8 @@
         peer = lax.bitwise_xor(me, s)
         outs[s][0 : chunk * per] = turned[peer].reshape(chunk * per, LANES)
         outs[s][chunk * per :] = lines[peer].astype(bf16)
+    for fetch in fetches:
+        fetch.wait()
 
 
 def filter_kernel(dims, idx_ref, *refs):
@@ -465,24 +469,28 @@
     taps = [own] + [shifted(own, s) for s in range(2, depth)]
 
     chunk = long_filter.shape[0] // LANES
-    pieces = pl.pallas_call(
+    vmem, hbm = pl.BlockSpec(memory_space=pltpu.VMEM), pl.BlockSpec(memory_space=pltpu.HBM)
+    *pieces, key_near, value_near = pl.pallas_call(
         functools.partial(filter_rows_kernel, (per, peers, chunk)),
         grid_spec=pltpu.PrefetchScalarGridSpec(
             num_scalar_prefetch=1,
             grid=(1,),
-            in_specs=[whole(long_filter)],
-            out_specs=[pl.BlockSpec((chunk * per + chunk, LANES), lambda *_: (0, 0))] * peers,
+            in_specs=[whole(long_filter), hbm, hbm],
+            out_specs=[pl.BlockSpec((chunk * per + chunk, LANES), lambda *_: (0, 0))] * peers
+            + [vmem] * 2,
             scratch_shapes=[
                 pltpu.VMEM((peers, chunk, per, LANES), bf16),
                 pltpu.VMEM((peers, chunk, LANES), f32),
+                pltpu.SemaphoreType.DMA((2,)),
             ],
         ),
-        out_shape=[pltpu.HBM((chunk * per + chunk, LANES), bf16)] * peers,
+        out_shape=[pltpu.HBM((chunk * per + chunk, LANES), bf16)] * peers
+        + [pltpu.VMEM((length, width), bf16)] * 2,
         compiler_params=vmem_limit(16),
         name="filter_rows",
-    )(me, long_filter)
+    )(me, long_filter, key, value)
     pieces = list(pieces)
-    early = [s for s in (2, 4) if s < peers]
+    early = [s for s in (2, 4, 6) if s < peers]
     edge, *ready = lax.optimization_barrier((edge, *taps[1:], *(pieces[s] for s in early)))
     taps[1:] = ready[: depth - 2]
     for s, piece in zip(early, ready[depth - 2 :]):
@@ -492,25 +500,21 @@
     row_spec = pl.BlockSpec((length, LANES), lambda j, _: (0, j))
     wire_shape = jax.ShapeDtypeStruct((peers, depth, lines + PAD, LANES), bf16)
     ext = pltpu.VMEM((length + 8, LANES), f32)
-    vmem, hbm = pl.BlockSpec(memory_space=pltpu.VMEM), pl.BlockSpec(memory_space=pltpu.HBM)
     count = width // LANES
     coded = pl.pallas_call(
         functools.partial(rows_out_kernel, (length, per, parts, tiles, count)),
-        in_specs=[pl.BlockSpec(memory_space=pltpu.SMEM), hbm, hbm] + [vmem] * depth,
+        in_specs=[pl.BlockSpec(memory_space=pltpu.SMEM)] + [vmem] * (depth + 2),
         out_specs=hbm,
         out_shape=wire_shape,
         scratch_shapes=[
-            pltpu.VMEM((length, width), bf16),
-            pltpu.VMEM((length, width), bf16),
             pltpu.VMEM(wire_shape.shape, bf16),
             ext,
             ext,
-            pltpu.SemaphoreType.DMA((2, count)),
             pltpu.SemaphoreType.DMA((count,)),
         ],
         compiler_params=vmem_limit(16),
         name="mixed_rows",
-    )(me, key, value, edge, *taps)
+    )(me, key_near, value_near, edge, *taps)
     coded, *ready = lax.optimization_barrier((coded, *(pieces[s] for s in early)))
     for s, piece in zip(early, ready):
         pieces[s] = piece
@@ -549,14 +553,12 @@
             out_specs=[row_spec, row_spec],
             scratch_shapes=[ext] * 3,
         ),
-        out_shape=[pltpu.HBM((length, width), f32)] * 2,
+        out_shape=[pltpu.VMEM((length, width), f32), pltpu.HBM((length, width), f32)],
         compiler_params=vmem_limit(12),
         name="gate_parts",
     )(me, query, key, value, edge, *taps)
 
-    query_short, skip, spectrum = (
-        pltpu.with_memory_space_constraint(a, pltpu.HBM) for a in (query_short, skip, spectrum)
-    )
+    skip, spectrum = (pltpu.with_memory_space_constraint(a, pltpu.HBM) for a in (skip, spectrum))
 
     convolved = pl.pallas_call(
         functools.partial(conv_kernel, (rows, per, lines, devices, group, 8)),
@@ -578,11 +580,11 @@
 
     return pl.pallas_call(
         functools.partial(gate_kernel, (length, per, parts, tiles, count)),
-        in_specs=[vmem, hbm, hbm],
+        in_specs=[vmem, vmem, hbm],
         out_specs=hbm,
         out_shape=jax.ShapeDtypeStruct((length, width), f32),
-        scratch_shapes=[pltpu.VMEM((length, width), f32)] * 3
-        + [pltpu.SemaphoreType.DMA((3, count))],
+        scratch_shapes=[pltpu.VMEM((length, width), f32)] * 2
+        + [pltpu.SemaphoreType.DMA((1, count))] * 2,
         compiler_params=vmem_limit(20),
         name="gate",
     )(returned, query_short, skip)

time: 105 us -> 103 us (0.981)
    all_to_all x1, starting transfers between devices: 4.3 us -> 6.81 us  [local(): lax.all_to_all(coded, BOTH, split_axis=0, concat_axis=0, tiled=True)]
    ppermute x7, starting transfers between devices: 7.97 us -> 6.07 us  [crossed(): lax.ppermute(array[s], axis, [(i, i ^ s) for i in range(count)])]
    all_to_all x1, waiting for transfers between devices: 0.01 us -> 1.5 us  [local(): lax.all_to_all(coded, BOTH, split_axis=0, concat_axis=0, tiled=True)]
    ppermute x3, waiting for transfers between devices: 1.5 us -> 0.04 us  [shifted(): lax.ppermute(array, BOTH, [(i, (i + by) % devices) for i in range(devices)])]
    pallas_call x1, Pallas kernels: 2.56 us -> 3.99 us  [local(): pl.pallas_call(functools.partial(filter_rows_kernel, (per, peers, chunk))...]
    ppermute x7, waiting for transfers between devices: 17 us -> 15.8 us  [crossed(): lax.ppermute(array[s], axis, [(i, i ^ s) for i in range(count)])]
    pallas_call x1, Pallas kernels: 5.39 us -> 4.29 us  [local(): pl.pallas_call(functools.partial(rows_out_kernel, (length, per, parts, ti...]
where the time goes in v5:
time: 103 us
  Pallas kernels  42.3 us (41%)
  waiting for transfers between devices  37.2 us (36%)
  starting transfers between devices  22.8 us (22%)
    all_to_all x1, waiting for transfers between devices, local(): lax.all_to_all(convolved, BOTH, split_axis=0, concat_axis=0, tiled=True)  19.8 us
    ppermute x7, waiting for transfers between devices, crossed(): lax.ppermute(array[s], axis, [(i, i ^ s) for i in range(count)])  15.8 us
    pallas_call x1, Pallas kernels, local(): pl.pallas_call(functools.partial(conv_kernel, (rows, per, lines, devices,...  13.7 us
    pallas_call x1, Pallas kernels, local(): pl.pallas_call(functools.partial(gate_parts_kernel, (length, tiles)), gri...  7.9 us
    pallas_call x1, Pallas kernels, local(): pl.pallas_call(functools.partial(filter_kernel, (rows, per, peers, group)...  7.82 us
    all_to_all x1, starting transfers between devices, local(): lax.all_to_all(coded, BOTH, split_axis=0, concat_axis=0, tiled=True)  6.81 us
    ppermute x3, starting transfers between devices, shifted(): lax.ppermute(array, BOTH, [(i, (i + by) % devices) for i in range(devices)])  6.15 us
    ppermute x7, starting transfers between devices, crossed(): lax.ppermute(array[s], axis, [(i, i ^ s) for i in range(count)])  6.07 us
  transfers between devices with their start and end apart: 12, of which 6 were waited for; matrix products, arithmetic and copies ran while one was open for 0% of the time, Pallas kernels for 23%

profile of v5, /device:TPU:1, one launch (start us, length us, event | category | flops | bytes accessed | tf_op | source)
XLA Modules:
  0.0 102.7 jit_solution(10675130143774768496)
XLA Ops:
  0.0 0.0 copy-start
  0.0 1.0 edges.1
  1.0 4.2 %collective-permute-start.2 = (f32[16,256]{1,0:T(8,128)S(1)}, f32[16,256]{1,0:T(8,128)S(1)}, u32[]{:S(2)}, u32[]{:S(2)}) collective-permute-start(f32[16,256]{1,0:T(8,128)S(1)} %get-tuple-element.32.refs_1_), channel_id=1, source_target_pairs={{0,3},{1,4},{2,5},{3,6},{4,7},{5,8},{6,9},{7,10},{8,11},{9,12},{10... | collective-permute-start | bytes 49160 | tf_op jit(solution)/shard_map/ppermute | solution.py:466
  5.2 0.6 collective-permute-start.1
  5.8 1.3 %collective-permute-start = (bf16[16,1024]{1,0:T(8,128)(2,1)S(1)}, bf16[16,1024]{1,0:T(8,128)(2,1)S(1)}, u32[]{:S(2)}, u32[]{:S(2)}) collective-permute-start(bf16[16,1024]{1,0:T(8,128)(2,1)S(1)} %get-tuple-element.31), channel_id=1, source_target_pairs={{0,1},{1,2},{2,3},{3,4},{4,5},{5,6},{6,7},{7,8},{8,9},{9,10},{10,1... | collective-permute-start | bytes 98312 | tf_op jit(solution)/shard_map/ppermute | solution.py:466
  7.1 0.1 pad_add_fusion.idx_ref
  7.2 0.0 copy-done
  7.2 4.0 %filter_rows.1 = (bf16[528,128]{1,0:T(8,128)(2,1)}, bf16[528,128]{1,0:T(8,128)(2,1)}, bf16[528,128]{1,0:T(8,128)(2,1)}, bf16[528,128]{1,0:T(8,128)(2,1)}, bf16[5...) custom-call(s32[2]{0:T(128)S(1)} %pad_add_fusion.idx_ref, ...), custom_call_target="tpu_custom_call" | custom-call | tf_op jit(solution)/shard_map/filter_rows/pallas_call | solution.py:473
  11.2 0.0 collective-permute-done.2.refs_3_
  11.2 0.0 collective-permute-done.1.refs_2_
  11.2 0.0 collective-permute-done.refs_0_
  11.3 1.2 %collective-permute-start.3 = (bf16[528,128]{1,0:T(8,128)(2,1)}, bf16[528,128]{1,0:T(8,128)(2,1)S(1)}, u32[]{:S(2)}, u32[]{:S(2)}) collective-permute-start(bf16[528,128]{1,0:T(8,128)(2,1)} %get-tuple-element.39), channel_id=1, source_target_pairs={{0,8},{4,12},{8,0},{12,4},{16,24},{20,28},{24,16},{28,20},{1,9},{5... | collective-permute-start | bytes 405512 | tf_op jit(solution)/shard_map/ppermute | solution.py:438
  12.5 0.6 collective-permute-start.4
  13.2 0.8 collective-permute-start.5
  14.0 0.0 copy-start.10
  14.0 0.0 copy-start.9
  14.0 0.0 copy-start.8
  14.0 0.0 copy-start.7
  14.0 0.0 copy-start.1
  14.0 0.0 copy-start.2
  14.0 0.0 copy-start.3
  14.0 0.0 copy-start.6
  14.0 4.3 %mixed_rows.1 = bf16[8,4,136,128]{3,2,1,0:T(8,128)(2,1)} custom-call(s32[2]{0:T(128)S(1)} %pad_add_fusion.idx_ref, bf16[512,1024]{1,0:T(8,128)(2,1)S(1)} %get-tuple-element.29.k_ref, bf16[512,1024]{1,0:T(8,128)(2,1)S(1)} %get-tuple-element.30.v_ref, bf16[16,1024]{1,0:T(8,128)(2,1)S(1)} %collective-permute-done.refs_0_, ...), custom_call_target="tpu_custom_call" | custom-call | tf_op jit(solution)/shard_map/mixed_rows/pallas_call | solution.py:504
  18.3 0.0 collective-permute-done.3.refs_2_
  18.3 0.0 collective-permute-done.4.refs_4_
  18.4 0.9 collective-permute-done.5.refs_6_
  19.2 6.8 %all-to-all-start = ((bf16[32,136,128]{2,1,0:T(8,128)(2,1)}), bf16[32,136,128]{2,1,0:T(8,128)(2,1)S(1)}, u32[]{:S(2)}, u32[]{:S(2)}) async-start(bf16[32,136,128]{2,1,0:T(8,128)(2,1)} %bitcast.3), calls=%async_computation | async-start | bytes 2228224 | tf_op jit(solution)/shard_map/all_to_all | solution.py:522
  26.1 0.0 copy-done.10
  26.1 0.3 collective-permute-start.6
  26.4 0.0 copy-done.9
  26.4 1.5 %collective-permute-start.7 = (bf16[528,128]{1,0:T(8,128)(2,1)S(1)}, bf16[528,128]{1,0:T(8,128)(2,1)S(1)}, u32[]{:S(2)}, u32[]{:S(2)}) collective-permute-start(bf16[528,128]{1,0:T(8,128)(2,1)S(1)} %copy-done.9), channel_id=1, source_target_pairs={{0,12},{4,8},{8,4},{12,0},{16,28},{20,24},{24,20},{28,16},{1,13},{... | collective-permute-start | bytes 405512 | tf_op jit(solution)/shard_map/ppermute | solution.py:438
  27.9 0.0 copy-done.8
  27.9 1.4 %collective-permute-start.8 = (bf16[528,128]{1,0:T(8,128)(2,1)S(1)}, bf16[528,128]{1,0:T(8,128)(2,1)S(1)}, u32[]{:S(2)}, u32[]{:S(2)}) collective-permute-start(bf16[528,128]{1,0:T(8,128)(2,1)S(1)} %copy-done.8), channel_id=1, source_target_pairs={{0,20},{4,16},{8,28},{12,24},{16,4},{20,0},{24,12},{28,8},{1,21},{... | collective-permute-start | bytes 405512 | tf_op jit(solution)/shard_map/ppermute | solution.py:438
  29.4 0.0 copy-done.7
  29.4 0.1 collective-permute-start.9
  29.5 0.0 collective-permute-done.6.refs_1_
  29.5 10.5 %collective-permute-done.7.refs_3_ = bf16[528,128]{1,0:T(8,128)(2,1)S(1)} collective-permute-done((bf16[528,128]{1,0:T(8,128)(2,1)S(1)}, bf16[528,128]{1,0:T(8,128)(2,1)S(1)}, u32[]{:S(2)}, u32[]{:S(2)}) %collective-permute-start.7) | collective-permute-done | bytes 135200 | tf_op jit(solution)/shard_map/ppermute | solution.py:438
  40.0 1.5 %collective-permute-done.8.refs_5_ = bf16[528,128]{1,0:T(8,128)(2,1)S(1)} collective-permute-done((bf16[528,128]{1,0:T(8,128)(2,1)S(1)}, bf16[528,128]{1,0:T(8,128)(2,1)S(1)}, u32[]{:S(2)}, u32[]{:S(2)}) %collective-permute-start.8) | collective-permute-done | bytes 135200 | tf_op jit(solution)/shard_map/ppermute | solution.py:438
  41.5 3.0 %collective-permute-done.9.refs_7_ = bf16[528,128]{1,0:T(8,128)(2,1)S(1)} collective-permute-done((bf16[528,128]{1,0:T(8,128)(2,1)S(1)}, bf16[528,128]{1,0:T(8,128)(2,1)S(1)}, u32[]{:S(2)}, u32[]{:S(2)}) %collective-permute-start.9) | collective-permute-done | bytes 135200 | tf_op jit(solution)/shard_map/ppermute | solution.py:438
  44.4 0.0 copy-done.1
  44.4 0.0 copy-done.2
  44.4 0.0 copy-done.3
  44.4 0.0 copy-done.6
  44.4 0.0 copy-start.4
  44.5 0.0 copy-start.5
  44.5 7.8 %filter_spectrum.1.h_hbm = f32[32,128,256]{2,1,0:T(8,128)} custom-call(s32[2]{0:T(128)S(1)} %pad_add_fusion.idx_ref, bf16[528,128]{1,0:T(8,128)(2,1)S(1)} %copy-done.6, bf16[528,128]{1,0:T(8,128)(2,1)S(1)} %collective-permute-done.6.refs_1_, bf16[528,128]{1,0:T(8,128)(2,1)S(1)} %collective-permute-done.3.refs_2_, ...), custom_call_target="tpu_custom_call" | custom-call | tf_op jit(solution)/shard_map/filter_spectrum/pallas_call | solution.py:524
  52.3 1.5 %all-to-all-done.x_ref = bf16[32,136,128]{2,1,0:T(8,128)(2,1)S(1)} async-done(((bf16[32,136,128]{2,1,0:T(8,128)(2,1)}), bf16[32,136,128]{2,1,0:T(8,128)(2,1)S(1)}, u32[]{:S(2)}, u32[]{:S(2)}) %all-to-all-start) | async-done | bytes 1114144 | tf_op jit(solution)/shard_map/all_to_all | solution.py:522
  53.8 0.0 copy-done.4
  53.8 0.0 copy-done.5
  53.8 13.7 %long_conv.1 = bf16[32,136,128]{2,1,0:T(8,128)(2,1)} custom-call(bf16[32,136,128]{2,1,0:T(8,128)(2,1)S(1)} %all-to-all-done.x_ref, f32[32,128,256]{2,1,0:T(8,128)} %filter_spectrum.1.h_hbm, bf16[256,384]{1,0:T(8,128)(2,1)S(1)} %copy-done.2, bf16[768,256]{1,0:T(8,128)(2,1)S(1)} %copy-done.1, bf16[768,256]{1,0:T(8,128)(2,1)S(1)} %copy-done.4, ...), custom_call_target="tpu_custom_call" | custom-call | tf_op jit(solution)/shard_map/long_conv/pallas_call | solution.py:563
  67.5 3.8 %all-to-all-start.1 = ((bf16[32,136,128]{2,1,0:T(8,128)(2,1)}), bf16[32,136,128]{2,1,0:T(8,128)(2,1)S(1)}, u32[]{:S(2)}, u32[]{:S(2)}) async-start(bf16[32,136,128]{2,1,0:T(8,128)(2,1)} %long_conv.1), calls=%async_computation.1 | async-start | bytes 2228224 | tf_op jit(solution)/shard_map/all_to_all | solution.py:578
  71.2 7.9 %gate_parts.1 = (f32[512,1024]{1,0:T(8,128)S(1)}, f32[512,1024]{1,0:T(8,128)}) custom-call(s32[2]{0:T(128)S(1)} %pad_add_fusion.idx_ref, bf16[512,1024]{1,0:T(8,128)(2,1)} %q_ref.3, bf16[512,1024]{1,0:T(8,128)(2,1)} %k_ref.3, bf16[512,1024]{1,0:T(8,128)(2,1)} %v_ref.3, bf16[16,1024]{1,0:T(8,128)(2,1)S(1)} %collective-permute-done.refs_0_, ...), custom_call_target="tpu_custom_call" | custom-call | tf_op jit(solution)/shard_map/gate_parts/pallas_call | solution.py:547
  79.1 19.8 %all-to-all-done.1 = bf16[32,136,128]{2,1,0:T(8,128)(2,1)S(1)} async-done(((bf16[32,136,128]{2,1,0:T(8,128)(2,1)}), bf16[32,136,128]{2,1,0:T(8,128)(2,1)S(1)}, u32[]{:S(2)}, u32[]{:S(2)}) %all-to-all-start.1) | async-done | bytes 1114144 | tf_op jit(solution)/shard_map/all_to_all | solution.py:578
  99.0 3.6 %gate.1 = f32[512,1024]{1,0:T(8,128)} custom-call(bf16[8,4,136,128]{3,2,1,0:T(8,128)(2,1)S(1)} %bitcast.5, f32[512,1024]{1,0:T(8,128)S(1)} %get-tuple-element.51.short_ref, f32[512,1024]{1,0:T(8,128)} %get-tuple-element.52.skip_hbm), custom_call_target="tpu_custom_call" | custom-call | tf_op jit(solution)/shard_map/gate/pallas_call | solution.py:581
Async XLA Ops:
  0.0 7.2 %copy-start = (f32[2048,256]{1,0:T(8,128)S(1)}, f32[2048,256]{1,0:T(8,128)}, u32[]{:S(2)}) copy-start(f32[2048,256]{1,0:T(8,128)} %h_ref.1) | copy-start | bytes 6291460
  1.0 10.2 %collective-permute-start.2 = (f32[16,256]{1,0:T(8,128)S(1)}, f32[16,256]{1,0:T(8,128)S(1)}, u32[]{:S(2)}, u32[]{:S(2)}) collective-permute-start(f32[16,256]{1,0:T(8,128)S(1)} %get-tuple-element.32.refs_1_), channel_id=1, source_target_pairs={{0,3},{1,4},{2,5},{3,6},{4,7},{5,8},{6,9},{7,10},{8,11},{9,12},{10... | collective-permute-start | bytes 49160 | tf_op jit(solution)/shard_map/ppermute | solution.py:466
  5.2 6.0 %collective-permute-start.1 = (f32[16,256]{1,0:T(8,128)S(1)}, f32[16,256]{1,0:T(8,128)S(1)}, u32[]{:S(2)}, u32[]{:S(2)}) collective-permute-start(f32[16,256]{1,0:T(8,128)S(1)} %get-tuple-element.32.refs_1_), channel_id=1, source_target_pairs={{0,2},{1,3},{2,4},{3,5},{4,6},{5,7},{6,8},{7,9},{8,10},{9,11},{10,... | collective-permute-start | bytes 49160 | tf_op jit(solution)/shard_map/ppermute | solution.py:466
  5.8 5.4 %collective-permute-start = (bf16[16,1024]{1,0:T(8,128)(2,1)S(1)}, bf16[16,1024]{1,0:T(8,128)(2,1)S(1)}, u32[]{:S(2)}, u32[]{:S(2)}) collective-permute-start(bf16[16,1024]{1,0:T(8,128)(2,1)S(1)} %get-tuple-element.31), channel_id=1, source_target_pairs={{0,1},{1,2},{2,3},{3,4},{4,5},{5,6},{6,7},{7,8},{8,9},{9,10},{10,1... | collective-permute-start | bytes 98312 | tf_op jit(solution)/shard_map/ppermute | solution.py:466
  11.3 7.0 %collective-permute-start.3 = (bf16[528,128]{1,0:T(8,128)(2,1)}, bf16[528,128]{1,0:T(8,128)(2,1)S(1)}, u32[]{:S(2)}, u32[]{:S(2)}) collective-permute-start(bf16[528,128]{1,0:T(8,128)(2,1)} %get-tuple-element.39), channel_id=1, source_target_pairs={{0,8},{4,12},{8,0},{12,4},{16,24},{20,28},{24,16},{28,20},{1,9},{5... | collective-permute-start | bytes 405512 | tf_op jit(solution)/shard_map/ppermute | solution.py:438
  12.5 5.8 %collective-permute-start.4 = (bf16[528,128]{1,0:T(8,128)(2,1)}, bf16[528,128]{1,0:T(8,128)(2,1)S(1)}, u32[]{:S(2)}, u32[]{:S(2)}) collective-permute-start(bf16[528,128]{1,0:T(8,128)(2,1)} %get-tuple-element.40), channel_id=1, source_target_pairs={{0,16},{4,20},{8,24},{12,28},{16,0},{20,4},{24,8},{28,12},{1,17},{... | collective-permute-start | bytes 405512 | tf_op jit(solution)/shard_map/ppermute | solution.py:438
  13.2 6.1 %collective-permute-start.5 = (bf16[528,128]{1,0:T(8,128)(2,1)}, bf16[528,128]{1,0:T(8,128)(2,1)S(1)}, u32[]{:S(2)}, u32[]{:S(2)}) collective-permute-start(bf16[528,128]{1,0:T(8,128)(2,1)} %get-tuple-element.41), channel_id=1, source_target_pairs={{0,24},{4,28},{8,16},{12,20},{16,8},{20,12},{24,0},{28,4},{1,25},{... | collective-permute-start | bytes 405512 | tf_op jit(solution)/shard_map/ppermute | solution.py:438
  14.0 12.1 %copy-start.10 = (bf16[528,128]{1,0:T(8,128)(2,1)S(1)}, bf16[528,128]{1,0:T(8,128)(2,1)}, u32[]{:S(2)}) copy-start(bf16[528,128]{1,0:T(8,128)(2,1)} %get-tuple-element.44) | copy-start | bytes 405508
  14.0 12.4 %copy-start.9 = (bf16[528,128]{1,0:T(8,128)(2,1)S(1)}, bf16[528,128]{1,0:T(8,128)(2,1)}, u32[]{:S(2)}) copy-start(bf16[528,128]{1,0:T(8,128)(2,1)} %get-tuple-element.46) | copy-start | bytes 405508
  14.0 14.0 %copy-start.8 = (bf16[528,128]{1,0:T(8,128)(2,1)S(1)}, bf16[528,128]{1,0:T(8,128)(2,1)}, u32[]{:S(2)}) copy-start(bf16[528,128]{1,0:T(8,128)(2,1)} %get-tuple-element.48) | copy-start | bytes 405508
  14.0 15.4 %copy-start.7 = (bf16[528,128]{1,0:T(8,128)(2,1)S(1)}, bf16[528,128]{1,0:T(8,128)(2,1)}, u32[]{:S(2)}) copy-start(bf16[528,128]{1,0:T(8,128)(2,1)} %get-tuple-element.50) | copy-start | bytes 405508
  14.0 30.4 %copy-start.1 = (bf16[768,256]{1,0:T(8,128)(2,1)S(1)}, bf16[768,256]{1,0:T(8,128)(2,1)}, u32[]{:S(2)}) copy-start(bf16[768,256]{1,0:T(8,128)(2,1)} %constant.20.clone.refs_9_.inner) | copy-start | bytes 1179652
  14.0 30.4 %copy-start.2 = (bf16[256,384]{1,0:T(8,128)(2,1)S(1)}, bf16[256,384]{1,0:T(8,128)(2,1)}, u32[]{:S(2)}) copy-start(bf16[256,384]{1,0:T(8,128)(2,1)} %constant.19.clone.refs_8_.outer) | copy-start | bytes 589828
  14.0 30.4 %copy-start.3 = (f32[2,128,128]{2,1,0:T(8,128)S(1)}, f32[2,128,128]{2,1,0:T(8,128)}, u32[]{:S(2)}) copy-start(f32[2,128,128]{2,1,0:T(8,128)} %constant.23.clone.refs_10_.twist) | copy-start | bytes 393220
  14.0 30.4 %copy-start.6 = (bf16[528,128]{1,0:T(8,128)(2,1)S(1)}, bf16[528,128]{1,0:T(8,128)(2,1)}, u32[]{:S(2)}) copy-start(bf16[528,128]{1,0:T(8,128)(2,1)} %get-tuple-element.43.refs_0_) | copy-start | bytes 405508
  19.2 34.6 %all-to-all-start = ((bf16[32,136,128]{2,1,0:T(8,128)(2,1)}), bf16[32,136,128]{2,1,0:T(8,128)(2,1)S(1)}, u32[]{:S(2)}, u32[]{:S(2)}) async-start(bf16[32,136,128]{2,1,0:T(8,128)(2,1)} %bitcast.3), calls=%async_computation | async-start | bytes 2228224 | tf_op jit(solution)/shard_map/all_to_all | solution.py:522
  26.1 3.4 %collective-permute-start.6 = (bf16[528,128]{1,0:T(8,128)(2,1)S(1)}, bf16[528,128]{1,0:T(8,128)(2,1)S(1)}, u32[]{:S(2)}, u32[]{:S(2)}) collective-permute-start(bf16[528,128]{1,0:T(8,128)(2,1)S(1)} %copy-done.10), channel_id=1, source_target_pairs={{0,4},{4,0},{8,12},{12,8},{16,20},{20,16},{24,28},{28,24},{1,5},{5... | collective-permute-start | bytes 405512 | tf_op jit(solution)/shard_map/ppermute | solution.py:438
  26.4 13.6 %collective-permute-start.7 = (bf16[528,128]{1,0:T(8,128)(2,1)S(1)}, bf16[528,128]{1,0:T(8,128)(2,1)S(1)}, u32[]{:S(2)}, u32[]{:S(2)}) collective-permute-start(bf16[528,128]{1,0:T(8,128)(2,1)S(1)} %copy-done.9), channel_id=1, source_target_pairs={{0,12},{4,8},{8,4},{12,0},{16,28},{20,24},{24,20},{28,16},{1,13},{... | collective-permute-start | bytes 405512 | tf_op jit(solution)/shard_map/ppermute | solution.py:438
  27.9 13.5 %collective-permute-start.8 = (bf16[528,128]{1,0:T(8,128)(2,1)S(1)}, bf16[528,128]{1,0:T(8,128)(2,1)S(1)}, u32[]{:S(2)}, u32[]{:S(2)}) collective-permute-start(bf16[528,128]{1,0:T(8,128)(2,1)S(1)} %copy-done.8), channel_id=1, source_target_pairs={{0,20},{4,16},{8,28},{12,24},{16,4},{20,0},{24,12},{28,8},{1,21},{... | collective-permute-start | bytes 405512 | tf_op jit(solution)/shard_map/ppermute | solution.py:438
  29.4 15.1 %collective-permute-start.9 = (bf16[528,128]{1,0:T(8,128)(2,1)S(1)}, bf16[528,128]{1,0:T(8,128)(2,1)S(1)}, u32[]{:S(2)}, u32[]{:S(2)}) collective-permute-start(bf16[528,128]{1,0:T(8,128)(2,1)S(1)} %copy-done.7), channel_id=1, source_target_pairs={{0,28},{4,24},{8,20},{12,16},{16,12},{20,8},{24,4},{28,0},{1,29},{... | collective-permute-start | bytes 405512 | tf_op jit(solution)/shard_map/ppermute | solution.py:438
  44.4 9.4 %copy-start.4 = (bf16[768,256]{1,0:T(8,128)(2,1)S(1)}, bf16[768,256]{1,0:T(8,128)(2,1)}, u32[]{:S(2)}) copy-start(bf16[768,256]{1,0:T(8,128)(2,1)} %constant.21.clone.inner_back) | copy-start | bytes 1179652
  44.5 9.3 %copy-start.5 = (bf16[128,768]{1,0:T(8,128)(2,1)S(1)}, bf16[128,768]{1,0:T(8,128)(2,1)}, u32[]{:S(2)}) copy-start(bf16[128,768]{1,0:T(8,128)(2,1)} %constant.22.clone.outer_back) | copy-start | bytes 589828
  67.5 31.5 %all-to-all-start.1 = ((bf16[32,136,128]{2,1,0:T(8,128)(2,1)}), bf16[32,136,128]{2,1,0:T(8,128)(2,1)S(1)}, u32[]{:S(2)}, u32[]{:S(2)}) async-start(bf16[32,136,128]{2,1,0:T(8,128)(2,1)} %long_conv.1), calls=%async_computation.1 | async-start | bytes 2228224 | tf_op jit(solution)/shard_map/all_to_all | solution.py:578

commit v6 on v5

--- a/solution.py
+++ b/solution.py
@@ -176,6 +176,7 @@
 def rows_out_kernel(dims, idx_ref, k_ref, v_ref, *refs):
     length, per, parts, tiles, count = dims
     out_hbm, out_ref, k_ext, v_ext, out_sems = refs[-5:]
+    aligned = per % 16 == 0
     steps = length // LANES
 
     def out_of(j):
@@ -192,14 +193,20 @@
             block = mixed[step * LANES : (step + 1) * LANES]
             scale = block_scale(jnp.max(jnp.abs(block), 0, keepdims=True))
             scales.append(scale)
-            codes.append(encode(block, 1.0 / scale).astype(bf16).T.astype(f32))
+            code = encode(block, 1.0 / scale).astype(bf16).T
+            codes.append(code if aligned else code.astype(f32))
         unused = [jnp.ones((PAD - steps, LANES), f32)]
         lines = jnp.concatenate([*scales, *unused], 0)
         for g in range(parts):
+            place = out_ref.at[lax.rem(j, tiles) * parts + g, j // tiles]
             piece = [code[g * per : (g + 1) * per] for code in codes]
             line = pltpu.roll(lines, (-g * per) % LANES, 1)
-            whole_piece = jnp.concatenate(piece + [line], 0).astype(bf16)
-            out_ref[lax.rem(j, tiles) * parts + g, j // tiles] = whole_piece
+            if aligned:
+                for step in range(steps):
+                    place[step * per : (step + 1) * per] = piece[step]
+                place[steps * per :] = line.astype(bf16)
+            else:
+                place[...] = jnp.concatenate(piece + [line], 0).astype(bf16)
         for copy in out_of(j):
             copy.start()
         return carry
@@ -229,14 +236,16 @@
     start_all(into, count)
 
     def tile(j, carry):
-        pieces = [
-            y_ref[lax.rem(j, tiles) * parts + g, j // tiles].astype(f32) for g in range(parts)
-        ]
+        pieces = [y_ref[lax.rem(j, tiles) * parts + g, j // tiles] for g in range(parts)]
+        marks = [piece[rows:].astype(f32) for piece in pieces]
+        if per % 16:
+            pieces = [piece.astype(f32) for piece in pieces]
         lane = lane_index((PAD, LANES))
-        moved = [pltpu.roll(pieces[g][rows:], g * per, 1) for g in range(parts)]
+        moved = [pltpu.roll(marks[g], g * per, 1) for g in range(parts)]
         values = []
         for step in range(steps):
             code = jnp.concatenate([t[step * per : (step + 1) * per] for t in pieces], 0).T
+            code = code.astype(f32)
             scale = jnp.ones((PAD, LANES), f32)
             for g in range(parts):
                 inside = (lane >= g * per) & (lane < (g + 1) * per)
@@ -348,10 +357,10 @@
 
 
 def conv_kernel(
-    dims, x_ref, h_hbm, outer, inner, inner_back, outer_back, twist, out_ref, *scratch
+    dims, x_ref, h_hbm, outer, inner, inner_back, outer_back, twist, out_hbm, *scratch
 ):
     rows, per, lines, blocks, group, batch = dims
-    held, h_ref, scales, found, sems = scratch
+    held, h_ref, scales, found, out_ref, sems, out_sems = scratch
     steps = lines // per
     fetches = []
     for i in range(per // group):
@@ -405,9 +414,16 @@
             line = jnp.concatenate([scales[i * batch + j], jnp.ones((PAD - steps, LANES), f32)], 0)
             tile = jnp.concatenate([held[pl.ds(start, lines), :], line], 0)
             out_ref[i * batch + j] = tile.astype(bf16)
+        for copy in out_of(i):
+            copy.start()
         return carry
 
+    def out_of(i):
+        part = pl.ds(i * batch, batch)
+        return [pltpu.make_async_copy(out_ref.at[part], out_hbm.at[part], out_sems.at[i])]
+
     lax.fori_loop(0, blocks // batch, pack, 0)
+    wait_all(out_of, blocks // batch)
 
 
 def whole(array):
@@ -428,7 +444,7 @@
     lines = length // LANES * per
     parts = LANES // per
     tiles = shard // LANES
-    group = min(8, per)
+    group, batch = min(8, per), 8
     me = jnp.stack([lax.axis_index(axis) for axis in BOTH]).astype(jnp.int32)
     tables = transform_tables(rows)
     outer, inner, inner_back, outer_back, twist = (jnp.asarray(t) for t in tables)
@@ -561,16 +577,18 @@
     skip, spectrum = (pltpu.with_memory_space_constraint(a, pltpu.HBM) for a in (skip, spectrum))
 
     convolved = pl.pallas_call(
-        functools.partial(conv_kernel, (rows, per, lines, devices, group, 8)),
+        functools.partial(conv_kernel, (rows, per, lines, devices, group, batch)),
         in_specs=[vmem, hbm] + [vmem] * 5,
-        out_specs=vmem,
+        out_specs=hbm,
         out_shape=jax.ShapeDtypeStruct((devices, lines + PAD, LANES), bf16),
         scratch_shapes=[
             pltpu.VMEM((rows * per, LANES), f32),
             pltpu.VMEM((per, rows, 2 * LANES), f32),
             pltpu.VMEM((devices, length // LANES, LANES), f32),
             pltpu.VMEM((rows, LANES), f32),
+            pltpu.VMEM((devices, lines + PAD, LANES), bf16),
             pltpu.SemaphoreType.DMA((per // group,)),
+            pltpu.SemaphoreType.DMA((devices // batch,)),
         ],
         compiler_params=vmem_limit(28),
         name="long_conv",

time: 103 us -> 103 us (level)
  no operation moved by 1% of the time
where the time goes in v6:
time: 103 us
  Pallas kernels  42.1 us (41%)
  waiting for transfers between devices  37.2 us (36%)
  starting transfers between devices  22.8 us (22%)
    all_to_all x1, waiting for transfers between devices, local(): lax.all_to_all(convolved, BOTH, split_axis=0, concat_axis=0, tiled=True)  19.8 us
    ppermute x7, waiting for transfers between devices, crossed(): lax.ppermute(array[s], axis, [(i, i ^ s) for i in range(count)])  15.8 us
    pallas_call x1, Pallas kernels, local(): pl.pallas_call(functools.partial(conv_kernel, (rows, per, lines, devices,...  13.6 us
    pallas_call x1, Pallas kernels, local(): pl.pallas_call(functools.partial(gate_parts_kernel, (length, tiles)), gri...  7.9 us
    pallas_call x1, Pallas kernels, local(): pl.pallas_call(functools.partial(filter_kernel, (rows, per, peers, group)...  7.82 us
    all_to_all x1, starting transfers between devices, local(): lax.all_to_all(coded, BOTH, split_axis=0, concat_axis=0, tiled=True)  6.81 us
    ppermute x3, starting transfers between devices, shifted(): lax.ppermute(array, BOTH, [(i, (i + by) % devices) for i in range(devices)])  6.15 us
    ppermute x7, starting transfers between devices, crossed(): lax.ppermute(array[s], axis, [(i, i ^ s) for i in range(count)])  6.07 us
  transfers between devices with their start and end apart: 12, of which 6 were waited for; matrix products, arithmetic and copies ran while one was open for 0% of the time, Pallas kernels for 23%

profile of v6, /device:TPU:1, one launch (start us, length us, event | category | flops | bytes accessed | tf_op | source)
XLA Modules:
  0.0 102.5 jit_solution(9100009557194642650)
XLA Ops:
  0.0 0.0 copy-start
  0.0 1.0 edges.1
  1.0 4.2 %collective-permute-start.2 = (f32[16,256]{1,0:T(8,128)S(1)}, f32[16,256]{1,0:T(8,128)S(1)}, u32[]{:S(2)}, u32[]{:S(2)}) collective-permute-start(f32[16,256]{1,0:T(8,128)S(1)} %get-tuple-element.32.refs_1_), channel_id=1, source_target_pairs={{0,3},{1,4},{2,5},{3,6},{4,7},{5,8},{6,9},{7,10},{8,11},{9,12},{10... | collective-permute-start | bytes 49160 | tf_op jit(solution)/shard_map/ppermute | solution.py:482
  5.2 0.6 collective-permute-start.1
  5.8 1.3 %collective-permute-start = (bf16[16,1024]{1,0:T(8,128)(2,1)S(1)}, bf16[16,1024]{1,0:T(8,128)(2,1)S(1)}, u32[]{:S(2)}, u32[]{:S(2)}) collective-permute-start(bf16[16,1024]{1,0:T(8,128)(2,1)S(1)} %get-tuple-element.31), channel_id=1, source_target_pairs={{0,1},{1,2},{2,3},{3,4},{4,5},{5,6},{6,7},{7,8},{8,9},{9,10},{10,1... | collective-permute-start | bytes 98312 | tf_op jit(solution)/shard_map/ppermute | solution.py:482
  7.1 0.1 pad_add_fusion.idx_ref
  7.2 0.0 copy-done
  7.2 4.0 %filter_rows.1 = (bf16[528,128]{1,0:T(8,128)(2,1)}, bf16[528,128]{1,0:T(8,128)(2,1)}, bf16[528,128]{1,0:T(8,128)(2,1)}, bf16[528,128]{1,0:T(8,128)(2,1)}, bf16[5...) custom-call(s32[2]{0:T(128)S(1)} %pad_add_fusion.idx_ref, ...), custom_call_target="tpu_custom_call" | custom-call | tf_op jit(solution)/shard_map/filter_rows/pallas_call | solution.py:489
  11.2 0.0 collective-permute-done.2.refs_3_
  11.2 0.0 collective-permute-done.1.refs_2_
  11.2 0.0 collective-permute-done.refs_0_
  11.3 1.2 %collective-permute-start.3 = (bf16[528,128]{1,0:T(8,128)(2,1)}, bf16[528,128]{1,0:T(8,128)(2,1)S(1)}, u32[]{:S(2)}, u32[]{:S(2)}) collective-permute-start(bf16[528,128]{1,0:T(8,128)(2,1)} %get-tuple-element.39), channel_id=1, source_target_pairs={{0,8},{4,12},{8,0},{12,4},{16,24},{20,28},{24,16},{28,20},{1,9},{5... | collective-permute-start | bytes 405512 | tf_op jit(solution)/shard_map/ppermute | solution.py:454
  12.5 0.6 collective-permute-start.4
  13.2 0.8 collective-permute-start.5
  14.0 0.0 copy-start.10
  14.0 0.0 copy-start.9
  14.0 0.0 copy-start.8
  14.0 0.0 copy-start.7
  14.0 0.0 copy-start.1
  14.0 0.0 copy-start.2
  14.0 0.0 copy-start.3
  14.0 0.0 copy-start.6
  14.0 4.3 %mixed_rows.1 = bf16[8,4,136,128]{3,2,1,0:T(8,128)(2,1)} custom-call(s32[2]{0:T(128)S(1)} %pad_add_fusion.idx_ref, bf16[512,1024]{1,0:T(8,128)(2,1)S(1)} %get-tuple-element.29.k_ref, bf16[512,1024]{1,0:T(8,128)(2,1)S(1)} %get-tuple-element.30.v_ref, bf16[16,1024]{1,0:T(8,128)(2,1)S(1)} %collective-permute-done.refs_0_, ...), custom_call_target="tpu_custom_call" | custom-call | tf_op jit(solution)/shard_map/mixed_rows/pallas_call | solution.py:520
  18.3 0.0 collective-permute-done.3.refs_2_
  18.3 0.0 collective-permute-done.4.refs_4_
  18.4 0.9 collective-permute-done.5.refs_6_
  19.2 6.8 %all-to-all-start = ((bf16[32,136,128]{2,1,0:T(8,128)(2,1)}), bf16[32,136,128]{2,1,0:T(8,128)(2,1)S(1)}, u32[]{:S(2)}, u32[]{:S(2)}) async-start(bf16[32,136,128]{2,1,0:T(8,128)(2,1)} %bitcast.3), calls=%async_computation | async-start | bytes 2228224 | tf_op jit(solution)/shard_map/all_to_all | solution.py:538
  26.1 0.0 copy-done.10
  26.1 0.3 collective-permute-start.6
  26.4 0.0 copy-done.9
  26.4 1.5 %collective-permute-start.7 = (bf16[528,128]{1,0:T(8,128)(2,1)S(1)}, bf16[528,128]{1,0:T(8,128)(2,1)S(1)}, u32[]{:S(2)}, u32[]{:S(2)}) collective-permute-start(bf16[528,128]{1,0:T(8,128)(2,1)S(1)} %copy-done.9), channel_id=1, source_target_pairs={{0,12},{4,8},{8,4},{12,0},{16,28},{20,24},{24,20},{28,16},{1,13},{... | collective-permute-start | bytes 405512 | tf_op jit(solution)/shard_map/ppermute | solution.py:454
  27.9 0.0 copy-done.8
  27.9 1.4 %collective-permute-start.8 = (bf16[528,128]{1,0:T(8,128)(2,1)S(1)}, bf16[528,128]{1,0:T(8,128)(2,1)S(1)}, u32[]{:S(2)}, u32[]{:S(2)}) collective-permute-start(bf16[528,128]{1,0:T(8,128)(2,1)S(1)} %copy-done.8), channel_id=1, source_target_pairs={{0,20},{4,16},{8,28},{12,24},{16,4},{20,0},{24,12},{28,8},{1,21},{... | collective-permute-start | bytes 405512 | tf_op jit(solution)/shard_map/ppermute | solution.py:454
  29.4 0.0 copy-done.7
  29.4 0.1 collective-permute-start.9
  29.5 0.0 collective-permute-done.6.refs_1_
  29.5 10.5 %collective-permute-done.7.refs_3_ = bf16[528,128]{1,0:T(8,128)(2,1)S(1)} collective-permute-done((bf16[528,128]{1,0:T(8,128)(2,1)S(1)}, bf16[528,128]{1,0:T(8,128)(2,1)S(1)}, u32[]{:S(2)}, u32[]{:S(2)}) %collective-permute-start.7) | collective-permute-done | bytes 135200 | tf_op jit(solution)/shard_map/ppermute | solution.py:454
  40.0 1.5 %collective-permute-done.8.refs_5_ = bf16[528,128]{1,0:T(8,128)(2,1)S(1)} collective-permute-done((bf16[528,128]{1,0:T(8,128)(2,1)S(1)}, bf16[528,128]{1,0:T(8,128)(2,1)S(1)}, u32[]{:S(2)}, u32[]{:S(2)}) %collective-permute-start.8) | collective-permute-done | bytes 135200 | tf_op jit(solution)/shard_map/ppermute | solution.py:454
  41.5 3.0 %collective-permute-done.9.refs_7_ = bf16[528,128]{1,0:T(8,128)(2,1)S(1)} collective-permute-done((bf16[528,128]{1,0:T(8,128)(2,1)S(1)}, bf16[528,128]{1,0:T(8,128)(2,1)S(1)}, u32[]{:S(2)}, u32[]{:S(2)}) %collective-permute-start.9) | collective-permute-done | bytes 135200 | tf_op jit(solution)/shard_map/ppermute | solution.py:454
  44.4 0.0 copy-done.1
  44.4 0.0 copy-done.2
  44.4 0.0 copy-done.3
  44.4 0.0 copy-done.6
  44.4 0.0 copy-start.4
  44.5 0.0 copy-start.5
  44.5 7.8 %filter_spectrum.1.h_hbm = f32[32,128,256]{2,1,0:T(8,128)} custom-call(s32[2]{0:T(128)S(1)} %pad_add_fusion.idx_ref, bf16[528,128]{1,0:T(8,128)(2,1)S(1)} %copy-done.6, bf16[528,128]{1,0:T(8,128)(2,1)S(1)} %collective-permute-done.6.refs_1_, bf16[528,128]{1,0:T(8,128)(2,1)S(1)} %collective-permute-done.3.refs_2_, ...), custom_call_target="tpu_custom_call" | custom-call | tf_op jit(solution)/shard_map/filter_spectrum/pallas_call | solution.py:540
  52.3 1.5 %all-to-all-done.x_ref = bf16[32,136,128]{2,1,0:T(8,128)(2,1)S(1)} async-done(((bf16[32,136,128]{2,1,0:T(8,128)(2,1)}), bf16[32,136,128]{2,1,0:T(8,128)(2,1)S(1)}, u32[]{:S(2)}, u32[]{:S(2)}) %all-to-all-start) | async-done | bytes 1114144 | tf_op jit(solution)/shard_map/all_to_all | solution.py:538
  53.8 0.0 copy-done.4
  53.8 0.0 copy-done.5
  53.8 13.6 %long_conv.1 = bf16[32,136,128]{2,1,0:T(8,128)(2,1)} custom-call(bf16[32,136,128]{2,1,0:T(8,128)(2,1)S(1)} %all-to-all-done.x_ref, f32[32,128,256]{2,1,0:T(8,128)} %filter_spectrum.1.h_hbm, bf16[256,384]{1,0:T(8,128)(2,1)S(1)} %copy-done.2, bf16[768,256]{1,0:T(8,128)(2,1)S(1)} %copy-done.1, bf16[768,256]{1,0:T(8,128)(2,1)S(1)} %copy-done.4, ...), custom_call_target="tpu_custom_call" | custom-call | tf_op jit(solution)/shard_map/long_conv/pallas_call | solution.py:579
  67.4 3.8 %all-to-all-start.1 = ((bf16[32,136,128]{2,1,0:T(8,128)(2,1)}), bf16[32,136,128]{2,1,0:T(8,128)(2,1)S(1)}, u32[]{:S(2)}, u32[]{:S(2)}) async-start(bf16[32,136,128]{2,1,0:T(8,128)(2,1)} %long_conv.1), calls=%async_computation.1 | async-start | bytes 2228224 | tf_op jit(solution)/shard_map/all_to_all | solution.py:596
  71.2 7.9 %gate_parts.1 = (f32[512,1024]{1,0:T(8,128)S(1)}, f32[512,1024]{1,0:T(8,128)}) custom-call(s32[2]{0:T(128)S(1)} %pad_add_fusion.idx_ref, bf16[512,1024]{1,0:T(8,128)(2,1)} %q_ref.3, bf16[512,1024]{1,0:T(8,128)(2,1)} %k_ref.3, bf16[512,1024]{1,0:T(8,128)(2,1)} %v_ref.3, bf16[16,1024]{1,0:T(8,128)(2,1)S(1)} %collective-permute-done.refs_0_, ...), custom_call_target="tpu_custom_call" | custom-call | tf_op jit(solution)/shard_map/gate_parts/pallas_call | solution.py:563
  79.1 19.8 %all-to-all-done.1 = bf16[32,136,128]{2,1,0:T(8,128)(2,1)S(1)} async-done(((bf16[32,136,128]{2,1,0:T(8,128)(2,1)}), bf16[32,136,128]{2,1,0:T(8,128)(2,1)S(1)}, u32[]{:S(2)}, u32[]{:S(2)}) %all-to-all-start.1) | async-done | bytes 1114144 | tf_op jit(solution)/shard_map/all_to_all | solution.py:596
  98.9 3.5 %gate.1 = f32[512,1024]{1,0:T(8,128)} custom-call(bf16[8,4,136,128]{3,2,1,0:T(8,128)(2,1)S(1)} %bitcast.5, f32[512,1024]{1,0:T(8,128)S(1)} %get-tuple-element.51.short_ref, f32[512,1024]{1,0:T(8,128)} %get-tuple-element.52.skip_hbm), custom_call_target="tpu_custom_call" | custom-call | tf_op jit(solution)/shard_map/gate/pallas_call | solution.py:599
Async XLA Ops:
  0.0 7.2 %copy-start = (f32[2048,256]{1,0:T(8,128)S(1)}, f32[2048,256]{1,0:T(8,128)}, u32[]{:S(2)}) copy-start(f32[2048,256]{1,0:T(8,128)} %h_ref.1) | copy-start | bytes 6291460
  1.0 10.2 %collective-permute-start.2 = (f32[16,256]{1,0:T(8,128)S(1)}, f32[16,256]{1,0:T(8,128)S(1)}, u32[]{:S(2)}, u32[]{:S(2)}) collective-permute-start(f32[16,256]{1,0:T(8,128)S(1)} %get-tuple-element.32.refs_1_), channel_id=1, source_target_pairs={{0,3},{1,4},{2,5},{3,6},{4,7},{5,8},{6,9},{7,10},{8,11},{9,12},{10... | collective-permute-start | bytes 49160 | tf_op jit(solution)/shard_map/ppermute | solution.py:482
  5.2 6.0 %collective-permute-start.1 = (f32[16,256]{1,0:T(8,128)S(1)}, f32[16,256]{1,0:T(8,128)S(1)}, u32[]{:S(2)}, u32[]{:S(2)}) collective-permute-start(f32[16,256]{1,0:T(8,128)S(1)} %get-tuple-element.32.refs_1_), channel_id=1, source_target_pairs={{0,2},{1,3},{2,4},{3,5},{4,6},{5,7},{6,8},{7,9},{8,10},{9,11},{10,... | collective-permute-start | bytes 49160 | tf_op jit(solution)/shard_map/ppermute | solution.py:482
  5.8 5.4 %collective-permute-start = (bf16[16,1024]{1,0:T(8,128)(2,1)S(1)}, bf16[16,1024]{1,0:T(8,128)(2,1)S(1)}, u32[]{:S(2)}, u32[]{:S(2)}) collective-permute-start(bf16[16,1024]{1,0:T(8,128)(2,1)S(1)} %get-tuple-element.31), channel_id=1, source_target_pairs={{0,1},{1,2},{2,3},{3,4},{4,5},{5,6},{6,7},{7,8},{8,9},{9,10},{10,1... | collective-permute-start | bytes 98312 | tf_op jit(solution)/shard_map/ppermute | solution.py:482
  11.3 7.0 %collective-permute-start.3 = (bf16[528,128]{1,0:T(8,128)(2,1)}, bf16[528,128]{1,0:T(8,128)(2,1)S(1)}, u32[]{:S(2)}, u32[]{:S(2)}) collective-permute-start(bf16[528,128]{1,0:T(8,128)(2,1)} %get-tuple-element.39), channel_id=1, source_target_pairs={{0,8},{4,12},{8,0},{12,4},{16,24},{20,28},{24,16},{28,20},{1,9},{5... | collective-permute-start | bytes 405512 | tf_op jit(solution)/shard_map/ppermute | solution.py:454
  12.5 5.8 %collective-permute-start.4 = (bf16[528,128]{1,0:T(8,128)(2,1)}, bf16[528,128]{1,0:T(8,128)(2,1)S(1)}, u32[]{:S(2)}, u32[]{:S(2)}) collective-permute-start(bf16[528,128]{1,0:T(8,128)(2,1)} %get-tuple-element.40), channel_id=1, source_target_pairs={{0,16},{4,20},{8,24},{12,28},{16,0},{20,4},{24,8},{28,12},{1,17},{... | collective-permute-start | bytes 405512 | tf_op jit(solution)/shard_map/ppermute | solution.py:454
  13.2 6.1 %collective-permute-start.5 = (bf16[528,128]{1,0:T(8,128)(2,1)}, bf16[528,128]{1,0:T(8,128)(2,1)S(1)}, u32[]{:S(2)}, u32[]{:S(2)}) collective-permute-start(bf16[528,128]{1,0:T(8,128)(2,1)} %get-tuple-element.41), channel_id=1, source_target_pairs={{0,24},{4,28},{8,16},{12,20},{16,8},{20,12},{24,0},{28,4},{1,25},{... | collective-permute-start | bytes 405512 | tf_op jit(solution)/shard_map/ppermute | solution.py:454
  14.0 12.1 %copy-start.10 = (bf16[528,128]{1,0:T(8,128)(2,1)S(1)}, bf16[528,128]{1,0:T(8,128)(2,1)}, u32[]{:S(2)}) copy-start(bf16[528,128]{1,0:T(8,128)(2,1)} %get-tuple-element.44) | copy-start | bytes 405508
  14.0 12.4 %copy-start.9 = (bf16[528,128]{1,0:T(8,128)(2,1)S(1)}, bf16[528,128]{1,0:T(8,128)(2,1)}, u32[]{:S(2)}) copy-start(bf16[528,128]{1,0:T(8,128)(2,1)} %get-tuple-element.46) | copy-start | bytes 405508
  14.0 14.0 %copy-start.8 = (bf16[528,128]{1,0:T(8,128)(2,1)S(1)}, bf16[528,128]{1,0:T(8,128)(2,1)}, u32[]{:S(2)}) copy-start(bf16[528,128]{1,0:T(8,128)(2,1)} %get-tuple-element.48) | copy-start | bytes 405508
  14.0 15.4 %copy-start.7 = (bf16[528,128]{1,0:T(8,128)(2,1)S(1)}, bf16[528,128]{1,0:T(8,128)(2,1)}, u32[]{:S(2)}) copy-start(bf16[528,128]{1,0:T(8,128)(2,1)} %get-tuple-element.50) | copy-start | bytes 405508
  14.0 30.4 %copy-start.1 = (bf16[768,256]{1,0:T(8,128)(2,1)S(1)}, bf16[768,256]{1,0:T(8,128)(2,1)}, u32[]{:S(2)}) copy-start(bf16[768,256]{1,0:T(8,128)(2,1)} %constant.20.clone.refs_9_.inner) | copy-start | bytes 1179652
  14.0 30.4 %copy-start.2 = (bf16[256,384]{1,0:T(8,128)(2,1)S(1)}, bf16[256,384]{1,0:T(8,128)(2,1)}, u32[]{:S(2)}) copy-start(bf16[256,384]{1,0:T(8,128)(2,1)} %constant.19.clone.refs_8_.outer) | copy-start | bytes 589828
  14.0 30.4 %copy-start.3 = (f32[2,128,128]{2,1,0:T(8,128)S(1)}, f32[2,128,128]{2,1,0:T(8,128)}, u32[]{:S(2)}) copy-start(f32[2,128,128]{2,1,0:T(8,128)} %constant.23.clone.refs_10_.twist) | copy-start | bytes 393220
  14.0 30.4 %copy-start.6 = (bf16[528,128]{1,0:T(8,128)(2,1)S(1)}, bf16[528,128]{1,0:T(8,128)(2,1)}, u32[]{:S(2)}) copy-start(bf16[528,128]{1,0:T(8,128)(2,1)} %get-tuple-element.43.refs_0_) | copy-start | bytes 405508
  19.2 34.6 %all-to-all-start = ((bf16[32,136,128]{2,1,0:T(8,128)(2,1)}), bf16[32,136,128]{2,1,0:T(8,128)(2,1)S(1)}, u32[]{:S(2)}, u32[]{:S(2)}) async-start(bf16[32,136,128]{2,1,0:T(8,128)(2,1)} %bitcast.3), calls=%async_computation | async-start | bytes 2228224 | tf_op jit(solution)/shard_map/all_to_all | solution.py:538
  26.1 3.4 %collective-permute-start.6 = (bf16[528,128]{1,0:T(8,128)(2,1)S(1)}, bf16[528,128]{1,0:T(8,128)(2,1)S(1)}, u32[]{:S(2)}, u32[]{:S(2)}) collective-permute-start(bf16[528,128]{1,0:T(8,128)(2,1)S(1)} %copy-done.10), channel_id=1, source_target_pairs={{0,4},{4,0},{8,12},{12,8},{16,20},{20,16},{24,28},{28,24},{1,5},{5... | collective-permute-start | bytes 405512 | tf_op jit(solution)/shard_map/ppermute | solution.py:454
  26.4 13.6 %collective-permute-start.7 = (bf16[528,128]{1,0:T(8,128)(2,1)S(1)}, bf16[528,128]{1,0:T(8,128)(2,1)S(1)}, u32[]{:S(2)}, u32[]{:S(2)}) collective-permute-start(bf16[528,128]{1,0:T(8,128)(2,1)S(1)} %copy-done.9), channel_id=1, source_target_pairs={{0,12},{4,8},{8,4},{12,0},{16,28},{20,24},{24,20},{28,16},{1,13},{... | collective-permute-start | bytes 405512 | tf_op jit(solution)/shard_map/ppermute | solution.py:454
  27.9 13.5 %collective-permute-start.8 = (bf16[528,128]{1,0:T(8,128)(2,1)S(1)}, bf16[528,128]{1,0:T(8,128)(2,1)S(1)}, u32[]{:S(2)}, u32[]{:S(2)}) collective-permute-start(bf16[528,128]{1,0:T(8,128)(2,1)S(1)} %copy-done.8), channel_id=1, source_target_pairs={{0,20},{4,16},{8,28},{12,24},{16,4},{20,0},{24,12},{28,8},{1,21},{... | collective-permute-start | bytes 405512 | tf_op jit(solution)/shard_map/ppermute | solution.py:454
  29.4 15.1 %collective-permute-start.9 = (bf16[528,128]{1,0:T(8,128)(2,1)S(1)}, bf16[528,128]{1,0:T(8,128)(2,1)S(1)}, u32[]{:S(2)}, u32[]{:S(2)}) collective-permute-start(bf16[528,128]{1,0:T(8,128)(2,1)S(1)} %copy-done.7), channel_id=1, source_target_pairs={{0,28},{4,24},{8,20},{12,16},{16,12},{20,8},{24,4},{28,0},{1,29},{... | collective-permute-start | bytes 405512 | tf_op jit(solution)/shard_map/ppermute | solution.py:454
  44.4 9.4 %copy-start.4 = (bf16[768,256]{1,0:T(8,128)(2,1)S(1)}, bf16[768,256]{1,0:T(8,128)(2,1)}, u32[]{:S(2)}) copy-start(bf16[768,256]{1,0:T(8,128)(2,1)} %constant.21.clone.inner_back) | copy-start | bytes 1179652
  44.5 9.3 %copy-start.5 = (bf16[128,768]{1,0:T(8,128)(2,1)S(1)}, bf16[128,768]{1,0:T(8,128)(2,1)}, u32[]{:S(2)}) copy-start(bf16[128,768]{1,0:T(8,128)(2,1)} %constant.22.clone.outer_back) | copy-start | bytes 589828
  67.4 31.5 %all-to-all-start.1 = ((bf16[32,136,128]{2,1,0:T(8,128)(2,1)}), bf16[32,136,128]{2,1,0:T(8,128)(2,1)S(1)}, u32[]{:S(2)}, u32[]{:S(2)}) async-start(bf16[32,136,128]{2,1,0:T(8,128)(2,1)} %long_conv.1), calls=%async_computation.1 | async-start | bytes 2228224 | tf_op jit(solution)/shard_map/all_to_all | solution.py:596
